TPU v7x, 128 devices: a whole 4x4x4 slice. The times are simulated.
128 devices in a mesh: slab: 32 (over z, x, core), sector: 4 (over y).
Axes of the slice: x: 4, y: 4, z: 4, core: 2. Of those that a mesh axis runs over, the one named last changes fastest.
Arguments:
- fields: float32 [9, 256, 128, 256], P(None, 'slab', 'sector'), may hold values from -6 to 6
- volume: float32 [256, 128, 256], P('slab', 'sector'), may hold values from 2 to 4
- swept_axial: float32 [256, 128, 256], P('slab', 'sector'), may hold values from -0.15 to 0.15
- swept_angular: float32 [256, 128, 256], P('slab', 'sector'), may hold values from -0.15 to 0.15
- swept_radial: float32 [256, 128, 256], P('slab', 'sector'), may hold values from -0.15 to 0.15
- conductivity: float32 [256, 128, 256], P('slab', 'sector'), may hold values from 0.1 to 1
- corner_areas: bfloat16 [3, 8, 256, 128, 256], P(None, None, 'slab', 'sector'), may hold values from -6 to 6
- parcel_loads: float32 [9, 524288], P(None, ('slab', 'sector')), may hold values from -6 to 6
- dest_device: int32 [524288, 1], P(('slab', 'sector')), may hold values from 0 to 127; in each aligned block of 4096 rows (0 to 4095, 4096 to 8191, ...) at most 64 rows name the same one
- dest_cell: int32 [524288], P(('slab', 'sector')), may hold values from 0 to 65535
Outputs:
- volume_new: float32 [256, 128, 256], P('slab', 'sector')
- diffused: float32 [9, 256, 128, 256], P(None, 'slab', 'sector')
- gradients: float32 [27, 256, 128, 256], P(None, 'slab', 'sector')
Inputs may be any that keep to these rules, and one draw needn't show every extreme that they name: `dest_device`: for the parcels of one device, at most 64 name the same destination device, and some destination gets exactly 64. `dest_cell`: A local cell index a 8192 + t * 256 + j in the destination device's block.
All inputs are finite; a program needn't handle non-finite values.
Results may differ from a plain program's by a relative error of at most 0.0003.
Values sent between devices are 32-bit elements; how exact they have to be, the bound alone decides.
A program may use at most 256 MiB of HBM per device.

v0:
```python
import jax
import jax.numpy as jnp
from jax import lax
from jax.sharding import PartitionSpec as P


def passed_along(array, axis, by):
    size = lax.axis_size(axis)
    pairs = [(i, i + by) for i in range(size) if 0 <= i + by < size]
    return lax.ppermute(array, axis, pairs)


def shifted(value, axis, steps):
    count = lax.axis_size(axis)
    pairs = [(source, (source + steps) % count) for source in range(count)]
    return lax.ppermute(value, axis, pairs)


def with_halo(cells, sides, width):
    for axis, dim in sides:
        count = lax.axis_size(axis)
        head = lax.slice_in_dim(cells, 0, width, axis=dim)
        tail = lax.slice_in_dim(cells, cells.shape[dim] - width, cells.shape[dim], axis=dim)
        cells = jnp.concatenate(
            [
                lax.ppermute(tail, axis, [(i, (i + 1) % count) for i in range(count)]),
                cells,
                lax.ppermute(head, axis, [((i + 1) % count, i) for i in range(count)]),
            ],
            axis=dim,
        )
    return cells


def local(
    fields,
    volume,
    swept_axial,
    swept_angular,
    swept_radial,
    conductivity,
    corner_areas,
    parcel_loads,
    dest_device,
    dest_cell,
):
    field_n, axial_n, angle_n, radial_n = fields.shape
    node_sums = jnp.zeros((3 * field_n + 1, axial_n + 1, angle_n + 1, radial_n), jnp.float32)
    for corner in range(8):
        step_z = corner // 4
        step_t = corner // 2 % 2
        step_r = corner % 2
        areas = corner_areas[:, corner].astype(jnp.float32)
        terms = (areas[:, None] * fields[None]).reshape(3 * field_n, axial_n, angle_n, radial_n)
        terms = jnp.concatenate([terms, (volume * 0.125)[None]], 0)
        if step_r == 0:
            terms = jnp.pad(terms[..., 1:], ((0, 0), (0, 0), (0, 0), (0, 1)))
        terms = jnp.pad(terms, ((0, 0), (step_z, 1 - step_z), (step_t, 1 - step_t), (0, 0)))
        node_sums = node_sums + terms
    rim_axial = jnp.pad(swept_axial[axial_n - 1], ((0, 1), (0, 0)))
    packed_z = jnp.concatenate([node_sums[:, axial_n], rim_axial[None]], 0)
    from_below = passed_along(packed_z, "slab", 1)
    node_sums = node_sums[:, :axial_n].at[:, 0].add(from_below[:-1])
    packed_t = jnp.concatenate([node_sums[:, :, angle_n], swept_angular[:, angle_n - 1][None]], 0)
    beside = shifted(packed_t, "sector", 1)
    node_sums = node_sums[:, :, :angle_n].at[:, :, 0].add(beside[:-1])
    gradients = node_sums[:-1] / node_sums[-1:]
    lower_z = jnp.concatenate([from_below[-1, :angle_n][None], swept_axial[:-1]], 0)
    lower_t = jnp.concatenate([beside[-1][:, None], swept_angular[:, :-1]], 1)
    lower_r = jnp.pad(swept_radial, ((0, 0), (0, 0), (1, 0)))[..., :-1]
    volume_new = volume + swept_axial - lower_z + swept_angular - lower_t + swept_radial - lower_r
    slab_count = lax.axis_size("slab")
    sector_count = lax.axis_size("sector")
    device_count = slab_count * sector_count
    parcel_n = dest_cell.shape[0]
    capacity = 2 * parcel_n // device_count
    target = dest_device[:, 0]
    matches = (target[:, None] == jnp.arange(device_count, dtype=jnp.int32)[None]).astype(jnp.int32)
    order_in = jnp.sum(matches * jnp.cumsum(matches, 0), 1) - 1
    slot_at = target * capacity + order_in
    records = jnp.concatenate([parcel_loads, dest_cell.astype(jnp.float32)[None]], 0)
    outgoing = (
        jnp.zeros((field_n + 1, device_count * capacity), jnp.float32).at[:, slot_at].set(records)
    )
    arrived = lax.all_to_all(
        outgoing.reshape(field_n + 1, device_count, capacity),
        ("slab", "sector"),
        split_axis=1,
        concat_axis=1,
        tiled=True,
    )
    arrived = arrived.reshape(field_n + 1, device_count * capacity)
    cell_ids = arrived[-1].astype(jnp.int32)
    deposit = (
        jnp.zeros((field_n, axial_n * angle_n * radial_n), jnp.float32)
        .at[:, cell_ids]
        .add(arrived[:-1])
    )
    deposit = deposit.reshape(field_n, axial_n, angle_n, radial_n)
    source_fields = fields + deposit / volume_new
    stacked = jnp.concatenate([source_fields, conductivity[None]], 0)
    padded = with_halo(stacked, (("slab", 1), ("sector", 2)), 1)
    position = lax.axis_index("slab")
    at_bottom = position == 0
    at_top = position == slab_count - 1
    kappa_pad = padded[-1]
    kappa_pad = kappa_pad.at[0].set(jnp.where(at_bottom, 0.0, kappa_pad[0]))
    kappa_pad = kappa_pad.at[-1].set(jnp.where(at_top, 0.0, kappa_pad[-1]))
    field_pad = padded[:-1]
    radial_fields = jnp.pad(source_fields, ((0, 0), (0, 0), (0, 0), (1, 1)))
    radial_kappa = jnp.pad(conductivity, ((0, 0), (0, 0), (1, 1)))
    near_fields = [
        field_pad[:, :-2, 1:-1],
        field_pad[:, 2:, 1:-1],
        field_pad[:, 1:-1, :-2],
        field_pad[:, 1:-1, 2:],
        radial_fields[..., :-2],
        radial_fields[..., 2:],
    ]
    near_kappas = [
        kappa_pad[:-2, 1:-1],
        kappa_pad[2:, 1:-1],
        kappa_pad[1:-1, :-2],
        kappa_pad[1:-1, 2:],
        radial_kappa[..., :-2],
        radial_kappa[..., 2:],
    ]
    flux_sum = jnp.zeros_like(source_fields)
    for near_field, near_kappa in zip(near_fields, near_kappas):
        conduct = 2.0 * conductivity * near_kappa / (conductivity + near_kappa)
        flux_sum = flux_sum + conduct * (near_field - source_fields)
    diffused = source_fields + 0.1 * flux_sum / volume_new
    return (volume_new, diffused, gradients)


def solution(mesh):
    in_specs = (
        P(None, "slab", "sector", None),
        P("slab", "sector", None),
        P("slab", "sector", None),
        P("slab", "sector", None),
        P("slab", "sector", None),
        P("slab", "sector", None),
        P(None, None, "slab", "sector", None),
        P(None, ("slab", "sector")),
        P(("slab", "sector"), None),
        P(("slab", "sector")),
    )
    out_specs = (
        P("slab", "sector", None),
        P(None, "slab", "sector", None),
        P(None, "slab", "sector", None),
    )
    return jax.shard_map(local, mesh=mesh, in_specs=in_specs, out_specs=out_specs, check_vma=False)
```

profile of v0, /device:TPU:0, one launch (start us, length us, event | category | flops | bytes accessed | tf_op | source)
XLA Modules:
  0.0 280.0 jit_solution(2600547571665993458)
XLA Ops:
  0.7 4.5 %bitcast_convert_fusion.7 = (f32[3,8,32,256]{3,2,1,0:T(8,128)S(1)}, f32[3,8,32,256]{3,2,1,0:T(8,128)}, f32[3,8,32,256]{3,2,1,0:T(8,128)}, f32[3,8,32,256]{3,2,1,...) fusion(bf16[3,8,8,32,256]{4,3,2,1,0:T(8,128)(2,1)} %param.24), kind=kLoop, calls=%fused_computation.84 | loop fusion | flops 1572864 | bytes 9437184 | tf_op jit(solution)/shard_map/mul | solution.py:54
  5.2 23.6 %broadcast_multiply_fusion.7 = (f32[3,9,8,32,256]{4,3,2,1,0:T(8,128)}, f32[3,9,8,32,256]{4,3,2,1,0:T(8,128)}, f32[3,9,8,32,256]{4,3,2,1,0:T(8,128)}, f32[3,9,8,3...) fusion(f32[9,8,32,256]{3,2,1,0:T(8,128)S(1)} %copy-done.1, ...), kind=kLoop, calls=%fused_computation.25 | loop fusion | flops 14155776 | bytes 65273856 | tf_op jit(solution)/shard_map/mul | solution.py:54
  28.7 36.1 %fusion.2 = (f32[28,8,32,256]{3,2,1,0:T(8,128)}, f32[28,8,32,256]{3,2,1,0:T(8,128)}, f32[28,8,32,256]{3,2,1,0:T(8,128)}, f32[28,8,32,256]{3,2,1,0:T(8,128)}, f32...) fusion(f32[1,8,32,256]{3,2,1,0:T(8,128)S(1)} %multiply_bitcast_, ...), kind=kLoop, calls=%fused_computation.13 | loop fusion | flops 25690112 | bytes 115605504 | tf_op jit(solution)/shard_map/concatenate | solution.py:55
  64.9 20.0 %pad_add_fusion = f32[28,9,33,256]{3,2,1,0:T(8,128)S(1)} fusion(f32[28,8,32,256]{3,2,1,0:T(8,128)} %get-tuple-element.87, f32[28,8,32,256]{3,2,1,0:T(8,128)} %get-tuple-element.83, f32[28,8,32,256]{3,2,1,0:T(8,128)} %get-tuple-element.85, f32[28,8,32,256]{3,2,1,0:T(8,128)} %get-tuple-element.82, f32[28,8,32,256]{3,2,1,0:T(8,128)} %get-tuple-element.86, ...), kind=kLoop, calls=%fused_computation.8 | loop fusion | flops 14902272 | bytes 67235840 | tf_op jit(solution)/shard_map/add | solution.py:59
  84.9 3.9 %copy-done = f32[28,9,33,256]{3,2,1,0:T(8,128)} copy-done((f32[28,9,33,256]{3,2,1,0:T(8,128)}, f32[28,9,33,256]{3,2,1,0:T(8,128)S(1)}, u32[]{:S(2)}) %copy-start) | copy-done | bytes 8515608
  90.3 1.5 collective-permute-start
  96.3 1.6 copy.84
  97.9 12.8 %scatter_custom_fusion = f32[10,8192]{0,1:T(8,128)} fusion(s32[4096]{0:T(1024)S(1)} %bitcast.115, f32[4096,10]{1,0:T(8,128)S(1)} %copy.84, f32[]{:T(128)} %constant.129.clone.1), kind=kCustom, calls=%fused_computation.65 | custom fusion | bytes 327684 | tf_op jit(solution)/shard_map/scatter | solution.py:83
  110.8 3.0 %copy.85 = f32[10,128,64]{2,0,1:T(8,128)S(1)} copy(f32[10,128,64]{0,2,1:T(8,128)} %bitcast.96) | data formatting | bytes 655360 | tf_op jit(solution)/shard_map/reshape | solution.py:86
  115.0 12.6 %all-to-all-start = ((f32[128,1,640]{2,1,0:T(1,128)}), f32[128,1,640]{2,1,0:T(1,128)S(1)}, u32[]{:S(2)}, u32[]{:S(2)}) async-start(f32[128,1,640]{2,1,0:T(1,128)} %reshape.283), calls=%async_computation | async-start | bytes 655360 | tf_op jit(solution)/shard_map/all_to_all | solution.py:85
  127.6 8.2 %slice.318 = f32[28,8,33,256]{3,2,1,0:T(8,128)} slice(f32[28,9,33,256]{3,2,1,0:T(8,128)} %copy-done), slice={[0:28], [0:8], [0:33], [0:256]} | slice | bytes 15138816 | tf_op jit(solution)/shard_map/slice | solution.py:63
  135.8 3.0 %all-to-all-done = f32[128,1,640]{2,1,0:T(1,128)S(1)} async-done(((f32[128,1,640]{2,1,0:T(1,128)}), f32[128,1,640]{2,1,0:T(1,128)S(1)}, u32[]{:S(2)}, u32[]{:S(2)}) %all-to-all-start) | async-done | bytes 327712 | tf_op jit(solution)/shard_map/all_to_all | solution.py:85
  141.4 2.9 %fusion.28 = f32[28,8,33,256]{3,2,1,0:T(8,128)} fusion(f32[28,8,33,256]{3,2,1,0:T(8,128)} %slice.318, f32[28,9,33,256]{3,2,1,0:T(8,128)} %copy-done, f32[28,33,256]{2,0,1:T(8,128)S(1)} %bitcast.106), kind=kLoop, calls=%fused_computation.69 | loop fusion | flops 236544 | bytes 3239936 | tf_op jit(solution)/shard_map/scatter-add | solution.py:63
  144.3 1.6 slice.321
  147.8 2.7 copy.87
  150.5 64.0 %scatter_custom_fusion.1 = f32[9,65536]{0,1:T(8,128)} fusion(s32[8192]{0:T(1024)S(1)} %bitcast.113, f32[8192,9]{1,0:T(8,128)} %copy.87, f32[]{:T(128)} %constant.129.clone.1), kind=kCustom, calls=%fused_computation.2 | custom fusion | flops 73728 | bytes 2359808 | tf_op jit(solution)/shard_map/scatter-add | solution.py:97
  214.4 20.5 %copy.88 = f32[9,8,32,256]{3,2,1,0:T(8,128)} copy(f32[9,8,32,256]{0,3,2,1:T(8,128)} %bitcast.87) | data formatting | bytes 4718592 | tf_op jit(solution)/shard_map/reshape | solution.py:99
  235.0 7.6 %slice.332 = f32[28,8,32,256]{3,2,1,0:T(8,128)} slice(f32[28,8,33,256]{3,2,1,0:T(8,128)} %fusion.28), slice={[0:28], [0:8], [0:32], [0:256]} | slice | bytes 14680064 | tf_op jit(solution)/shard_map/slice | solution.py:66
  245.2 5.1 %collective-permute-start.3 = (f32[10,1,32,256]{3,2,1,0:T(8,128)}, f32[10,1,32,256]{3,2,1,0:T(8,128)S(1)}, u32[]{:S(2)}, u32[]{:S(2)}) collective-permute-start(f32[10,1,32,256]{3,2,1,0:T(8,128)} %get-tuple-element.65), channel_id=1, source_target_pairs={{4,0},{8,4},{12,8},{16,12},{20,16},{24,20},{28,24},{32,28},{36,32}... | collective-permute-start | bytes 983048 | tf_op jit(solution)/shard_map/ppermute | solution.py:28
  250.3 2.4 slice_add_fusion.1
  252.7 6.2 %scatter-add.19 = f32[28,8,32,256]{3,2,1,0:T(8,128)} dynamic-update-slice(f32[28,8,32,256]{3,2,1,0:T(8,128)} %slice.332, f32[28,8,1,256]{3,2,1,0:T(1,128)} %slice_add_fusion.1, s32[]{:T(128)} %constant.130.clone.1, s32[]{:T(128)} %constant.130.clone.1, s32[]{:T(128)} %constant.130.clone.1, s32[]{:T(128)} %constant.130.clone.1) | dynamic-update-slice | bytes 458756 | tf_op jit(solution)/shard_map/scatter-add | solution.py:66
  260.2 3.5 %collective-permute-start.5 = (f32[10,10,1,256]{3,1,2,0:T(8,128)S(1)}, f32[10,10,1,256]{3,1,2,0:T(8,128)S(1)}, u32[]{:S(2)}, u32[]{:S(2)}) collective-permute-start(f32[10,10,1,256]{3,1,2,0:T(8,128)S(1)} %copy.90), channel_id=1, source_target_pairs={{1,0},{2,1},{3,2},{0,3},{5,4},{6,5},{7,6},{4,7},{9,8},{10,9},{11,1... | collective-permute-start | bytes 307208 | tf_op jit(solution)/shard_map/ppermute | solution.py:28
  263.7 7.6 %slice_divide_fusion = f32[27,8,32,256]{3,2,1,0:T(8,128)} fusion(f32[28,8,32,256]{3,2,1,0:T(8,128)} %scatter-add.19, f32[8,32,256]{2,1,0:T(8,128)S(1)} %slice_bitcast_fusion.1), kind=kLoop, calls=%fused_computation.15 | loop fusion | flops 1769472 | bytes 14417920 | tf_op jit(solution)/shard_map/div | solution.py:67
  272.0 8.0 %fusion.9 = f32[9,8,32,256]{3,2,1,0:T(8,128)} fusion(f32[9,8,32,256]{3,2,1,0:T(8,128)S(1)} %divide_add_fusion, f32[10,10,1,256]{3,2,1,0:T(1,128)S(1)} %copy.92, f32[10,1,32,256]{3,2,1,0:T(8,128)S(1)} %collective-permute-done.3, f32[10,1,32,256]{3,2,1,0:T(8,128)S(1)} %collective-permute-done.2, f32[1,8,32,256]{3,2,1,0:T(8,128)S(1)} %bitcast.101, ...), kind=kLoop, calls=%fused_computation.32 | loop fusion | flops 18874368 | bytes 7675904 | tf_op jit(solution)/shard_map/add | solution.py:132
  (93 shorter events, 15.8 us)
Async XLA Ops:
  0.6 4.5 %copy-start.9 = (f32[8,32,256]{2,1,0:T(8,128)S(1)}, f32[8,32,256]{2,1,0:T(8,128)}, u32[]{:S(2)}) copy-start(f32[8,32,256]{2,1,0:T(8,128)} %param.19) | copy-start | bytes 786436
  0.6 4.5 %copy-start.1 = (f32[9,8,32,256]{3,2,1,0:T(8,128)S(1)}, f32[9,8,32,256]{3,2,1,0:T(8,128)}, u32[]{:S(2)}) copy-start(f32[9,8,32,256]{3,2,1,0:T(8,128)} %param.18) | copy-start | bytes 7077892
  64.9 24.0 %copy-start.7 = (f32[8,32,256]{2,1,0:T(8,128)S(1)}, f32[8,32,256]{2,1,0:T(8,128)}, u32[]{:S(2)}) copy-start(f32[8,32,256]{2,1,0:T(8,128)} %param.20) | copy-start | bytes 786436
  84.9 3.9 %copy-start = (f32[28,9,33,256]{3,2,1,0:T(8,128)}, f32[28,9,33,256]{3,2,1,0:T(8,128)S(1)}, u32[]{:S(2)}) copy-start(f32[28,9,33,256]{3,2,1,0:T(8,128)S(1)} %pad_add_fusion) | copy-start | bytes 25546756
  88.8 3.0 %copy-start.15 = (s32[4096,1]{0,1:T(1,128)S(1)}, s32[4096,1]{0,1:T(1,128)}, u32[]{:S(2)}) copy-start(s32[4096,1]{0,1:T(1,128)} %param.26) | copy-start | bytes 49156
  90.3 51.1 %collective-permute-start = (f32[29,33,256]{2,0,1:T(8,128)}, f32[29,33,256]{2,0,1:T(8,128)S(1)}, u32[]{:S(2)}, u32[]{:S(2)}) collective-permute-start(f32[29,33,256]{2,0,1:T(8,128)} %copy.77), channel_id=1, source_target_pairs={{0,4},{4,8},{8,12},{12,16},{16,20},{20,24},{24,28},{28,32},{32,36}... | collective-permute-start | bytes 2939912 | tf_op jit(solution)/shard_map/ppermute | solution.py:10
  92.9 2.7 copy-start.16
  92.9 2.7 copy-start.12
  115.0 23.9 %all-to-all-start = ((f32[128,1,640]{2,1,0:T(1,128)}), f32[128,1,640]{2,1,0:T(1,128)S(1)}, u32[]{:S(2)}, u32[]{:S(2)}) async-start(f32[128,1,640]{2,1,0:T(1,128)} %reshape.283), calls=%async_computation | async-start | bytes 655360 | tf_op jit(solution)/shard_map/all_to_all | solution.py:85
  127.6 8.2 %copy-start.6 = (f32[8,32,256]{2,1,0:T(8,128)S(1)}, f32[8,32,256]{2,1,0:T(8,128)}, u32[]{:S(2)}) copy-start(f32[8,32,256]{2,1,0:T(8,128)} %param.21) | copy-start | bytes 786436
  146.7 96.0 %collective-permute-start.1 = (f32[29,8,256]{2,1,0:T(8,128)}, f32[29,8,256]{2,1,0:T(8,128)S(1)}, u32[]{:S(2)}, u32[]{:S(2)}) collective-permute-start(f32[29,8,256]{2,1,0:T(8,128)} %pad_maximum_fusion.19), channel_id=1, source_target_pairs={{0,1},{1,2},{2,3},{3,0},{4,5},{5,6},{6,7},{7,4},{8,9},{9,10},{10,1... | collective-permute-start | bytes 712712 | tf_op jit(solution)/shard_map/ppermute | solution.py:16
  235.0 8.4 %copy-start.8 = (f32[8,32,256]{2,1,0:T(8,128)S(1)}, f32[8,32,256]{2,1,0:T(8,128)}, u32[]{:S(2)}) copy-start(f32[8,32,256]{2,1,0:T(8,128)} %param.20) | copy-start | bytes 786436
  235.0 8.4 %slice-start = ((f32[8,32,256]{2,1,0:T(8,128)}), f32[7,32,256]{2,1,0:T(8,128)S(1)}, s32[]{:S(2)}) async-start(f32[8,32,256]{2,1,0:T(8,128)} %param.20), calls=%async_computation.1 | async-start | bytes 458752 | tf_op jit(solution)/shard_map/slice | solution.py:68
  235.0 8.4 %copy-start.10 = (f32[8,32,256]{2,1,0:T(8,128)S(1)}, f32[8,32,256]{2,1,0:T(8,128)}, u32[]{:S(2)}) copy-start(f32[8,32,256]{2,1,0:T(8,128)} %param.19) | copy-start | bytes 786436
  235.0 8.4 %copy-start.11 = (f32[8,32,256]{2,1,0:T(8,128)S(1)}, f32[8,32,256]{2,1,0:T(8,128)}, u32[]{:S(2)}) copy-start(f32[8,32,256]{2,1,0:T(8,128)} %param.22) | copy-start | bytes 786436
  235.0 8.6 %copy-start.2 = (f32[9,8,32,256]{3,2,1,0:T(8,128)S(1)}, f32[9,8,32,256]{3,2,1,0:T(8,128)}, u32[]{:S(2)}) copy-start(f32[9,8,32,256]{3,2,1,0:T(8,128)} %param.18) | copy-start | bytes 7077892
  235.0 8.6 %copy-start.3 = (f32[9,8,32,256]{3,2,1,0:T(8,128)S(1)}, f32[9,8,32,256]{3,2,1,0:T(8,128)}, u32[]{:S(2)}) copy-start(f32[9,8,32,256]{3,2,1,0:T(8,128)} %copy.88) | copy-start | bytes 7077892
  243.4 1.0 copy-start.4
  243.6 28.4 %copy-start.5 = (f32[8,32,256]{2,1,0:T(8,128)}, f32[8,32,256]{2,1,0:T(8,128)S(1)}, u32[]{:S(2)}) copy-start(f32[8,32,256]{2,1,0:T(8,128)S(1)} %fusion.30) | copy-start | bytes 786436
  243.6 6.6 %copy-start.14 = (f32[29,8,256]{2,1,0:T(8,128)S(1)}, f32[29,8,256]{2,1,0:T(8,128)}, u32[]{:S(2)}) copy-start(f32[29,8,256]{2,1,0:T(8,128)} %copy-done.13) | copy-start | bytes 712708
  245.2 14.7 %collective-permute-start.2 = (f32[10,1,32,256]{3,2,1,0:T(8,128)}, f32[10,1,32,256]{3,2,1,0:T(8,128)S(1)}, u32[]{:S(2)}, u32[]{:S(2)}) collective-permute-start(f32[10,1,32,256]{3,2,1,0:T(8,128)} %get-tuple-element.64), channel_id=1, source_target_pairs={{0,4},{4,8},{8,12},{12,16},{16,20},{20,24},{24,28},{28,32},{32,36}... | collective-permute-start | bytes 983048 | tf_op jit(solution)/shard_map/ppermute | solution.py:26
  245.2 14.7 %collective-permute-start.3 = (f32[10,1,32,256]{3,2,1,0:T(8,128)}, f32[10,1,32,256]{3,2,1,0:T(8,128)S(1)}, u32[]{:S(2)}, u32[]{:S(2)}) collective-permute-start(f32[10,1,32,256]{3,2,1,0:T(8,128)} %get-tuple-element.65), channel_id=1, source_target_pairs={{4,0},{8,4},{12,8},{16,12},{20,16},{24,20},{28,24},{32,28},{36,32}... | collective-permute-start | bytes 983048 | tf_op jit(solution)/shard_map/ppermute | solution.py:28
  260.1 11.2 %collective-permute-start.4 = (f32[10,10,1,256]{3,1,2,0:T(8,128)S(1)}, f32[10,10,1,256]{3,1,2,0:T(8,128)S(1)}, u32[]{:S(2)}, u32[]{:S(2)}) collective-permute-start(f32[10,10,1,256]{3,1,2,0:T(8,128)S(1)} %copy.89), channel_id=1, source_target_pairs={{0,1},{1,2},{2,3},{3,0},{4,5},{5,6},{6,7},{7,4},{8,9},{9,10},{10,1... | collective-permute-start | bytes 307208 | tf_op jit(solution)/shard_map/ppermute | solution.py:26
  260.2 11.2 %collective-permute-start.5 = (f32[10,10,1,256]{3,1,2,0:T(8,128)S(1)}, f32[10,10,1,256]{3,1,2,0:T(8,128)S(1)}, u32[]{:S(2)}, u32[]{:S(2)}) collective-permute-start(f32[10,10,1,256]{3,1,2,0:T(8,128)S(1)} %copy.90), channel_id=1, source_target_pairs={{1,0},{2,1},{3,2},{0,3},{5,4},{6,5},{7,6},{4,7},{9,8},{10,9},{11,1... | collective-permute-start | bytes 307208 | tf_op jit(solution)/shard_map/ppermute | solution.py:28
  (1 other events, 0.7 us)
where the time goes:
time: 281 us; the launch traced here: 280 us
  other arithmetic  177 us (63%)
  local copies, waits for them, and re-layouts  75.4 us (27%)
  starting transfers between devices  23.5 us (8%)
  waiting for transfers between devices  3.06 us (1%)
    scatter-add x1, other arithmetic, local(): deposit = jnp.zeros((field_n, axial_n * angle_n * radial_n), jnp.float32)...  64 us
    concatenate x1, other arithmetic, local(): terms = jnp.concatenate([terms, (volume * 0.125)[None]], 0)  36.1 us
    mul x2, other arithmetic, local(): areas[:, None] * fields[None]  28.1 us
    reshape x1, local copies, waits for them, and re-layouts, local(): deposit = deposit.reshape(field_n, axial_n, angle_n, radial_n)  20.5 us
    add x1, other arithmetic, local(): node_sums = node_sums + terms  20 us
    scatter x1, local copies, waits for them, and re-layouts, local(): jnp.zeros((field_n + 1, device_count * capacity), jnp.float32)  12.8 us
    all_to_all x1, starting transfers between devices, local(): lax.all_to_all(outgoing.reshape(field_n + 1, device_count, capacity), ('s...  12.6 us
    ppermute x2, starting transfers between devices, with_halo(): lax.ppermute(head, axis, [((i + 1) % count, i) for i in range(count)])  8.61 us
  transfers between devices with their start and end apart: 7, of which 1 were waited for; matrix products, arithmetic and copies ran while one was open for 52% of the time, Pallas kernels for 0%

commit v1 on v0

v1 whole, which is shorter than its diff:
```python
import jax
import jax.numpy as jnp
from jax import lax
from jax.experimental import pallas as pl
from jax.experimental.pallas import tpu as pltpu

F32, BF16, I32 = jnp.float32, jnp.bfloat16, jnp.int32
VM = pl.BlockSpec(memory_space=pltpu.VMEM)


def nt(a, b):
    return lax.dot_general(a, b, (((1,), (1,)), ((), ())), preferred_element_type=F32)


def iota(shape, dim):
    return lax.broadcasted_iota(I32, shape, dim)


def one_hot(row, count):
    n = row.shape[1]
    return jnp.where(iota((count, n), 0) == row, 1.0, 0.0).astype(BF16)


def split(x):
    hi = x.astype(BF16)
    return hi, (x - hi.astype(F32)).astype(BF16)


def before(n):
    return jnp.where(iota((n, n), 0) < iota((n, n), 1), 1.0, 0.0).astype(BF16)


def bucket_kernel(loads_ref, dest_ref, cell_ref, out_ref, acc_ref):
    blk = 256
    devices = 128
    earlier = before(blk)
    carry = jnp.zeros((devices, 1), F32)
    acc_ref[...] = jnp.zeros_like(acc_ref)
    for b in range(4096 // blk):
        sl = pl.ds(b * blk, blk)
        d = one_hot(dest_ref[:, sl], devices)
        df = d.astype(F32)
        count = jnp.dot(d, earlier, preferred_element_type=F32)
        rank = jnp.sum(df * (count + carry), axis=0, keepdims=True).astype(I32)
        carry = carry + jnp.sum(df, axis=1, keepdims=True)
        o = one_hot(rank, 64)
        hi, lo = split(loads_ref[:, sl])
        cell = cell_ref[:, sl]
        row = (lax.shift_right_logical(cell, 8) * 256).astype(F32).astype(BF16)
        col = ((cell & 255) + 1).astype(F32).astype(BF16)
        his = [hi[c : c + 1] * o for c in range(9)] + [row * o]
        los = [lo[c : c + 1] * o for c in range(9)] + [col * o]
        rhs = jnp.concatenate([jnp.concatenate(his, 0), jnp.concatenate(los, 0)], 1)
        acc_ref[...] += nt(jnp.concatenate([d, d], 1), rhs)
    for s in range(5):
        out_ref[:, s, :] = acc_ref[:, s * 128 : (s + 1) * 128]


def bucket(loads, dest, cell):
    return pl.pallas_call(
        bucket_kernel,
        out_shape=jax.ShapeDtypeStruct((128, 5, 128), F32),
        in_specs=[VM] * 3,
        out_specs=VM,
        scratch_shapes=[pltpu.VMEM((128, 640), F32)],
        name="bucket",
    )(loads, dest.reshape(1, 4096), cell.reshape(1, 4096))


GROUPS, ROWS, SLOTS, CHUNK = 16, 16, 256, 2048


def deposit_kernel(
    recv_ref, fields_ref, vol_ref, sa_ref, st_ref, sr_ref, saz_ref, stt_ref,
    vn_ref, src_ref, zlo_ref, zhi_ref, tlo_ref, thi_ref,
    chan_ref, sort_ref, acc_ref, rank_ref,
):
    sa, st, sr = sa_ref[...], st_ref[...], sr_ref[...]
    for a in range(8):
        below = saz_ref[...] if a == 0 else sa_ref[a - 1]
        stp = st_ref[a]
        row = iota((32, 256), 0)
        side = jnp.where(row == 0, stt_ref[a : a + 1], pltpu.roll(stp, 1, 0))
        srp = sr_ref[a]
        lane = iota((32, 256), 1)
        inner = jnp.where(lane == 0, 0.0, pltpu.roll(srp, 1, 1))
        vn_ref[a] = vol_ref[a] + sa_ref[a] - below + stp - side + srp - inner
    lane = iota((64, 128), 1) < 64
    for s in range(5):
        first, second = recv_ref[0:64, s, :], recv_ref[64:128, s, :]
        chan_ref[2 * s] = jnp.where(lane, first, pltpu.roll(second, 64, 1))
        chan_ref[2 * s + 1] = jnp.where(lane, pltpu.roll(first, 64, 1), second)
    acc_ref[...] = jnp.zeros_like(acc_ref)
    earlier = before(256)

    def rows_of(c, start, count):
        part = chan_ref[c, start : start + count, :]
        return jnp.concatenate([part[i : i + 1] for i in range(count)], 1)

    for ch in range(8192 // CHUNK):
        nrow = CHUNK // 128
        carry = jnp.zeros((GROUPS, 1), F32)
        cell = rows_of(9, ch * nrow, nrow).astype(I32) - 1
        group = lax.shift_right_arithmetic(cell, 12)
        g = one_hot(group, GROUPS)
        gf = g.astype(F32)
        ranks = []
        for b in range(CHUNK // 256):
            gb = gf[:, b * 256 : (b + 1) * 256]
            count = jnp.dot(g[:, b * 256 : (b + 1) * 256], earlier, preferred_element_type=F32)
            ranks.append(jnp.sum(gb * (count + carry) , axis=0, keepdims=True))
            carry = carry + jnp.sum(gb, axis=1, keepdims=True)
        rank_ref[...] = jnp.concatenate(ranks, 1).astype(I32)
        most = jnp.max(carry).astype(I32)
        his, los = [], []
        for c in range(9):
            hi, lo = split(rows_of(c, ch * nrow, nrow))
            his.append(hi * g)
            los.append(lo * g)
        rowin = (lax.shift_right_logical(cell, 8) & 15).astype(F32).astype(BF16)
        colin = (cell & 255).astype(F32).astype(BF16)
        lhs = jnp.concatenate(his + los + [(rowin + 1.0) * g, colin * g], 0)

        def one_round(r, carry_unused):
            o = one_hot(rank_ref[...] - r * SLOTS, SLOTS)
            sort_ref[...] = nt(lhs, o)
            for gi in range(GROUPS):
                pick = lambda c: sort_ref[c * GROUPS + gi : c * GROUPS + gi + 1, :]
                rm = one_hot(pick(18).astype(I32) - 1, ROWS)
                j = one_hot(pick(19).astype(I32), 256)
                left = jnp.concatenate([pick(c).astype(BF16) * rm for c in range(18)], 0)
                out = nt(left, j)
                for f in range(9):
                    acc_ref[f, gi // 2, (gi % 2) * 16 : (gi % 2) * 16 + 16, :] += (
                        out[f * 16 : f * 16 + 16] + out[(9 + f) * 16 : (9 + f) * 16 + 16]
                    )
            return carry_unused

        lax.fori_loop(0, (most + SLOTS - 1) // SLOTS, one_round, 0)
    for a in range(8):
        inv = 1.0 / vn_ref[a]
        for f in range(9):
            v = fields_ref[f, a] + acc_ref[f, a] * inv
            src_ref[f, a] = v
            if a == 0:
                zlo_ref[f] = v
            if a == 7:
                zhi_ref[f] = v
            tlo_ref[f, a : a + 1, :] = v[0:1]
            thi_ref[f, a : a + 1, :] = v[31:32]


def deposit(recv, fields, volume, sa, st, sr, saz, stt):
    sd = jax.ShapeDtypeStruct
    return pl.pallas_call(
        deposit_kernel,
        out_shape=(
            sd((8, 32, 256), F32), sd((9, 8, 32, 256), F32),
            sd((9, 32, 256), F32), sd((9, 32, 256), F32), sd((9, 8, 256), F32), sd((9, 8, 256), F32),
        ),
        in_specs=[VM] * 8,
        out_specs=[VM] * 6,
        scratch_shapes=[
            pltpu.VMEM((10, 64, 128), F32),
            pltpu.VMEM((320, 256), F32),
            pltpu.VMEM((9, 8, 32, 256), F32),
            pltpu.VMEM((1, CHUNK), I32),
        ],
        name="deposit",
    )(recv, fields, volume, sa, st, sr, saz, stt)


def t_shift(x, edge):
    return jnp.where(iota(x.shape, 0) == 0, edge, pltpu.roll(x, 1, 0))


def r_shift(x):
    n = x.shape[1]
    return jnp.where(iota(x.shape, 1) == n - 1, 0.0, pltpu.roll(x, n - 1, 1))


def gradient_kernel(fields_ref, areas_ref, vol_ref, zh_ref, th_ref, out_ref, fv_ref, a1_ref, a0_ref, w_ref):
    a = pl.program_id(0)
    now = lax.rem(a, 2)
    prev = 1 - now

    def prepare(slot, field, area1, vol, edge):
        for f in range(9):
            x = field(f)
            xt = t_shift(x, edge(f))
            fv_ref[slot, 0, f] = r_shift(x)
            fv_ref[slot, 1, f] = x
            fv_ref[slot, 2, f] = r_shift(xt)
            fv_ref[slot, 3, f] = xt
        for i in range(3):
            for q in range(4):
                x = area1(i, q)
                if q // 2 == 1:
                    x = t_shift(x, edge(9 + 4 * i + 2 + q % 2))
                a1_ref[slot, i, q] = x if q % 2 == 1 else pltpu.roll(x, 255, 1)
        v = vol * 0.125
        v = v + t_shift(v, edge(21) * 0.125)
        w_ref[slot] = v + r_shift(v)

    @pl.when(a == 0)
    def _():
        prepare(1, lambda f: zh_ref[f], lambda i, q: zh_ref[9 + 4 * i + q], zh_ref[21],
                lambda c: th_ref[c, 8:9, :])

    here = lambda c: th_ref[c, pl.ds(a, 1), :]
    prepare(now, lambda f: fields_ref[f, 0], lambda i, q: areas_ref[i, 4 + q, 0].astype(F32), vol_ref[0], here)
    for i in range(3):
        for q in range(4):
            x = areas_ref[i, q, 0].astype(F32)
            if q // 2 == 1:
                x = t_shift(x, here(9 + 4 * i + q % 2))
            a0_ref[i, q] = x if q % 2 == 1 else pltpu.roll(x, 255, 1)
    for t in range(4):
        for h in range(2):
            at = (pl.ds(8 * t, 8), pl.ds(128 * h, 128))
            acc = [[None] * 9 for _ in range(3)]
            for dz in range(2):
                slot = prev if dz else now
                for q in range(4):
                    area = [(a1_ref[(slot, i, q) + at] if dz else a0_ref[(i, q) + at]) for i in range(3)]
                    for f in range(9):
                        x = fv_ref[(slot, q, f) + at]
                        for i in range(3):
                            term = area[i] * x
                            acc[i][f] = term if acc[i][f] is None else acc[i][f] + term
            inv = 1.0 / (w_ref[(now,) + at] + w_ref[(prev,) + at])
            for i in range(3):
                for f in range(9):
                    out_ref[(9 * i + f, 0) + at] = acc[i][f] * inv


def gradients(fields, areas, volume, zh, th):
    whole = lambda shape: pl.BlockSpec(shape, lambda a: (0,) * len(shape))
    return pl.pallas_call(
        gradient_kernel,
        grid=(8,),
        out_shape=jax.ShapeDtypeStruct((27, 8, 32, 256), F32),
        in_specs=[
            pl.BlockSpec((9, 1, 32, 256), lambda a: (0, a, 0, 0)),
            pl.BlockSpec((3, 8, 1, 32, 256), lambda a: (0, 0, a, 0, 0)),
            pl.BlockSpec((1, 32, 256), lambda a: (a, 0, 0)),
            whole((24, 32, 256)),
            whole((24, 9, 256)),
        ],
        out_specs=pl.BlockSpec((27, 1, 32, 256), lambda a: (0, a, 0, 0)),
        scratch_shapes=[
            pltpu.VMEM((2, 4, 9, 32, 256), F32),
            pltpu.VMEM((2, 3, 4, 32, 256), F32),
            pltpu.VMEM((3, 4, 32, 256), F32),
            pltpu.VMEM((2, 32, 256), F32),
        ],
        cost_estimate=pl.CostEstimate(flops=30_000_000, bytes_accessed=14_000_000, transcendentals=0),
        name="gradients",
    )(fields, areas, volume, zh, th)


def diffuse_kernel(src_ref, zlo_ref, zhi_ref, tlo_ref, thi_ref, k_ref, vn_ref, kzl_ref, kzh_ref, ktl_ref, kth_ref, out_ref, w_ref):
    row = iota((32, 256), 0)
    lane = iota((32, 256), 1)

    @pl.when(pl.program_id(0) == 0)
    def _():
        for a in range(8):
            k = k_ref[a]
            near = [
                kzl_ref[...] if a == 0 else k_ref[a - 1],
                kzh_ref[...] if a == 7 else k_ref[a + 1],
                jnp.where(row == 0, ktl_ref[a : a + 1], pltpu.roll(k, 1, 0)),
                jnp.where(row == 31, kth_ref[a : a + 1], pltpu.roll(k, 31, 0)),
                jnp.where(lane == 0, 0.0, pltpu.roll(k, 1, 1)),
                jnp.where(lane == 255, 0.0, pltpu.roll(k, 255, 1)),
            ]
            scale = (0.2 * k) / vn_ref[a]
            total = None
            for n, kn in enumerate(near):
                w = scale * kn / (k + kn)
                w_ref[n, a] = w
                total = w if total is None else total + w
            w_ref[6, a] = 1.0 - total

    for a in range(8):
        s = src_ref[0, a]
        near = [
            zlo_ref[0] if a == 0 else src_ref[0, a - 1],
            zhi_ref[0] if a == 7 else src_ref[0, a + 1],
            jnp.where(row == 0, tlo_ref[0, a : a + 1], pltpu.roll(s, 1, 0)),
            jnp.where(row == 31, thi_ref[0, a : a + 1], pltpu.roll(s, 31, 0)),
            pltpu.roll(s, 1, 1),
            pltpu.roll(s, 255, 1),
        ]
        out = w_ref[6, a] * s
        for n in range(6):
            out = out + w_ref[n, a] * near[n]
        out_ref[0, a] = out


def diffuse(src, zlo, zhi, tlo, thi, k, vn, kzl, kzh, ktl, kth):
    whole = lambda shape: pl.BlockSpec(shape, lambda f: (0,) * len(shape))
    each = lambda shape: pl.BlockSpec((1,) + shape, lambda f: (f,) + (0,) * len(shape))
    return pl.pallas_call(
        diffuse_kernel,
        grid=(9,),
        out_shape=jax.ShapeDtypeStruct((9, 8, 32, 256), F32),
        in_specs=[
            each((8, 32, 256)), each((32, 256)), each((32, 256)), each((8, 256)), each((8, 256)),
            whole((8, 32, 256)), whole((8, 32, 256)), whole((32, 256)), whole((32, 256)), whole((8, 256)), whole((8, 256)),
        ],
        out_specs=each((8, 32, 256)),
        scratch_shapes=[pltpu.VMEM((7, 8, 32, 256), F32)],
        name="diffuse",
    )(src, zlo, zhi, tlo, thi, k, vn, kzl, kzh, ktl, kth)


def exchange_kernel(src_ref, out_ref, send_sem, recv_sem, own_sem):
    slab, sector = lax.axis_index("slab"), lax.axis_index("sector")
    me = slab * 4 + sector
    own = pltpu.make_async_copy(src_ref.at[me], out_ref.at[me], own_sem)
    own.start()

    def send(k, unused):
        to = lax.rem(me + k, 128)
        pltpu.make_async_remote_copy(
            src_ref=src_ref.at[to],
            dst_ref=out_ref.at[me],
            send_sem=send_sem,
            recv_sem=recv_sem,
            device_id=(to // 4, lax.rem(to, 4)),
            device_id_type=pl.DeviceIdType.MESH,
        ).start()
        return unused

    lax.fori_loop(1, 128, send, 0)
    own.wait()
    most = pl.ds(0, 127)
    pltpu.make_async_copy(src_ref.at[most], out_ref.at[most], send_sem).wait()
    pltpu.make_async_copy(src_ref.at[most], out_ref.at[most], recv_sem).wait()


def exchange(outgoing):
    hbm = pl.BlockSpec(memory_space=pl.ANY)
    return pl.pallas_call(
        exchange_kernel,
        out_shape=jax.ShapeDtypeStruct((128, 5, 128), F32),
        in_specs=[hbm],
        out_specs=hbm,
        scratch_shapes=[pltpu.SemaphoreType.DMA, pltpu.SemaphoreType.DMA, pltpu.SemaphoreType.DMA],
        compiler_params=pltpu.CompilerParams(has_side_effects=True),
        name="exchange",
    )(outgoing)


def up(x):
    return lax.ppermute(x, "slab", [(i, i + 1) for i in range(31)])


def down(x):
    return lax.ppermute(x, "slab", [(i + 1, i) for i in range(31)])


def onward(x):
    return lax.ppermute(x, "sector", [(i, (i + 1) % 4) for i in range(4)])


def backward(x):
    return lax.ppermute(x, "sector", [((i + 1) % 4, i) for i in range(4)])


def local(fields, volume, swept_axial, swept_angular, swept_radial, conductivity, corner_areas, parcel_loads, dest_device, dest_cell):
    zh = up(jnp.concatenate(
        [fields[:, 7], corner_areas[:, 4:8, 7].astype(F32).reshape(12, 32, 256), volume[7:8], swept_axial[7:8], conductivity[7:8]], 0
    ))
    k_above = down(conductivity[0])
    k_next = backward(conductivity[:, 0])
    own = jnp.concatenate(
        [fields[:, :, 31], jnp.stack([corner_areas[:, k, :, 31] for k in (2, 3, 6, 7)], 1).astype(F32).reshape(12, 8, 256),
         volume[:, 31][None], swept_angular[:, 31][None], conductivity[:, 31][None]], 0
    )
    th = onward(jnp.concatenate([own, zh[:, 31:32]], 1))
    outgoing = bucket(parcel_loads, dest_device, dest_cell)
    recv = exchange(outgoing)
    vn, src, zlo, zhi, tlo, thi = deposit(
        recv, fields, volume, swept_axial, swept_angular, swept_radial, zh[22], th[22, :8]
    )
    below, above = up(zhi), down(zlo)
    before_, after = onward(thi), backward(tlo)
    grads = gradients(fields, corner_areas, volume, zh, th)
    diffused = diffuse(src, below, above, before_, after, conductivity, vn, zh[23], k_above, th[23, :8], k_next)
    return vn, diffused, grads


def solution(mesh):
    P = jax.sharding.PartitionSpec
    cells = P("slab", "sector", None)
    in_specs = (
        P(None, "slab", "sector", None), cells, cells, cells, cells, cells,
        P(None, None, "slab", "sector", None), P(None, ("slab", "sector")), P(("slab", "sector"), None), P(("slab", "sector")),
    )
    out_specs = (cells, P(None, "slab", "sector", None), P(None, "slab", "sector", None))
    return jax.shard_map(local, mesh=mesh, in_specs=in_specs, out_specs=out_specs, check_vma=False)
```

time: 281 us -> 109 us (0.39)
  the two profiles are of different devices: /device:TPU:0 before, /device:TPU:33 now
where the time goes in v1:
time: 109 us; the launch traced here: 108 us
  Pallas kernels  63.1 us (58%)
  starting transfers between devices  19.2 us (18%)
  waiting for transfers between devices  13.2 us (12%)
  local copies, waits for them, and re-layouts  11.3 us (10%)
    pallas_call x1, Pallas kernels, exchange(): pl.pallas_call(exchange_kernel, out_shape=jax.ShapeDtypeStruct((128, 5, 1...  19.6 us
    pallas_call x1, Pallas kernels, deposit(): pl.pallas_call(deposit_kernel, out_shape=(sd((8, 32, 256), F32), sd((9, 8...  14.3 us
    pallas_call x1, Pallas kernels, gradients(): pl.pallas_call(gradient_kernel, grid=(8,), out_shape=jax.ShapeDtypeStruct...  13 us
    ppermute x2, waiting for transfers between devices, onward(): return lax.ppermute(x, 'sector', [(i, (i + 1) % 4) for i in range(4)])  10.4 us
    ppermute x2, starting transfers between devices, down(): return lax.ppermute(x, 'slab', [(i + 1, i) for i in range(31)])  9.32 us
    pallas_call x1, Pallas kernels, bucket(): pl.pallas_call(bucket_kernel, out_shape=jax.ShapeDtypeStruct((128, 5, 128...  8.23 us
    pallas_call x1, Pallas kernels, diffuse(): pl.pallas_call(diffuse_kernel, grid=(9,), out_shape=jax.ShapeDtypeStruct(...  7.96 us
    ppermute x2, starting transfers between devices, up(): return lax.ppermute(x, 'slab', [(i, i + 1) for i in range(31)])  6.62 us
  transfers between devices with their start and end apart: 8, of which 2 were waited for; matrix products, arithmetic and copies ran while one was open for 5% of the time, Pallas kernels for 38%

profile of v1, /device:TPU:33, one launch (start us, length us, event | category | flops | bytes accessed | tf_op | source)
XLA Modules:
  0.0 107.7 jit_solution(9870022621887387421)
XLA Ops:
  0.6 0.9 slice.61
  1.6 1.0 bitcast_dynamic-update-slice_fusion
  2.6 0.8 slice_dynamic-update-slice_fusion.2
  3.4 0.8 slice_dynamic-update-slice_fusion.1
  4.1 0.8 slice_bitcast_fusion.2
  4.9 3.7 %collective-permute-start = (f32[24,32,256]{2,1,0:T(8,128)S(1)}, f32[24,32,256]{2,1,0:T(8,128)S(1)}, u32[]{:S(2)}, u32[]{:S(2)}) collective-permute-start(f32[24,32,256]{2,1,0:T(8,128)S(1)} %get-tuple-element.26), channel_id=1, source_target_pairs={{0,4},{4,8},{8,12},{12,16},{16,20},{20,24},{24,28},{28,32},{32,36}... | collective-permute-start | bytes 2359304 | tf_op jit(solution)/shard_map/ppermute | solution.py:358
  8.6 0.9 slice.71
  9.4 1.1 %slice.66 = f32[9,8,1,256]{3,2,1,0:T(1,128)S(1)} slice(f32[9,8,32,256]{3,2,1,0:T(8,128)} %fields_ref.3), slice={[0:9], [0:8], [31:32], [0:256]} | slice | bytes 147456 | tf_op jit(solution)/shard_map/slice | solution.py:380
  10.6 1.2 %fusion.1 = (bf16[3,1,8,1,256]{4,3,2,1,0:T(2,128)(2,1)S(1)}, bf16[3,1,8,1,256]{4,3,2,1,0:T(2,128)(2,1)S(1)}, bf16[3,1,8,1,256]{4,3,2,1,0:T(2,128)(2,1)S(1)}, bf16[3,1,8,1,256]{4,3,2,1,0:T(2,128)(2,1)S(1)}) fusion(bf16[3,8,8,32,256]{4,3,2,1,0:T(8,128)(2,1)} %areas_ref.1), kind=kLoop, calls=%fused_computation.26 | loop fusion | bytes 98304 | tf_op jit(solution)/shard_map/slice | solution.py:380
  11.9 0.9 slice.72
  12.7 8.2 %bucket.1.src_ref = f32[128,5,128]{2,1,0:T(8,128)} custom-call(f32[9,4096]{1,0:T(8,128)} %loads_ref.1, s32[1,4096]{1,0:T(1,128)} %bitcast.48, s32[1,4096]{1,0:T(1,128)} %bitcast.49), custom_call_target="tpu_custom_call" | custom-call | tf_op jit(solution)/shard_map/bucket/pallas_call | solution.py:60
  20.9 19.6 %exchange.1.recv_ref = f32[128,5,128]{2,1,0:T(8,128)} custom-call(f32[128,5,128]{2,1,0:T(8,128)} %bucket.1.src_ref), custom_call_target="tpu_custom_call" | custom-call | tf_op jit(solution)/shard_map/exchange/pallas_call | solution.py:346
  40.6 0.9 fusion.2
  42.0 0.6 slice_bitcast_fusion
  42.7 10.4 %collective-permute-done.1.th_ref = f32[24,9,256]{2,1,0:T(8,128)S(1)} collective-permute-done((f32[24,9,256]{2,1,0:T(8,128)S(1)}, f32[24,9,256]{2,1,0:T(8,128)S(1)}, u32[]{:S(2)}, u32[]{:S(2)}) %collective-permute-start.1) | collective-permute-done | bytes 221216 | tf_op jit(solution)/shard_map/ppermute | solution.py:366
  53.1 0.6 slice_bitcast_fusion.3
  53.7 14.3 %deposit.1 = (f32[8,32,256]{2,1,0:T(8,128)}, f32[9,8,32,256]{3,2,1,0:T(8,128)}, f32[9,32,256]{2,1,0:T(8,128)}, f32[9,32,256]{2,1,0:T(8,128)}, f32[9,8,256]{2,1,0:T(8,128)}, /*index=5*/f32[9,8,256]{2,1,0:T(8,128)}) custom-call(f32[128,5,128]{2,1,0:T(8,128)} %exchange.1.recv_ref, f32[9,8,32,256]{3,2,1,0:T(8,128)} %fields_ref.3, f32[8,32,256]{2,1,0:T(8,128)} %vol_ref.3, ...), custom_call_target="tpu_custom_call" | custom-call | tf_op jit(solution)/shard_map/deposit/pallas_call | solution.py:155
  68.0 3.0 %collective-permute-start.2 = (f32[9,32,256]{2,1,0:T(8,128)}, f32[9,32,256]{2,1,0:T(8,128)S(1)}, u32[]{:S(2)}, u32[]{:S(2)}) collective-permute-start(f32[9,32,256]{2,1,0:T(8,128)} %get-tuple-element.11), channel_id=1, source_target_pairs={{0,4},{4,8},{8,12},{12,16},{16,20},{20,24},{24,28},{28,32},{32,36}... | collective-permute-start | bytes 884744 | tf_op jit(solution)/shard_map/ppermute | solution.py:358
  71.0 2.2 %collective-permute-start.3 = (f32[9,32,256]{2,1,0:T(8,128)}, f32[9,32,256]{2,1,0:T(8,128)S(1)}, u32[]{:S(2)}, u32[]{:S(2)}) collective-permute-start(f32[9,32,256]{2,1,0:T(8,128)} %get-tuple-element.12), channel_id=1, source_target_pairs={{4,0},{8,4},{12,8},{16,12},{20,16},{24,20},{28,24},{32,28},{36,32}... | collective-permute-start | bytes 884744 | tf_op jit(solution)/shard_map/ppermute | solution.py:362
  73.2 2.7 %collective-permute-start.5 = (f32[9,8,256]{2,1,0:T(8,128)}, f32[9,8,256]{2,1,0:T(8,128)S(1)}, u32[]{:S(2)}, u32[]{:S(2)}) collective-permute-start(f32[9,8,256]{2,1,0:T(8,128)} %get-tuple-element.14), channel_id=1, source_target_pairs={{1,0},{2,1},{3,2},{0,3},{5,4},{6,5},{7,6},{4,7},{9,8},{10,9},{11,1... | collective-permute-start | bytes 221192 | tf_op jit(solution)/shard_map/ppermute | solution.py:370
  75.9 2.8 %collective-permute-done.7.kth_ref = f32[8,256]{1,0:T(8,128)S(1)} collective-permute-done((f32[8,256]{1,0:T(8,128)S(1)}, f32[8,256]{1,0:T(8,128)S(1)}, u32[]{:S(2)}, u32[]{:S(2)}) %collective-permute-start.7) | collective-permute-done | bytes 8224 | tf_op jit(solution)/shard_map/ppermute | solution.py:370
  78.7 7.2 %collective-permute-start.6 = (f32[32,256]{1,0:T(8,128)S(1)}, f32[32,256]{1,0:T(8,128)S(1)}, u32[]{:S(2)}, u32[]{:S(2)}) collective-permute-start(f32[32,256]{1,0:T(8,128)S(1)} %get-tuple-element.25), channel_id=1, source_target_pairs={{4,0},{8,4},{12,8},{16,12},{20,16},{24,20},{28,24},{32,28},{36,32}... | collective-permute-start | bytes 98312 | tf_op jit(solution)/shard_map/ppermute | solution.py:362
  85.9 13.0 %gradients.1 = f32[27,8,32,256]{3,2,1,0:T(8,128)} custom-call(f32[9,8,32,256]{3,2,1,0:T(8,128)} %fields_ref.3, bf16[3,8,8,32,256]{4,3,2,1,0:T(8,128)(2,1)} %areas_ref.1, f32[8,32,256]{2,1,0:T(8,128)} %vol_ref.3, f32[24,32,256]{2,1,0:T(8,128)} %copy-done, f32[24,9,256]{2,1,0:T(8,128)} %copy-done.1), custom_call_target="tpu_custom_call" | custom-call | flops 30000000 | bytes 14000000 | tf_op jit(solution)/shard_map/gradients/pallas_call | solution.py:239
  99.8 8.0 %diffuse.1 = f32[9,8,32,256]{3,2,1,0:T(8,128)} custom-call(f32[9,8,32,256]{3,2,1,0:T(8,128)} %get-tuple-element.10.src_ref, f32[9,32,256]{2,1,0:T(8,128)} %copy-done.2, f32[9,32,256]{2,1,0:T(8,128)} %copy-done.3, f32[9,8,256]{2,1,0:T(8,128)} %copy-done.4, f32[9,8,256]{2,1,0:T(8,128)} %copy-done.5, f32[8,32,256]{2,1,0:T(8,128)} %k_ref.1, ...), custom_call_target="tpu_custom_call" | custom-call | tf_op jit(solution)/shard_map/diffuse/pallas_call | solution.py:305
  (38 shorter events, 1.6 us)
Async XLA Ops:
  4.9 36.6 %collective-permute-start = (f32[24,32,256]{2,1,0:T(8,128)S(1)}, f32[24,32,256]{2,1,0:T(8,128)S(1)}, u32[]{:S(2)}, u32[]{:S(2)}) collective-permute-start(f32[24,32,256]{2,1,0:T(8,128)S(1)} %get-tuple-element.26), channel_id=1, source_target_pairs={{0,4},{4,8},{8,12},{12,16},{16,20},{20,24},{24,28},{28,32},{32,36}... | collective-permute-start | bytes 2359304 | tf_op jit(solution)/shard_map/ppermute | solution.py:358
  41.5 26.5 %copy-start = (f32[24,32,256]{2,1,0:T(8,128)}, f32[24,32,256]{2,1,0:T(8,128)S(1)}, u32[]{:S(2)}) copy-start(f32[24,32,256]{2,1,0:T(8,128)S(1)} %collective-permute-done.zh_ref) | copy-start | bytes 2359300
  41.6 11.5 %collective-permute-start.1 = (f32[24,9,256]{2,1,0:T(8,128)S(1)}, f32[24,9,256]{2,1,0:T(8,128)S(1)}, u32[]{:S(2)}, u32[]{:S(2)}) collective-permute-start(f32[24,9,256]{2,1,0:T(8,128)S(1)} %pad_maximum_fusion), channel_id=1, source_target_pairs={{0,1},{1,2},{2,3},{3,0},{4,5},{5,6},{6,7},{7,4},{8,9},{9,10},{10,1... | collective-permute-start | bytes 663560 | tf_op jit(solution)/shard_map/ppermute | solution.py:366
  53.1 32.8 %copy-start.1 = (f32[24,9,256]{2,1,0:T(8,128)}, f32[24,9,256]{2,1,0:T(8,128)S(1)}, u32[]{:S(2)}) copy-start(f32[24,9,256]{2,1,0:T(8,128)S(1)} %collective-permute-done.1.th_ref) | copy-start | bytes 663556
  68.0 30.9 %collective-permute-start.2 = (f32[9,32,256]{2,1,0:T(8,128)}, f32[9,32,256]{2,1,0:T(8,128)S(1)}, u32[]{:S(2)}, u32[]{:S(2)}) collective-permute-start(f32[9,32,256]{2,1,0:T(8,128)} %get-tuple-element.11), channel_id=1, source_target_pairs={{0,4},{4,8},{8,12},{12,16},{16,20},{20,24},{24,28},{28,32},{32,36}... | collective-permute-start | bytes 884744 | tf_op jit(solution)/shard_map/ppermute | solution.py:358
  71.0 28.0 %collective-permute-start.3 = (f32[9,32,256]{2,1,0:T(8,128)}, f32[9,32,256]{2,1,0:T(8,128)S(1)}, u32[]{:S(2)}, u32[]{:S(2)}) collective-permute-start(f32[9,32,256]{2,1,0:T(8,128)} %get-tuple-element.12), channel_id=1, source_target_pairs={{4,0},{8,4},{12,8},{16,12},{20,16},{24,20},{28,24},{32,28},{36,32}... | collective-permute-start | bytes 884744 | tf_op jit(solution)/shard_map/ppermute | solution.py:362
  73.1 25.8 %collective-permute-start.4 = (f32[9,8,256]{2,1,0:T(8,128)}, f32[9,8,256]{2,1,0:T(8,128)S(1)}, u32[]{:S(2)}, u32[]{:S(2)}) collective-permute-start(f32[9,8,256]{2,1,0:T(8,128)} %get-tuple-element.13), channel_id=1, source_target_pairs={{0,1},{1,2},{2,3},{3,0},{4,5},{5,6},{6,7},{7,4},{8,9},{9,10},{10,1... | collective-permute-start | bytes 221192 | tf_op jit(solution)/shard_map/ppermute | solution.py:366
  73.2 25.7 %collective-permute-start.5 = (f32[9,8,256]{2,1,0:T(8,128)}, f32[9,8,256]{2,1,0:T(8,128)S(1)}, u32[]{:S(2)}, u32[]{:S(2)}) collective-permute-start(f32[9,8,256]{2,1,0:T(8,128)} %get-tuple-element.14), channel_id=1, source_target_pairs={{1,0},{2,1},{3,2},{0,3},{5,4},{6,5},{7,6},{4,7},{9,8},{10,9},{11,1... | collective-permute-start | bytes 221192 | tf_op jit(solution)/shard_map/ppermute | solution.py:370
  75.9 2.8 %collective-permute-start.7 = (f32[8,256]{1,0:T(8,128)S(1)}, f32[8,256]{1,0:T(8,128)S(1)}, u32[]{:S(2)}, u32[]{:S(2)}) collective-permute-start(f32[8,256]{1,0:T(8,128)S(1)} %bitcast.50), channel_id=1, source_target_pairs={{1,0},{2,1},{3,2},{0,3},{5,4},{6,5},{7,6},{4,7},{9,8},{10,9},{11,1... | collective-permute-start | bytes 24584 | tf_op jit(solution)/shard_map/ppermute | solution.py:370
  78.7 20.2 %copy-start.7 = (f32[8,256]{1,0:T(8,128)}, f32[8,256]{1,0:T(8,128)S(1)}, u32[]{:S(2)}) copy-start(f32[8,256]{1,0:T(8,128)S(1)} %collective-permute-done.7.kth_ref) | copy-start | bytes 24580
  78.7 20.2 %collective-permute-start.6 = (f32[32,256]{1,0:T(8,128)S(1)}, f32[32,256]{1,0:T(8,128)S(1)}, u32[]{:S(2)}, u32[]{:S(2)}) collective-permute-start(f32[32,256]{1,0:T(8,128)S(1)} %get-tuple-element.25), channel_id=1, source_target_pairs={{4,0},{8,4},{12,8},{16,12},{20,16},{24,20},{28,24},{32,28},{36,32}... | collective-permute-start | bytes 98312 | tf_op jit(solution)/shard_map/ppermute | solution.py:362
  98.9 0.6 copy-start.6
  98.9 0.6 copy-start.4
  98.9 0.6 copy-start.5
  98.9 0.7 copy-start.2
  99.0 0.8 copy-start.3

commit v2 on v1

--- a/solution.py
+++ b/solution.py
@@ -30,50 +30,13 @@
     return jnp.where(iota((n, n), 0) < iota((n, n), 1), 1.0, 0.0).astype(BF16)
 
 
-def bucket_kernel(loads_ref, dest_ref, cell_ref, out_ref, acc_ref):
-    blk = 256
-    devices = 128
-    earlier = before(blk)
-    carry = jnp.zeros((devices, 1), F32)
-    acc_ref[...] = jnp.zeros_like(acc_ref)
-    for b in range(4096 // blk):
-        sl = pl.ds(b * blk, blk)
-        d = one_hot(dest_ref[:, sl], devices)
-        df = d.astype(F32)
-        count = jnp.dot(d, earlier, preferred_element_type=F32)
-        rank = jnp.sum(df * (count + carry), axis=0, keepdims=True).astype(I32)
-        carry = carry + jnp.sum(df, axis=1, keepdims=True)
-        o = one_hot(rank, 64)
-        hi, lo = split(loads_ref[:, sl])
-        cell = cell_ref[:, sl]
-        row = (lax.shift_right_logical(cell, 8) * 256).astype(F32).astype(BF16)
-        col = ((cell & 255) + 1).astype(F32).astype(BF16)
-        his = [hi[c : c + 1] * o for c in range(9)] + [row * o]
-        los = [lo[c : c + 1] * o for c in range(9)] + [col * o]
-        rhs = jnp.concatenate([jnp.concatenate(his, 0), jnp.concatenate(los, 0)], 1)
-        acc_ref[...] += nt(jnp.concatenate([d, d], 1), rhs)
-    for s in range(5):
-        out_ref[:, s, :] = acc_ref[:, s * 128 : (s + 1) * 128]
-
-
-def bucket(loads, dest, cell):
-    return pl.pallas_call(
-        bucket_kernel,
-        out_shape=jax.ShapeDtypeStruct((128, 5, 128), F32),
-        in_specs=[VM] * 3,
-        out_specs=VM,
-        scratch_shapes=[pltpu.VMEM((128, 640), F32)],
-        name="bucket",
-    )(loads, dest.reshape(1, 4096), cell.reshape(1, 4096))
-
-
 GROUPS, ROWS, SLOTS, CHUNK = 16, 16, 256, 2048
 
 
 def deposit_kernel(
-    recv_ref, fields_ref, vol_ref, sa_ref, st_ref, sr_ref, saz_ref, stt_ref,
+    chan_ref, fields_ref, vol_ref, sa_ref, st_ref, sr_ref, saz_ref, stt_ref,
     vn_ref, src_ref, zlo_ref, zhi_ref, tlo_ref, thi_ref,
-    chan_ref, sort_ref, acc_ref, rank_ref,
+    sort_ref, acc_ref, rank_ref,
 ):
     sa, st, sr = sa_ref[...], st_ref[...], sr_ref[...]
     for a in range(8):
@@ -85,11 +48,6 @@
         lane = iota((32, 256), 1)
         inner = jnp.where(lane == 0, 0.0, pltpu.roll(srp, 1, 1))
         vn_ref[a] = vol_ref[a] + sa_ref[a] - below + stp - side + srp - inner
-    lane = iota((64, 128), 1) < 64
-    for s in range(5):
-        first, second = recv_ref[0:64, s, :], recv_ref[64:128, s, :]
-        chan_ref[2 * s] = jnp.where(lane, first, pltpu.roll(second, 64, 1))
-        chan_ref[2 * s + 1] = jnp.where(lane, pltpu.roll(first, 64, 1), second)
     acc_ref[...] = jnp.zeros_like(acc_ref)
     earlier = before(256)
 
@@ -150,7 +108,7 @@
             thi_ref[f, a : a + 1, :] = v[31:32]
 
 
-def deposit(recv, fields, volume, sa, st, sr, saz, stt):
+def deposit(chan, fields, volume, sa, st, sr, saz, stt):
     sd = jax.ShapeDtypeStruct
     return pl.pallas_call(
         deposit_kernel,
@@ -161,13 +119,12 @@
         in_specs=[VM] * 8,
         out_specs=[VM] * 6,
         scratch_shapes=[
-            pltpu.VMEM((10, 64, 128), F32),
             pltpu.VMEM((320, 256), F32),
             pltpu.VMEM((9, 8, 32, 256), F32),
             pltpu.VMEM((1, CHUNK), I32),
         ],
         name="deposit",
-    )(recv, fields, volume, sa, st, sr, saz, stt)
+    )(chan, fields, volume, sa, st, sr, saz, stt)
 
 
 def t_shift(x, edge):
@@ -316,42 +273,155 @@
     )(src, zlo, zhi, tlo, thi, k, vn, kzl, kzh, ktl, kth)
 
 
-def exchange_kernel(src_ref, out_ref, send_sem, recv_sem, own_sem):
+def exchange_kernel(
+    loads_ref, dest_ref, cell_ref, fz_ref, az_ref, vz_ref, sz_ref, kz_ref, kz0_ref,
+    ft_ref, at_ref, vt_ref, st_ref, kt_ref, kt0_ref,
+    chan_ref, zh_ref, th_ref, kza_ref, kn_ref,
+    acc_ref, d_ref, rank_ref, out_buf, in_buf, azs, ts, cs, kbs, zr, tr, cr, kar, knr,
+    send_sems, recv_sems, psend_sem, precv_sem, own_sem,
+):
     slab, sector = lax.axis_index("slab"), lax.axis_index("sector")
     me = slab * 4 + sector
-    own = pltpu.make_async_copy(src_ref.at[me], out_ref.at[me], own_sem)
+    barrier = pltpu.get_barrier_semaphore()
+
+    def greet(k, unused):
+        to = lax.rem(me + k, 128)
+        pl.semaphore_signal(barrier, inc=1, device_id=(to // 4, lax.rem(to, 4)), device_id_type=pl.DeviceIdType.MESH)
+        return unused
+
+    lax.fori_loop(1, 128, greet, 0)
+
+    for n in range(12):
+        azs[n] = az_ref[n // 4, n % 4, 0].astype(F32)
+    areas_t = [at_ref[i, k, :, 7, :].astype(F32) for i in range(3) for k in (2, 3, 6, 7)]
+    for f in range(9):
+        ts[f] = ft_ref[f, :, 7, :]
+        cs[f : f + 1] = fz_ref[f, 0, 31:32]
+    for n in range(12):
+        ts[9 + n] = areas_t[n]
+        cs[9 + n : 10 + n] = az_ref[n // 4, n % 4, 0].astype(F32)[31:32]
+    for n, (t_ref, z_ref) in enumerate(((vt_ref, vz_ref), (st_ref, sz_ref), (kt_ref, kz_ref))):
+        ts[21 + n] = t_ref[:, 7, :]
+        cs[21 + n : 22 + n] = z_ref[0, 31:32]
+    kbs[...] = kt0_ref[:, 0, :]
+
+    blk, devices = 256, 128
+    earlier = before(blk)
+    carry = jnp.zeros((devices, 1), F32)
+    count = 4096 // blk
+    for b in range(count):
+        d_ref[b * 128 : (b + 1) * 128, :] = one_hot(dest_ref[:, b * blk : (b + 1) * blk], devices)
+    counts = jnp.dot(d_ref[...], earlier, preferred_element_type=F32)
+    for b in range(count):
+        df = d_ref[b * 128 : (b + 1) * 128, :].astype(F32)
+        rank_ref[:, b * blk : (b + 1) * blk] = jnp.sum(
+            df * (counts[b * 128 : (b + 1) * 128] + carry), axis=0, keepdims=True
+        ).astype(I32)
+        carry = carry + jnp.sum(df, axis=1, keepdims=True)
+
+    above = (lax.rem(slab + 1, 32), sector)
+    below = (lax.rem(slab + 31, 32), sector)
+    ahead = (slab, lax.rem(sector + 1, 4))
+    behind = (slab, lax.rem(sector + 3, 4))
+    across = (lax.rem(slab + 1, 32), lax.rem(sector + 1, 4))
+    halo = [
+        (sz_ref.at[0], zr.at[22], above),
+        (kz_ref.at[0], zr.at[23], above),
+        (kz0_ref.at[0], kar, below),
+        (kbs, knr, behind),
+        (ts, tr, ahead),
+        (cs, cr, across),
+        (vz_ref.at[0], zr.at[21], above),
+        (fz_ref.at[:, 0], zr.at[0:9], above),
+        (azs, zr.at[9:21], above),
+    ]
+    copies = [
+        pltpu.make_async_remote_copy(
+            src_ref=s, dst_ref=t, send_sem=send_sems.at[n], recv_sem=recv_sems.at[n],
+            device_id=to, device_id_type=pl.DeviceIdType.MESH,
+        )
+        for n, (s, t, to) in enumerate(halo)
+    ]
+    pl.semaphore_wait(barrier, 127)
+    for copy in copies:
+        copy.start()
+
+    acc_ref[...] = jnp.zeros_like(acc_ref)
+    part = 512
+    for b in range(4096 // part):
+        sl = pl.ds(b * part, part)
+        o = one_hot(rank_ref[:, sl], 64)
+        hi, lo = split(loads_ref[:, sl])
+        cell = cell_ref[:, sl]
+        row = (lax.shift_right_logical(cell, 8) * 256).astype(F32).astype(BF16)
+        col = ((cell & 255) + 1).astype(F32).astype(BF16)
+        his = jnp.concatenate([hi[c : c + 1] * o for c in range(9)] + [row * o], 0)
+        los = jnp.concatenate([lo[c : c + 1] * o for c in range(9)] + [col * o], 0)
+        d = jnp.concatenate([d_ref[(2 * b + i) * 128 : (2 * b + i + 1) * 128, :] for i in range(2)], 1)
+        acc_ref[...] += nt(jnp.concatenate([his, los], 1), jnp.concatenate([d, d], 1))
+    for s in range(5):
+        out_buf[:, s, :] = acc_ref[s * 128 : (s + 1) * 128, :].T
+
+    own = pltpu.make_async_copy(out_buf.at[me], in_buf.at[me], own_sem)
     own.start()
 
     def send(k, unused):
         to = lax.rem(me + k, 128)
         pltpu.make_async_remote_copy(
-            src_ref=src_ref.at[to],
-            dst_ref=out_ref.at[me],
-            send_sem=send_sem,
-            recv_sem=recv_sem,
-            device_id=(to // 4, lax.rem(to, 4)),
-            device_id_type=pl.DeviceIdType.MESH,
+            src_ref=out_buf.at[to], dst_ref=in_buf.at[me], send_sem=psend_sem, recv_sem=precv_sem,
+            device_id=(to // 4, lax.rem(to, 4)), device_id_type=pl.DeviceIdType.MESH,
         ).start()
         return unused
 
     lax.fori_loop(1, 128, send, 0)
     own.wait()
+    for copy in copies:
+        copy.wait()
+    inside = slab > 0
+    zh_ref[...] = jnp.where(inside, zr[...], 0.0)
+    th_ref[:, 0:8, :] = tr[...]
+    th_ref[:, 8, :] = jnp.where(inside, cr[...], 0.0)
+    kza_ref[...] = jnp.where(slab < 31, kar[...], 0.0)
+    kn_ref[...] = knr[...]
     most = pl.ds(0, 127)
-    pltpu.make_async_copy(src_ref.at[most], out_ref.at[most], send_sem).wait()
-    pltpu.make_async_copy(src_ref.at[most], out_ref.at[most], recv_sem).wait()
-
-
-def exchange(outgoing):
-    hbm = pl.BlockSpec(memory_space=pl.ANY)
+    pltpu.make_async_copy(out_buf.at[most], in_buf.at[most], psend_sem).wait()
+    pltpu.make_async_copy(out_buf.at[most], in_buf.at[most], precv_sem).wait()
+    lane = iota((64, 128), 1) < 64
+    for s in range(5):
+        first, second = in_buf[0:64, s, :], in_buf[64:128, s, :]
+        chan_ref[2 * s] = jnp.where(lane, first, pltpu.roll(second, 64, 1))
+        chan_ref[2 * s + 1] = jnp.where(lane, pltpu.roll(first, 64, 1), second)
+
+
+def exchange(loads, dest, cell, fields, areas, volume, sa, st, k):
+    at = lambda shape, *index: pl.BlockSpec(shape, lambda i: index)
+    whole = lambda *shape: at(shape, *(0,) * len(shape))
+    shapes = [(10, 64, 128), (24, 32, 256), (24, 9, 256), (32, 256), (8, 256)]
+    dma = pltpu.SemaphoreType.DMA
+    vm = lambda *shape, t=F32: pltpu.VMEM(shape, t)
+    plane, column = (1, 32, 256), (8, 8, 256)
     return pl.pallas_call(
         exchange_kernel,
-        out_shape=jax.ShapeDtypeStruct((128, 5, 128), F32),
-        in_specs=[hbm],
-        out_specs=hbm,
-        scratch_shapes=[pltpu.SemaphoreType.DMA, pltpu.SemaphoreType.DMA, pltpu.SemaphoreType.DMA],
-        compiler_params=pltpu.CompilerParams(has_side_effects=True),
+        grid=(1,),
+        out_shape=[jax.ShapeDtypeStruct(s, F32) for s in shapes],
+        in_specs=[
+            whole(9, 4096), whole(1, 4096), whole(1, 4096),
+            at((9, 1, 32, 256), 0, 7, 0, 0), at((3, 4, 1, 32, 256), 0, 1, 7, 0, 0),
+            at(plane, 7, 0, 0), at(plane, 7, 0, 0), at(plane, 7, 0, 0), at(plane, 0, 0, 0),
+            at((9, 8, 8, 256), 0, 0, 3, 0), at((3, 8, 8, 8, 256), 0, 0, 0, 3, 0),
+            at(column, 0, 3, 0), at(column, 0, 3, 0), at(column, 0, 3, 0), at(column, 0, 0, 0),
+        ],
+        out_specs=[whole(*s) for s in shapes],
+        scratch_shapes=[
+            vm(640, 128), vm(2048, 256, t=BF16), vm(1, 4096, t=I32), vm(128, 5, 128), vm(128, 5, 128),
+            vm(12, 32, 256), vm(24, 8, 256), vm(24, 256), vm(8, 256),
+            vm(24, 32, 256), vm(24, 8, 256), vm(24, 256), vm(32, 256), vm(8, 256),
+            dma((9,)), dma((9,)), dma, dma, dma,
+        ],
+        compiler_params=pltpu.CompilerParams(has_side_effects=True, collective_id=0),
         name="exchange",
-    )(outgoing)
+    )(loads, dest.reshape(1, 4096), cell.reshape(1, 4096), fields, areas, volume, sa, k, k,
+      fields, areas, volume, st, k, k)
 
 
 def up(x):
@@ -371,20 +441,11 @@
 
 
 def local(fields, volume, swept_axial, swept_angular, swept_radial, conductivity, corner_areas, parcel_loads, dest_device, dest_cell):
-    zh = up(jnp.concatenate(
-        [fields[:, 7], corner_areas[:, 4:8, 7].astype(F32).reshape(12, 32, 256), volume[7:8], swept_axial[7:8], conductivity[7:8]], 0
-    ))
-    k_above = down(conductivity[0])
-    k_next = backward(conductivity[:, 0])
-    own = jnp.concatenate(
-        [fields[:, :, 31], jnp.stack([corner_areas[:, k, :, 31] for k in (2, 3, 6, 7)], 1).astype(F32).reshape(12, 8, 256),
-         volume[:, 31][None], swept_angular[:, 31][None], conductivity[:, 31][None]], 0
+    chan, zh, th, k_above, k_next = exchange(
+        parcel_loads, dest_device, dest_cell, fields, corner_areas, volume, swept_axial, swept_angular, conductivity
     )
-    th = onward(jnp.concatenate([own, zh[:, 31:32]], 1))
-    outgoing = bucket(parcel_loads, dest_device, dest_cell)
-    recv = exchange(outgoing)
     vn, src, zlo, zhi, tlo, thi = deposit(
-        recv, fields, volume, swept_axial, swept_angular, swept_radial, zh[22], th[22, :8]
+        chan, fields, volume, swept_axial, swept_angular, swept_radial, zh[22], th[22, :8]
     )
     below, above = up(zhi), down(zlo)
     before_, after = onward(thi), backward(tlo)

time: 109 us -> 79.7 us (0.73)
  the two profiles are of different devices: /device:TPU:33 before, /device:TPU:32 now
where the time goes in v2:
time: 79.7 us; the launch traced here: 79 us
  Pallas kernels  63.8 us (80%)
  starting transfers between devices  11 us (14%)
  local copies, waits for them, and re-layouts  3.56 us (4%)
    pallas_call x1, Pallas kernels, exchange(): pl.pallas_call(exchange_kernel, grid=(1,), out_shape=[jax.ShapeDtypeStruc...  28.9 us
    pallas_call x1, Pallas kernels, deposit(): pl.pallas_call(deposit_kernel, out_shape=(sd((8, 32, 256), F32), sd((9, 8...  14 us
    pallas_call x1, Pallas kernels, gradients(): pl.pallas_call(gradient_kernel, grid=(8,), out_shape=jax.ShapeDtypeStruct...  13 us
    pallas_call x1, Pallas kernels, diffuse(): pl.pallas_call(diffuse_kernel, grid=(9,), out_shape=jax.ShapeDtypeStruct(...  7.96 us
    ppermute x1, starting transfers between devices, down(): return lax.ppermute(x, 'slab', [(i + 1, i) for i in range(31)])  5.66 us
    ppermute x1, starting transfers between devices, backward(): return lax.ppermute(x, 'sector', [((i + 1) % 4, i) for i in range(4)])  2.45 us
    ppermute x1, starting transfers between devices, up(): return lax.ppermute(x, 'slab', [(i, i + 1) for i in range(31)])  2 us
  transfers between devices with their start and end apart: 4, of which 0 were waited for; matrix products, arithmetic and copies ran while one was open for 0% of the time, Pallas kernels for 16%

profile of v2, /device:TPU:32, one launch (start us, length us, event | category | flops | bytes accessed | tf_op | source)
XLA Modules:
  0.0 79.0 jit_solution(17334777659223417661)
XLA Ops:
  0.6 28.9 %exchange.1 = (f32[10,64,128]{2,1,0:T(8,128)}, f32[24,32,256]{2,1,0:T(8,128)}, f32[24,9,256]{2,1,0:T(8,128)}, f32[32,256]{1,0:T(8,128)}, f32[8,256]{1,0:T(8,128)}) custom-call(f32[9,4096]{1,0:T(8,128)} %loads_ref.1, s32[1,4096]{1,0:T(1,128)} %bitcast.10, s32[1,4096]{1,0:T(1,128)} %bitcast.11, f32[9,8,32,256]{3,2,1,0:T(8,128)} %fields_ref.3, ...), custom_call_target="tpu_custom_call" | custom-call | tf_op jit(solution)/shard_map/exchange/pallas_call | solution.py:403
  29.5 1.3 %slice_bitcast_fusion.2 = (f32[8,256]{1,0:T(8,128)}, f32[8,256]{1,0:T(8,128)}) fusion(f32[24,9,256]{2,1,0:T(8,128)} %get-tuple-element.16.th_ref), kind=kLoop, calls=%fused_computation.2 | loop fusion | bytes 32768 | tf_op jit(solution)/shard_map/squeeze | solution.py:453
  30.9 1.4 %slice_bitcast_fusion = (f32[32,256]{1,0:T(8,128)}, f32[32,256]{1,0:T(8,128)}) fusion(f32[24,32,256]{2,1,0:T(8,128)} %get-tuple-element.15.zh_ref), kind=kLoop, calls=%fused_computation | loop fusion | bytes 131072 | tf_op jit(solution)/shard_map/squeeze | solution.py:453
  32.3 14.0 %deposit.1 = (f32[8,32,256]{2,1,0:T(8,128)}, f32[9,8,32,256]{3,2,1,0:T(8,128)}, f32[9,32,256]{2,1,0:T(8,128)}, f32[9,32,256]{2,1,0:T(8,128)}, f32[9,8,256]{2,1,0:T(8,128)}, /*index=5*/f32[9,8,256]{2,1,0:T(8,128)}) custom-call(f32[10,64,128]{2,1,0:T(8,128)} %get-tuple-element.14.chan_ref, f32[9,8,32,256]{3,2,1,0:T(8,128)} %fields_ref.3, ...), custom_call_target="tpu_custom_call" | custom-call | tf_op jit(solution)/shard_map/deposit/pallas_call | solution.py:113
  46.2 2.0 %collective-permute-start = (f32[9,32,256]{2,1,0:T(8,128)}, f32[9,32,256]{2,1,0:T(8,128)S(1)}, u32[]{:S(2)}, u32[]{:S(2)}) collective-permute-start(f32[9,32,256]{2,1,0:T(8,128)} %get-tuple-element.19), channel_id=1, source_target_pairs={{0,4},{4,8},{8,12},{12,16},{16,20},{20,24},{24,28},{28,32},{32,36}... | collective-permute-start | bytes 884744 | tf_op jit(solution)/shard_map/ppermute | solution.py:428
  48.2 5.7 %collective-permute-start.1 = (f32[9,32,256]{2,1,0:T(8,128)}, f32[9,32,256]{2,1,0:T(8,128)S(1)}, u32[]{:S(2)}, u32[]{:S(2)}) collective-permute-start(f32[9,32,256]{2,1,0:T(8,128)} %get-tuple-element.20), channel_id=1, source_target_pairs={{4,0},{8,4},{12,8},{16,12},{20,16},{24,20},{28,24},{32,28},{36,32}... | collective-permute-start | bytes 884744 | tf_op jit(solution)/shard_map/ppermute | solution.py:432
  53.9 0.9 %collective-permute-start.2 = (f32[9,8,256]{2,1,0:T(8,128)}, f32[9,8,256]{2,1,0:T(8,128)S(1)}, u32[]{:S(2)}, u32[]{:S(2)}) collective-permute-start(f32[9,8,256]{2,1,0:T(8,128)} %get-tuple-element.21), channel_id=1, source_target_pairs={{0,1},{1,2},{2,3},{3,0},{4,5},{5,6},{6,7},{7,4},{8,9},{9,10},{10,1... | collective-permute-start | bytes 221192 | tf_op jit(solution)/shard_map/ppermute | solution.py:436
  54.8 2.5 %collective-permute-start.3 = (f32[9,8,256]{2,1,0:T(8,128)}, f32[9,8,256]{2,1,0:T(8,128)S(1)}, u32[]{:S(2)}, u32[]{:S(2)}) collective-permute-start(f32[9,8,256]{2,1,0:T(8,128)} %get-tuple-element.22), channel_id=1, source_target_pairs={{1,0},{2,1},{3,2},{0,3},{5,4},{6,5},{7,6},{4,7},{9,8},{10,9},{11,1... | collective-permute-start | bytes 221192 | tf_op jit(solution)/shard_map/ppermute | solution.py:440
  57.2 13.0 %gradients.1 = f32[27,8,32,256]{3,2,1,0:T(8,128)} custom-call(f32[9,8,32,256]{3,2,1,0:T(8,128)} %fields_ref.3, bf16[3,8,8,32,256]{4,3,2,1,0:T(8,128)(2,1)} %areas_ref.1, f32[8,32,256]{2,1,0:T(8,128)} %vol_ref.3, f32[24,32,256]{2,1,0:T(8,128)} %get-tuple-element.15.zh_ref, f32[24,9,256]{2,1,0:T(8,128)} %get-tuple-element.16.th_ref), custom_call_target="tpu_custom_call" | custom-call | flops 30000000 | bytes 14000000 | tf_op jit(solution)/shard_map/gradients/pallas_call | solution.py:196
  70.2 0.0 collective-permute-done.2.tlo_ref
  70.2 0.0 copy-start.2
  70.2 0.0 collective-permute-done.3.thi_ref
  70.2 0.0 copy-start.3
  70.2 0.0 collective-permute-done.zlo_ref
  70.2 0.0 copy-start
  70.2 0.0 collective-permute-done.1.zhi_ref
  70.2 0.0 copy-start.1
  70.2 0.6 copy-done.2
  70.8 0.0 copy-done.3
  70.8 0.1 copy-done
  70.9 0.1 copy-done.1
  71.1 8.0 %diffuse.1 = f32[9,8,32,256]{3,2,1,0:T(8,128)} custom-call(f32[9,8,32,256]{3,2,1,0:T(8,128)} %get-tuple-element.18.src_ref, f32[9,32,256]{2,1,0:T(8,128)} %copy-done, f32[9,32,256]{2,1,0:T(8,128)} %copy-done.1, f32[9,8,256]{2,1,0:T(8,128)} %copy-done.2, f32[9,8,256]{2,1,0:T(8,128)} %copy-done.3, f32[8,32,256]{2,1,0:T(8,128)} %k_ref.1, ...), custom_call_target="tpu_custom_call" | custom-call | tf_op jit(solution)/shard_map/diffuse/pallas_call | solution.py:262
Async XLA Ops:
  46.2 24.0 %collective-permute-start = (f32[9,32,256]{2,1,0:T(8,128)}, f32[9,32,256]{2,1,0:T(8,128)S(1)}, u32[]{:S(2)}, u32[]{:S(2)}) collective-permute-start(f32[9,32,256]{2,1,0:T(8,128)} %get-tuple-element.19), channel_id=1, source_target_pairs={{0,4},{4,8},{8,12},{12,16},{16,20},{20,24},{24,28},{28,32},{32,36}... | collective-permute-start | bytes 884744 | tf_op jit(solution)/shard_map/ppermute | solution.py:428
  48.2 22.0 %collective-permute-start.1 = (f32[9,32,256]{2,1,0:T(8,128)}, f32[9,32,256]{2,1,0:T(8,128)S(1)}, u32[]{:S(2)}, u32[]{:S(2)}) collective-permute-start(f32[9,32,256]{2,1,0:T(8,128)} %get-tuple-element.20), channel_id=1, source_target_pairs={{4,0},{8,4},{12,8},{16,12},{20,16},{24,20},{28,24},{32,28},{36,32}... | collective-permute-start | bytes 884744 | tf_op jit(solution)/shard_map/ppermute | solution.py:432
  53.9 16.3 %collective-permute-start.2 = (f32[9,8,256]{2,1,0:T(8,128)}, f32[9,8,256]{2,1,0:T(8,128)S(1)}, u32[]{:S(2)}, u32[]{:S(2)}) collective-permute-start(f32[9,8,256]{2,1,0:T(8,128)} %get-tuple-element.21), channel_id=1, source_target_pairs={{0,1},{1,2},{2,3},{3,0},{4,5},{5,6},{6,7},{7,4},{8,9},{9,10},{10,1... | collective-permute-start | bytes 221192 | tf_op jit(solution)/shard_map/ppermute | solution.py:436
  54.8 15.4 %collective-permute-start.3 = (f32[9,8,256]{2,1,0:T(8,128)}, f32[9,8,256]{2,1,0:T(8,128)S(1)}, u32[]{:S(2)}, u32[]{:S(2)}) collective-permute-start(f32[9,8,256]{2,1,0:T(8,128)} %get-tuple-element.22), channel_id=1, source_target_pairs={{1,0},{2,1},{3,2},{0,3},{5,4},{6,5},{7,6},{4,7},{9,8},{10,9},{11,1... | collective-permute-start | bytes 221192 | tf_op jit(solution)/shard_map/ppermute | solution.py:440
  70.2 0.6 copy-start.2
  70.2 0.7 copy-start.3
  70.2 0.7 copy-start
  70.2 0.8 %copy-start.1 = (f32[9,32,256]{2,1,0:T(8,128)}, f32[9,32,256]{2,1,0:T(8,128)S(1)}, u32[]{:S(2)}) copy-start(f32[9,32,256]{2,1,0:T(8,128)S(1)} %collective-permute-done.1.zhi_ref) | copy-start | bytes 884740

commit v3 on v2

--- a/solution.py
+++ b/solution.py
@@ -34,10 +34,13 @@
 
 
 def deposit_kernel(
-    chan_ref, fields_ref, vol_ref, sa_ref, st_ref, sr_ref, saz_ref, stt_ref,
-    vn_ref, src_ref, zlo_ref, zhi_ref, tlo_ref, thi_ref,
-    sort_ref, acc_ref, rank_ref,
+    chan_ref, fields_ref, vol_ref, sa_ref, st_ref, sr_ref, saz_ref, stt_ref, grads_ref,
+    vn_ref, src_ref, zlo_ref, zhi_ref, tlo_ref, thi_ref, grads_out_ref,
+    sort_ref, acc_ref, rank_ref, gbuf, sems,
 ):
+    arriving = pltpu.make_async_copy(grads_ref, gbuf, sems.at[0])
+    leaving = pltpu.make_async_copy(gbuf, grads_out_ref, sems.at[1])
+    arriving.start()
     sa, st, sr = sa_ref[...], st_ref[...], sr_ref[...]
     for a in range(8):
         below = saz_ref[...] if a == 0 else sa_ref[a - 1]
@@ -68,6 +71,9 @@
             count = jnp.dot(g[:, b * 256 : (b + 1) * 256], earlier, preferred_element_type=F32)
             ranks.append(jnp.sum(gb * (count + carry) , axis=0, keepdims=True))
             carry = carry + jnp.sum(gb, axis=1, keepdims=True)
+        if ch == 1:
+            arriving.wait()
+            leaving.start()
         rank_ref[...] = jnp.concatenate(ranks, 1).astype(I32)
         most = jnp.max(carry).astype(I32)
         his, los = [], []
@@ -95,6 +101,7 @@
             return carry_unused
 
         lax.fori_loop(0, (most + SLOTS - 1) // SLOTS, one_round, 0)
+    leaving.wait()
     for a in range(8):
         inv = 1.0 / vn_ref[a]
         for f in range(9):
@@ -108,23 +115,26 @@
             thi_ref[f, a : a + 1, :] = v[31:32]
 
 
-def deposit(chan, fields, volume, sa, st, sr, saz, stt):
+def deposit(chan, fields, volume, sa, st, sr, saz, stt, grads):
     sd = jax.ShapeDtypeStruct
     return pl.pallas_call(
         deposit_kernel,
         out_shape=(
             sd((8, 32, 256), F32), sd((9, 8, 32, 256), F32),
             sd((9, 32, 256), F32), sd((9, 32, 256), F32), sd((9, 8, 256), F32), sd((9, 8, 256), F32),
+            sd((27, 8, 32, 256), F32),
         ),
-        in_specs=[VM] * 8,
-        out_specs=[VM] * 6,
+        in_specs=[VM] * 8 + [pl.BlockSpec(memory_space=pl.ANY)],
+        out_specs=[VM] * 6 + [pl.BlockSpec(memory_space=pl.ANY)],
         scratch_shapes=[
             pltpu.VMEM((320, 256), F32),
             pltpu.VMEM((9, 8, 32, 256), F32),
             pltpu.VMEM((1, CHUNK), I32),
+            pltpu.VMEM((27, 8, 32, 256), F32),
+            pltpu.SemaphoreType.DMA((2,)),
         ],
         name="deposit",
-    )(chan, fields, volume, sa, st, sr, saz, stt)
+    )(chan, fields, volume, sa, st, sr, saz, stt, grads)
 
 
 def t_shift(x, edge):
@@ -136,84 +146,43 @@
     return jnp.where(iota(x.shape, 1) == n - 1, 0.0, pltpu.roll(x, n - 1, 1))
 
 
-def gradient_kernel(fields_ref, areas_ref, vol_ref, zh_ref, th_ref, out_ref, fv_ref, a1_ref, a0_ref, w_ref):
-    a = pl.program_id(0)
-    now = lax.rem(a, 2)
-    prev = 1 - now
-
-    def prepare(slot, field, area1, vol, edge):
-        for f in range(9):
-            x = field(f)
-            xt = t_shift(x, edge(f))
-            fv_ref[slot, 0, f] = r_shift(x)
-            fv_ref[slot, 1, f] = x
-            fv_ref[slot, 2, f] = r_shift(xt)
-            fv_ref[slot, 3, f] = xt
-        for i in range(3):
-            for q in range(4):
-                x = area1(i, q)
-                if q // 2 == 1:
-                    x = t_shift(x, edge(9 + 4 * i + 2 + q % 2))
-                a1_ref[slot, i, q] = x if q % 2 == 1 else pltpu.roll(x, 255, 1)
-        v = vol * 0.125
-        v = v + t_shift(v, edge(21) * 0.125)
-        w_ref[slot] = v + r_shift(v)
-
-    @pl.when(a == 0)
-    def _():
-        prepare(1, lambda f: zh_ref[f], lambda i, q: zh_ref[9 + 4 * i + q], zh_ref[21],
-                lambda c: th_ref[c, 8:9, :])
-
-    here = lambda c: th_ref[c, pl.ds(a, 1), :]
-    prepare(now, lambda f: fields_ref[f, 0], lambda i, q: areas_ref[i, 4 + q, 0].astype(F32), vol_ref[0], here)
+def prepare(f_ref, w_ref, slot, field, vol, edge):
+    for f in range(9):
+        x = field(f)
+        xt = t_shift(x, edge(f))
+        f_ref[slot, 0, f] = r_shift(x)
+        f_ref[slot, 1, f] = x
+        f_ref[slot, 2, f] = r_shift(xt)
+        f_ref[slot, 3, f] = xt
+    v = vol * 0.125
+    v = v + t_shift(v, edge(21) * 0.125)
+    w_ref[slot] = v + r_shift(v)
+
+
+def prepare_areas(a_ref, area, edge):
     for i in range(3):
         for q in range(4):
-            x = areas_ref[i, q, 0].astype(F32)
+            x = area(i, q)
             if q // 2 == 1:
-                x = t_shift(x, here(9 + 4 * i + q % 2))
-            a0_ref[i, q] = x if q % 2 == 1 else pltpu.roll(x, 255, 1)
+                x = t_shift(x, edge(i, q))
+            a_ref[i, q] = x if q % 2 == 1 else pltpu.roll(x, 255, 1)
+
+
+def gradient_plane(f_ref, w_ref, a0_ref, a1_ref, now, prev, out_ref, a):
     for t in range(4):
         for h in range(2):
             at = (pl.ds(8 * t, 8), pl.ds(128 * h, 128))
-            acc = [[None] * 9 for _ in range(3)]
-            for dz in range(2):
-                slot = prev if dz else now
-                for q in range(4):
-                    area = [(a1_ref[(slot, i, q) + at] if dz else a0_ref[(i, q) + at]) for i in range(3)]
-                    for f in range(9):
-                        x = fv_ref[(slot, q, f) + at]
-                        for i in range(3):
-                            term = area[i] * x
-                            acc[i][f] = term if acc[i][f] is None else acc[i][f] + term
             inv = 1.0 / (w_ref[(now,) + at] + w_ref[(prev,) + at])
             for i in range(3):
+                acc = [None] * 9
+                for dz in range(2):
+                    for q in range(4):
+                        area = (a1_ref if dz else a0_ref)[(i, q) + at]
+                        for f in range(9):
+                            term = area * f_ref[(prev if dz else now, q, f) + at]
+                            acc[f] = term if dz + q == 0 else acc[f] + term
                 for f in range(9):
-                    out_ref[(9 * i + f, 0) + at] = acc[i][f] * inv
-
-
-def gradients(fields, areas, volume, zh, th):
-    whole = lambda shape: pl.BlockSpec(shape, lambda a: (0,) * len(shape))
-    return pl.pallas_call(
-        gradient_kernel,
-        grid=(8,),
-        out_shape=jax.ShapeDtypeStruct((27, 8, 32, 256), F32),
-        in_specs=[
-            pl.BlockSpec((9, 1, 32, 256), lambda a: (0, a, 0, 0)),
-            pl.BlockSpec((3, 8, 1, 32, 256), lambda a: (0, 0, a, 0, 0)),
-            pl.BlockSpec((1, 32, 256), lambda a: (a, 0, 0)),
-            whole((24, 32, 256)),
-            whole((24, 9, 256)),
-        ],
-        out_specs=pl.BlockSpec((27, 1, 32, 256), lambda a: (0, a, 0, 0)),
-        scratch_shapes=[
-            pltpu.VMEM((2, 4, 9, 32, 256), F32),
-            pltpu.VMEM((2, 3, 4, 32, 256), F32),
-            pltpu.VMEM((3, 4, 32, 256), F32),
-            pltpu.VMEM((2, 32, 256), F32),
-        ],
-        cost_estimate=pl.CostEstimate(flops=30_000_000, bytes_accessed=14_000_000, transcendentals=0),
-        name="gradients",
-    )(fields, areas, volume, zh, th)
+                    out_ref[(9 * i + f, a) + at] = acc[f] * inv
 
 
 def diffuse_kernel(src_ref, zlo_ref, zhi_ref, tlo_ref, thi_ref, k_ref, vn_ref, kzl_ref, kzh_ref, ktl_ref, kth_ref, out_ref, w_ref):
@@ -274,15 +243,22 @@
 
 
 def exchange_kernel(
-    loads_ref, dest_ref, cell_ref, fz_ref, az_ref, vz_ref, sz_ref, kz_ref, kz0_ref,
-    ft_ref, at_ref, vt_ref, st_ref, kt_ref, kt0_ref,
-    chan_ref, zh_ref, th_ref, kza_ref, kn_ref,
+    loads_ref, dest_ref, cell_ref, sz_ref, kz_ref, kz0_ref, st_ref, kt_ref, kt0_ref,
+    fields_ref, areas_ref, vol_ref,
+    chan_ref, saz_ref, stt_ref, kzl_ref, kzh_ref, ktl_ref, kth_ref, grads_ref,
     acc_ref, d_ref, rank_ref, out_buf, in_buf, azs, ts, cs, kbs, zr, tr, cr, kar, knr,
-    send_sems, recv_sems, psend_sem, precv_sem, own_sem,
+    fbuf, abuf, vbuf, gbuf, f_ref, w_ref, a0_ref, a1_ref,
+    send_sems, recv_sems, psend_sem, precv_sem, own_sem, load_sems, store_sems,
 ):
     slab, sector = lax.axis_index("slab"), lax.axis_index("sector")
     me = slab * 4 + sector
     barrier = pltpu.get_barrier_semaphore()
+    loading = [
+        pltpu.make_async_copy(s, t, load_sems.at[n])
+        for n, (s, t) in enumerate(((fields_ref, fbuf), (areas_ref, abuf), (vol_ref, vbuf)))
+    ]
+    for copy in loading:
+        copy.start()
 
     def greet(k, unused):
         to = lax.rem(me + k, 128)
@@ -290,20 +266,6 @@
         return unused
 
     lax.fori_loop(1, 128, greet, 0)
-
-    for n in range(12):
-        azs[n] = az_ref[n // 4, n % 4, 0].astype(F32)
-    areas_t = [at_ref[i, k, :, 7, :].astype(F32) for i in range(3) for k in (2, 3, 6, 7)]
-    for f in range(9):
-        ts[f] = ft_ref[f, :, 7, :]
-        cs[f : f + 1] = fz_ref[f, 0, 31:32]
-    for n in range(12):
-        ts[9 + n] = areas_t[n]
-        cs[9 + n : 10 + n] = az_ref[n // 4, n % 4, 0].astype(F32)[31:32]
-    for n, (t_ref, z_ref) in enumerate(((vt_ref, vz_ref), (st_ref, sz_ref), (kt_ref, kz_ref))):
-        ts[21 + n] = t_ref[:, 7, :]
-        cs[21 + n : 22 + n] = z_ref[0, 31:32]
-    kbs[...] = kt0_ref[:, 0, :]
 
     blk, devices = 256, 128
     earlier = before(blk)
@@ -319,6 +281,24 @@
         ).astype(I32)
         carry = carry + jnp.sum(df, axis=1, keepdims=True)
 
+    for copy in loading:
+        copy.wait()
+    for n in range(12):
+        x = abuf[n // 4, 4 + n % 4, 7].astype(F32)
+        azs[n] = x
+        cs[9 + n : 10 + n] = x[31:32]
+        for a in range(8):
+            ts[9 + n, a : a + 1, :] = abuf[n // 4, (2, 3, 6, 7)[n % 4], a].astype(F32)[31:32]
+    for f in range(9):
+        ts[f] = fbuf[f, :, 31, :]
+        cs[f : f + 1] = fbuf[f, 7, 31:32]
+    ts[21] = vbuf[:, 31, :]
+    cs[21:22] = vbuf[7, 31:32]
+    for n, (t_ref, z_ref) in enumerate(((st_ref, sz_ref), (kt_ref, kz_ref))):
+        ts[22 + n] = t_ref[:, 7, :]
+        cs[22 + n : 23 + n] = z_ref[0, 31:32]
+    kbs[...] = kt0_ref[:, 0, :]
+
     above = (lax.rem(slab + 1, 32), sector)
     below = (lax.rem(slab + 31, 32), sector)
     ahead = (slab, lax.rem(sector + 1, 4))
@@ -331,8 +311,8 @@
         (kbs, knr, behind),
         (ts, tr, ahead),
         (cs, cr, across),
-        (vz_ref.at[0], zr.at[21], above),
-        (fz_ref.at[:, 0], zr.at[0:9], above),
+        (vbuf.at[7], zr.at[21], above),
+        (fbuf.at[:, 7], zr.at[0:9], above),
         (azs, zr.at[9:21], above),
     ]
     copies = [
@@ -374,15 +354,56 @@
         return unused
 
     lax.fori_loop(1, 128, send, 0)
+    copies[4].wait()
+
+    def beside(plane):
+        return lambda c: tr[c, pl.ds(plane, 1), :]
+
+    def prepare_own(slot, plane):
+        prepare(f_ref, w_ref, slot, lambda f: fbuf[f, plane], vbuf[plane], beside(plane))
+
+    def own_areas(ref, plane, dz):
+        prepare_areas(
+            ref, lambda i, q: abuf[i, 4 * dz + q, plane].astype(F32),
+            lambda i, q: beside(plane)(9 + 4 * i + 2 * dz + q % 2),
+        )
+
+    def store(a):
+        return pltpu.make_async_copy(gbuf.at[:, a], grads_ref.at[:, a], store_sems.at[a])
+
+    prepare_own(1, 7)
+
+    def plane(n, unused):
+        a = 7 - n
+        now = lax.rem(a, 2)
+        prepare_own(1 - now, a - 1)
+        own_areas(a0_ref, a, 0)
+        own_areas(a1_ref, a - 1, 1)
+        gradient_plane(f_ref, w_ref, a0_ref, a1_ref, now, 1 - now, gbuf, a)
+        store(a).start()
+        return unused
+
+    lax.fori_loop(0, 7, plane, 0)
     own.wait()
-    for copy in copies:
-        copy.wait()
+    for n, copy in enumerate(copies):
+        if n != 4:
+            copy.wait()
     inside = slab > 0
-    zh_ref[...] = jnp.where(inside, zr[...], 0.0)
-    th_ref[:, 0:8, :] = tr[...]
-    th_ref[:, 8, :] = jnp.where(inside, cr[...], 0.0)
-    kza_ref[...] = jnp.where(slab < 31, kar[...], 0.0)
-    kn_ref[...] = knr[...]
+
+    def under(x):
+        return jnp.where(inside, x, 0.0)
+
+    prepare(f_ref, w_ref, 1, lambda f: under(zr[f]), under(zr[21]), lambda c: under(cr[c : c + 1, :]))
+    own_areas(a0_ref, 0, 0)
+    prepare_areas(a1_ref, lambda i, q: zr[9 + 4 * i + q], lambda i, q: cr[9 + 4 * i + q : 10 + 4 * i + q, :])
+    gradient_plane(f_ref, w_ref, a0_ref, a1_ref, 0, 1, gbuf, 0)
+    store(0).start()
+    saz_ref[...] = under(zr[22])
+    kzl_ref[...] = under(zr[23])
+    kzh_ref[...] = jnp.where(slab < 31, kar[...], 0.0)
+    stt_ref[...] = tr[22]
+    ktl_ref[...] = tr[23]
+    kth_ref[...] = knr[...]
     most = pl.ds(0, 127)
     pltpu.make_async_copy(out_buf.at[most], in_buf.at[most], psend_sem).wait()
     pltpu.make_async_copy(out_buf.at[most], in_buf.at[most], precv_sem).wait()
@@ -391,37 +412,40 @@
         first, second = in_buf[0:64, s, :], in_buf[64:128, s, :]
         chan_ref[2 * s] = jnp.where(lane, first, pltpu.roll(second, 64, 1))
         chan_ref[2 * s + 1] = jnp.where(lane, pltpu.roll(first, 64, 1), second)
+    for a in range(8):
+        store(a).wait()
 
 
 def exchange(loads, dest, cell, fields, areas, volume, sa, st, k):
     at = lambda shape, *index: pl.BlockSpec(shape, lambda i: index)
     whole = lambda *shape: at(shape, *(0,) * len(shape))
-    shapes = [(10, 64, 128), (24, 32, 256), (24, 9, 256), (32, 256), (8, 256)]
+    any_ = pl.BlockSpec(memory_space=pl.ANY)
+    shapes = [(10, 64, 128), (32, 256), (8, 256), (32, 256), (32, 256), (8, 256), (8, 256)]
     dma = pltpu.SemaphoreType.DMA
     vm = lambda *shape, t=F32: pltpu.VMEM(shape, t)
     plane, column = (1, 32, 256), (8, 8, 256)
     return pl.pallas_call(
         exchange_kernel,
         grid=(1,),
-        out_shape=[jax.ShapeDtypeStruct(s, F32) for s in shapes],
+        out_shape=[jax.ShapeDtypeStruct(s, F32) for s in shapes + [(27, 8, 32, 256)]],
         in_specs=[
             whole(9, 4096), whole(1, 4096), whole(1, 4096),
-            at((9, 1, 32, 256), 0, 7, 0, 0), at((3, 4, 1, 32, 256), 0, 1, 7, 0, 0),
-            at(plane, 7, 0, 0), at(plane, 7, 0, 0), at(plane, 7, 0, 0), at(plane, 0, 0, 0),
-            at((9, 8, 8, 256), 0, 0, 3, 0), at((3, 8, 8, 8, 256), 0, 0, 0, 3, 0),
-            at(column, 0, 3, 0), at(column, 0, 3, 0), at(column, 0, 3, 0), at(column, 0, 0, 0),
+            at(plane, 7, 0, 0), at(plane, 7, 0, 0), at(plane, 0, 0, 0),
+            at(column, 0, 3, 0), at(column, 0, 3, 0), at(column, 0, 0, 0),
+            any_, any_, any_,
         ],
-        out_specs=[whole(*s) for s in shapes],
+        out_specs=[whole(*s) for s in shapes] + [any_],
         scratch_shapes=[
             vm(640, 128), vm(2048, 256, t=BF16), vm(1, 4096, t=I32), vm(128, 5, 128), vm(128, 5, 128),
             vm(12, 32, 256), vm(24, 8, 256), vm(24, 256), vm(8, 256),
             vm(24, 32, 256), vm(24, 8, 256), vm(24, 256), vm(32, 256), vm(8, 256),
-            dma((9,)), dma((9,)), dma, dma, dma,
+            vm(9, 8, 32, 256), vm(3, 8, 8, 32, 256, t=BF16), vm(8, 32, 256), vm(27, 8, 32, 256),
+            vm(2, 4, 9, 32, 256), vm(2, 32, 256), vm(3, 4, 32, 256), vm(3, 4, 32, 256),
+            dma((9,)), dma((9,)), dma, dma, dma, dma((3,)), dma((8,)),
         ],
         compiler_params=pltpu.CompilerParams(has_side_effects=True, collective_id=0),
         name="exchange",
-    )(loads, dest.reshape(1, 4096), cell.reshape(1, 4096), fields, areas, volume, sa, k, k,
-      fields, areas, volume, st, k, k)
+    )(loads, dest.reshape(1, 4096), cell.reshape(1, 4096), sa, k, k, st, k, k, fields, areas, volume)
 
 
 def up(x):
@@ -441,16 +465,15 @@
 
 
 def local(fields, volume, swept_axial, swept_angular, swept_radial, conductivity, corner_areas, parcel_loads, dest_device, dest_cell):
-    chan, zh, th, k_above, k_next = exchange(
+    chan, saz, stt, kzl, kzh, ktl, kth, grads = exchange(
         parcel_loads, dest_device, dest_cell, fields, corner_areas, volume, swept_axial, swept_angular, conductivity
     )
-    vn, src, zlo, zhi, tlo, thi = deposit(
-        chan, fields, volume, swept_axial, swept_angular, swept_radial, zh[22], th[22, :8]
+    vn, src, zlo, zhi, tlo, thi, grads = deposit(
+        chan, fields, volume, swept_axial, swept_angular, swept_radial, saz, stt, grads
     )
     below, above = up(zhi), down(zlo)
     before_, after = onward(thi), backward(tlo)
-    grads = gradients(fields, corner_areas, volume, zh, th)
-    diffused = diffuse(src, below, above, before_, after, conductivity, vn, zh[23], k_above, th[23, :8], k_next)
+    diffused = diffuse(src, below, above, before_, after, conductivity, vn, kzl, kzh, ktl, kth)
     return vn, diffused, grads
 
 

time: 79.7 us -> 66.9 us (0.84)
  the two profiles are of different devices: /device:TPU:32 before, /device:TPU:7 now
where the time goes in v3:
time: 66.9 us; the launch traced here: 66.5 us
  Pallas kernels  49.4 us (74%)
  starting transfers between devices  10 us (15%)
  waiting for transfers between devices  5.67 us (8%)
  local copies, waits for them, and re-layouts  0.71 us (1%)
  between operations  0.68 us (1%)
    pallas_call x1, Pallas kernels, exchange(): pl.pallas_call(exchange_kernel, grid=(1,), out_shape=[jax.ShapeDtypeStruc...  27.2 us
    pallas_call x1, Pallas kernels, deposit(): pl.pallas_call(deposit_kernel, out_shape=(sd((8, 32, 256), F32), sd((9, 8...  14.3 us
    pallas_call x1, Pallas kernels, diffuse(): pl.pallas_call(diffuse_kernel, grid=(9,), out_shape=jax.ShapeDtypeStruct(...  7.96 us
    ppermute x1, starting transfers between devices, up(): return lax.ppermute(x, 'slab', [(i, i + 1) for i in range(31)])  5.37 us
    ppermute x1, waiting for transfers between devices, down(): return lax.ppermute(x, 'slab', [(i + 1, i) for i in range(31)])  3.37 us
    ppermute x1, waiting for transfers between devices, onward(): return lax.ppermute(x, 'sector', [(i, (i + 1) % 4) for i in range(4)])  2.29 us
    ppermute x1, starting transfers between devices, backward(): return lax.ppermute(x, 'sector', [((i + 1) % 4, i) for i in range(4)])  2.27 us
    ppermute x1, starting transfers between devices, down(): return lax.ppermute(x, 'slab', [(i + 1, i) for i in range(31)])  1.92 us
  transfers between devices with their start and end apart: 4, of which 2 were waited for; matrix products, arithmetic and copies ran while one was open for 0% of the time, Pallas kernels for 0%

profile of v3, /device:TPU:7, one launch (start us, length us, event | category | flops | bytes accessed | tf_op | source)
XLA Modules:
  0.0 66.5 jit_solution(3320810278037161338)
XLA Ops:
  0.6 27.2 %exchange.1 = (f32[10,64,128]{2,1,0:T(8,128)}, f32[32,256]{1,0:T(8,128)}, f32[8,256]{1,0:T(8,128)}, f32[32,256]{1,0:T(8,128)}, f32[32,256]{1,0:T(8,128)}, /*inde...) custom-call(f32[9,4096]{1,0:T(8,128)} %loads_ref.1, s32[1,4096]{1,0:T(1,128)} %bitcast.2, ...), custom_call_target="tpu_custom_call" | custom-call | tf_op jit(solution)/shard_map/exchange/pallas_call | solution.py:427
  27.8 14.3 %deposit.1 = (f32[8,32,256]{2,1,0:T(8,128)}, f32[9,8,32,256]{3,2,1,0:T(8,128)}, f32[9,32,256]{2,1,0:T(8,128)}, f32[9,32,256]{2,1,0:T(8,128)}, f32[9,8,256]{2,1,0...) custom-call(f32[10,64,128]{2,1,0:T(8,128)} %get-tuple-element.18.chan_ref, f32[9,8,32,256]{3,2,1,0:T(8,128)} %fields_ref.3, ...), custom_call_target="tpu_custom_call" | custom-call | tf_op jit(solution)/shard_map/deposit/pallas_call | solution.py:120
  42.1 5.4 %collective-permute-start = (f32[9,32,256]{2,1,0:T(8,128)}, f32[9,32,256]{2,1,0:T(8,128)S(1)}, u32[]{:S(2)}, u32[]{:S(2)}) collective-permute-start(f32[9,32,256]{2,1,0:T(8,128)} %get-tuple-element.24), channel_id=1, source_target_pairs={{0,4},{4,8},{8,12},{12,16},{16,20},{20,24},{24,28},{28,32},{32,36}... | collective-permute-start | bytes 884744 | tf_op jit(solution)/shard_map/ppermute | solution.py:452
  47.5 1.9 %collective-permute-start.1 = (f32[9,32,256]{2,1,0:T(8,128)}, f32[9,32,256]{2,1,0:T(8,128)S(1)}, u32[]{:S(2)}, u32[]{:S(2)}) collective-permute-start(f32[9,32,256]{2,1,0:T(8,128)} %get-tuple-element.25), channel_id=1, source_target_pairs={{4,0},{8,4},{12,8},{16,12},{20,16},{24,20},{28,24},{32,28},{36,32}... | collective-permute-start | bytes 884744 | tf_op jit(solution)/shard_map/ppermute | solution.py:456
  49.4 0.5 collective-permute-start.2
  49.9 2.3 %collective-permute-start.3 = (f32[9,8,256]{2,1,0:T(8,128)}, f32[9,8,256]{2,1,0:T(8,128)S(1)}, u32[]{:S(2)}, u32[]{:S(2)}) collective-permute-start(f32[9,8,256]{2,1,0:T(8,128)} %get-tuple-element.27), channel_id=1, source_target_pairs={{1,0},{2,1},{3,2},{0,3},{5,4},{6,5},{7,6},{4,7},{9,8},{10,9},{11,1... | collective-permute-start | bytes 221192 | tf_op jit(solution)/shard_map/ppermute | solution.py:464
  52.2 2.3 %collective-permute-done.2.tlo_ref = f32[9,8,256]{2,1,0:T(8,128)S(1)} collective-permute-done((f32[9,8,256]{2,1,0:T(8,128)}, f32[9,8,256]{2,1,0:T(8,128)S(1)}, u32[]{:S(2)}, u32[]{:S(2)}) %collective-permute-start.2) | collective-permute-done | bytes 73760 | tf_op jit(solution)/shard_map/ppermute | solution.py:460
  54.5 0.0 copy-start.2
  54.5 0.0 collective-permute-done.3.thi_ref
  54.5 0.0 copy-start.3
  54.5 0.0 collective-permute-done.zlo_ref
  54.5 0.0 copy-start
  54.5 3.4 %collective-permute-done.1.zhi_ref = f32[9,32,256]{2,1,0:T(8,128)S(1)} collective-permute-done((f32[9,32,256]{2,1,0:T(8,128)}, f32[9,32,256]{2,1,0:T(8,128)S(1)}, u32[]{:S(2)}, u32[]{:S(2)}) %collective-permute-start.1) | collective-permute-done | bytes 294944 | tf_op jit(solution)/shard_map/ppermute | solution.py:456
  57.9 0.0 copy-start.1
  57.9 0.0 copy-done.2
  57.9 0.0 copy-done.3
  57.9 0.0 copy-done
  57.9 0.7 %copy-done.1 = f32[9,32,256]{2,1,0:T(8,128)} copy-done((f32[9,32,256]{2,1,0:T(8,128)}, f32[9,32,256]{2,1,0:T(8,128)S(1)}, u32[]{:S(2)}) %copy-start.1) | copy-done | bytes 294936
  58.6 8.0 %diffuse.1 = f32[9,8,32,256]{3,2,1,0:T(8,128)} custom-call(f32[9,8,32,256]{3,2,1,0:T(8,128)} %get-tuple-element.23.src_ref, f32[9,32,256]{2,1,0:T(8,128)} %copy-done, f32[9,32,256]{2,1,0:T(8,128)} %copy-done.1, f32[9,8,256]{2,1,0:T(8,128)} %copy-done.2, f32[9,8,256]{2,1,0:T(8,128)} %copy-done.3, f32[8,32,256]{2,1,0:T(8,128)} %k_ref.1, ...), custom_call_target="tpu_custom_call" | custom-call | tf_op jit(solution)/shard_map/diffuse/pallas_call | solution.py:231
Async XLA Ops:
  42.1 12.4 %collective-permute-start = (f32[9,32,256]{2,1,0:T(8,128)}, f32[9,32,256]{2,1,0:T(8,128)S(1)}, u32[]{:S(2)}, u32[]{:S(2)}) collective-permute-start(f32[9,32,256]{2,1,0:T(8,128)} %get-tuple-element.24), channel_id=1, source_target_pairs={{0,4},{4,8},{8,12},{12,16},{16,20},{20,24},{24,28},{28,32},{32,36}... | collective-permute-start | bytes 884744 | tf_op jit(solution)/shard_map/ppermute | solution.py:452
  47.5 10.4 %collective-permute-start.1 = (f32[9,32,256]{2,1,0:T(8,128)}, f32[9,32,256]{2,1,0:T(8,128)S(1)}, u32[]{:S(2)}, u32[]{:S(2)}) collective-permute-start(f32[9,32,256]{2,1,0:T(8,128)} %get-tuple-element.25), channel_id=1, source_target_pairs={{4,0},{8,4},{12,8},{16,12},{20,16},{24,20},{28,24},{32,28},{36,32}... | collective-permute-start | bytes 884744 | tf_op jit(solution)/shard_map/ppermute | solution.py:456
  49.4 5.0 %collective-permute-start.2 = (f32[9,8,256]{2,1,0:T(8,128)}, f32[9,8,256]{2,1,0:T(8,128)S(1)}, u32[]{:S(2)}, u32[]{:S(2)}) collective-permute-start(f32[9,8,256]{2,1,0:T(8,128)} %get-tuple-element.26), channel_id=1, source_target_pairs={{0,1},{1,2},{2,3},{3,0},{4,5},{5,6},{6,7},{7,4},{8,9},{9,10},{10,1... | collective-permute-start | bytes 221192 | tf_op jit(solution)/shard_map/ppermute | solution.py:460
  49.9 4.6 %collective-permute-start.3 = (f32[9,8,256]{2,1,0:T(8,128)}, f32[9,8,256]{2,1,0:T(8,128)S(1)}, u32[]{:S(2)}, u32[]{:S(2)}) collective-permute-start(f32[9,8,256]{2,1,0:T(8,128)} %get-tuple-element.27), channel_id=1, source_target_pairs={{1,0},{2,1},{3,2},{0,3},{5,4},{6,5},{7,6},{4,7},{9,8},{10,9},{11,1... | collective-permute-start | bytes 221192 | tf_op jit(solution)/shard_map/ppermute | solution.py:464
  54.5 3.4 %copy-start.2 = (f32[9,8,256]{2,1,0:T(8,128)}, f32[9,8,256]{2,1,0:T(8,128)S(1)}, u32[]{:S(2)}) copy-start(f32[9,8,256]{2,1,0:T(8,128)S(1)} %collective-permute-done.2.tlo_ref) | copy-start | bytes 221188
  54.5 3.4 %copy-start.3 = (f32[9,8,256]{2,1,0:T(8,128)}, f32[9,8,256]{2,1,0:T(8,128)S(1)}, u32[]{:S(2)}) copy-start(f32[9,8,256]{2,1,0:T(8,128)S(1)} %collective-permute-done.3.thi_ref) | copy-start | bytes 221188
  54.5 3.4 %copy-start = (f32[9,32,256]{2,1,0:T(8,128)}, f32[9,32,256]{2,1,0:T(8,128)S(1)}, u32[]{:S(2)}) copy-start(f32[9,32,256]{2,1,0:T(8,128)S(1)} %collective-permute-done.zlo_ref) | copy-start | bytes 884740
  57.9 0.7 %copy-start.1 = (f32[9,32,256]{2,1,0:T(8,128)}, f32[9,32,256]{2,1,0:T(8,128)S(1)}, u32[]{:S(2)}) copy-start(f32[9,32,256]{2,1,0:T(8,128)S(1)} %collective-permute-done.1.zhi_ref) | copy-start | bytes 884740

commit v4 on v3

--- a/solution.py
+++ b/solution.py
@@ -35,7 +35,7 @@
 
 def deposit_kernel(
     chan_ref, fields_ref, vol_ref, sa_ref, st_ref, sr_ref, saz_ref, stt_ref, grads_ref,
-    vn_ref, src_ref, zlo_ref, zhi_ref, tlo_ref, thi_ref, grads_out_ref,
+    vn_ref, src_ref, tlo_ref, thi_ref, grads_out_ref,
     sort_ref, acc_ref, rank_ref, gbuf, sems,
 ):
     arriving = pltpu.make_async_copy(grads_ref, gbuf, sems.at[0])
@@ -107,10 +107,6 @@
         for f in range(9):
             v = fields_ref[f, a] + acc_ref[f, a] * inv
             src_ref[f, a] = v
-            if a == 0:
-                zlo_ref[f] = v
-            if a == 7:
-                zhi_ref[f] = v
             tlo_ref[f, a : a + 1, :] = v[0:1]
             thi_ref[f, a : a + 1, :] = v[31:32]
 
@@ -121,11 +117,11 @@
         deposit_kernel,
         out_shape=(
             sd((8, 32, 256), F32), sd((9, 8, 32, 256), F32),
-            sd((9, 32, 256), F32), sd((9, 32, 256), F32), sd((9, 8, 256), F32), sd((9, 8, 256), F32),
+            sd((9, 8, 256), F32), sd((9, 8, 256), F32),
             sd((27, 8, 32, 256), F32),
         ),
         in_specs=[VM] * 8 + [pl.BlockSpec(memory_space=pl.ANY)],
-        out_specs=[VM] * 6 + [pl.BlockSpec(memory_space=pl.ANY)],
+        out_specs=[VM] * 4 + [pl.BlockSpec(memory_space=pl.ANY)],
         scratch_shapes=[
             pltpu.VMEM((320, 256), F32),
             pltpu.VMEM((9, 8, 32, 256), F32),
@@ -169,77 +165,133 @@
 
 
 def gradient_plane(f_ref, w_ref, a0_ref, a1_ref, now, prev, out_ref, a):
-    for t in range(4):
-        for h in range(2):
-            at = (pl.ds(8 * t, 8), pl.ds(128 * h, 128))
-            inv = 1.0 / (w_ref[(now,) + at] + w_ref[(prev,) + at])
-            for i in range(3):
-                acc = [None] * 9
-                for dz in range(2):
-                    for q in range(4):
-                        area = (a1_ref if dz else a0_ref)[(i, q) + at]
-                        for f in range(9):
-                            term = area * f_ref[(prev if dz else now, q, f) + at]
-                            acc[f] = term if dz + q == 0 else acc[f] + term
+    def part(n, unused):
+        i = lax.rem(n, 3)
+        rows = pl.ds(pl.multiple_of(n // 3 * 8, 8), 8)
+        inv = 1.0 / (w_ref[now, rows] + w_ref[prev, rows])
+        acc = [None] * 9
+        for dz in range(2):
+            for q in range(4):
+                area = (a1_ref if dz else a0_ref)[i, q, rows]
                 for f in range(9):
-                    out_ref[(9 * i + f, a) + at] = acc[f] * inv
-
-
-def diffuse_kernel(src_ref, zlo_ref, zhi_ref, tlo_ref, thi_ref, k_ref, vn_ref, kzl_ref, kzh_ref, ktl_ref, kth_ref, out_ref, w_ref):
+                    term = area * f_ref[prev if dz else now, q, f, rows]
+                    acc[f] = term if dz + q == 0 else acc[f] + term
+        for f in range(9):
+            out_ref[9 * i + f, a, rows] = acc[f] * inv
+        return unused
+
+    lax.fori_loop(0, 12, part, 0)
+
+
+def diffuse_kernel(
+    src_ref, tlo_ref, thi_ref, k_ref, vn_ref, kzl_ref, kzh_ref, ktl_ref, kth_ref, out_ref,
+    sbuf, obuf, zlo, zhi, tlo, thi, w_ref, send_sems, recv_sems, load_sem, store_sems,
+):
+    slab, sector = lax.axis_index("slab"), lax.axis_index("sector")
+    above = (lax.rem(slab + 1, 32), sector)
+    below = (lax.rem(slab + 31, 32), sector)
+    ahead = (slab, lax.rem(sector + 1, 4))
+    behind = (slab, lax.rem(sector + 3, 4))
+    barrier = pltpu.get_barrier_semaphore()
+    for to in (above, below, ahead, behind):
+        pl.semaphore_signal(barrier, inc=1, device_id=to, device_id_type=pl.DeviceIdType.MESH)
+    loading = pltpu.make_async_copy(src_ref, sbuf, load_sem)
+    loading.start()
+    halo = [
+        (thi_ref, tlo, ahead), (tlo_ref, thi, behind),
+        (src_ref.at[:, 7], zlo, above), (src_ref.at[:, 0], zhi, below),
+    ]
+    copies = [
+        pltpu.make_async_remote_copy(
+            src_ref=s, dst_ref=t, send_sem=send_sems.at[n], recv_sem=recv_sems.at[n],
+            device_id=to, device_id_type=pl.DeviceIdType.MESH,
+        )
+        for n, (s, t, to) in enumerate(halo)
+    ]
+    pl.semaphore_wait(barrier, 4)
+    for copy in copies:
+        copy.start()
     row = iota((32, 256), 0)
     lane = iota((32, 256), 1)
-
-    @pl.when(pl.program_id(0) == 0)
-    def _():
-        for a in range(8):
-            k = k_ref[a]
-            near = [
-                kzl_ref[...] if a == 0 else k_ref[a - 1],
-                kzh_ref[...] if a == 7 else k_ref[a + 1],
-                jnp.where(row == 0, ktl_ref[a : a + 1], pltpu.roll(k, 1, 0)),
-                jnp.where(row == 31, kth_ref[a : a + 1], pltpu.roll(k, 31, 0)),
-                jnp.where(lane == 0, 0.0, pltpu.roll(k, 1, 1)),
-                jnp.where(lane == 255, 0.0, pltpu.roll(k, 255, 1)),
-            ]
-            scale = (0.2 * k) / vn_ref[a]
-            total = None
-            for n, kn in enumerate(near):
-                w = scale * kn / (k + kn)
-                w_ref[n, a] = w
-                total = w if total is None else total + w
-            w_ref[6, a] = 1.0 - total
-
     for a in range(8):
-        s = src_ref[0, a]
+        k = k_ref[a]
         near = [
-            zlo_ref[0] if a == 0 else src_ref[0, a - 1],
-            zhi_ref[0] if a == 7 else src_ref[0, a + 1],
-            jnp.where(row == 0, tlo_ref[0, a : a + 1], pltpu.roll(s, 1, 0)),
-            jnp.where(row == 31, thi_ref[0, a : a + 1], pltpu.roll(s, 31, 0)),
+            kzl_ref[...] if a == 0 else k_ref[a - 1],
+            kzh_ref[...] if a == 7 else k_ref[a + 1],
+            jnp.where(row == 0, ktl_ref[a : a + 1], pltpu.roll(k, 1, 0)),
+            jnp.where(row == 31, kth_ref[a : a + 1], pltpu.roll(k, 31, 0)),
+            jnp.where(lane == 0, 0.0, pltpu.roll(k, 1, 1)),
+            jnp.where(lane == 255, 0.0, pltpu.roll(k, 255, 1)),
+        ]
+        scale = (0.2 * k) / vn_ref[a]
+        total = None
+        for n, kn in enumerate(near):
+            w = scale * kn / (k + kn)
+            w_ref[n, a] = w
+            total = w if total is None else total + w
+        w_ref[6, a] = 1.0 - total
+    loading.wait()
+    copies[0].wait()
+    copies[1].wait()
+
+    def plane(f, a, under, over):
+        s = sbuf[f, a]
+        near = [
+            under, over,
+            jnp.where(row == 0, tlo[f, a : a + 1], pltpu.roll(s, 1, 0)),
+            jnp.where(row == 31, thi[f, a : a + 1], pltpu.roll(s, 31, 0)),
             pltpu.roll(s, 1, 1),
             pltpu.roll(s, 255, 1),
         ]
         out = w_ref[6, a] * s
         for n in range(6):
             out = out + w_ref[n, a] * near[n]
-        out_ref[0, a] = out
-
-
-def diffuse(src, zlo, zhi, tlo, thi, k, vn, kzl, kzh, ktl, kth):
-    whole = lambda shape: pl.BlockSpec(shape, lambda f: (0,) * len(shape))
-    each = lambda shape: pl.BlockSpec((1,) + shape, lambda f: (f,) + (0,) * len(shape))
+        obuf[f, a] = out
+
+    def inner(f, unused):
+        for a in range(1, 7):
+            plane(f, a, sbuf[f, a - 1], sbuf[f, a + 1])
+        return unused
+
+    lax.fori_loop(0, 9, inner, 0)
+    middle = pltpu.make_async_copy(obuf.at[:, 1:7], out_ref.at[:, 1:7], store_sems.at[0])
+    middle.start()
+    copies[2].wait()
+    copies[3].wait()
+
+    def ends(f, unused):
+        plane(f, 0, zlo[f], sbuf[f, 1])
+        plane(f, 7, sbuf[f, 6], zhi[f])
+        return unused
+
+    lax.fori_loop(0, 9, ends, 0)
+    first = pltpu.make_async_copy(obuf.at[:, 0], out_ref.at[:, 0], store_sems.at[1])
+    last = pltpu.make_async_copy(obuf.at[:, 7], out_ref.at[:, 7], store_sems.at[2])
+    first.start()
+    last.start()
+    middle.wait()
+    first.wait()
+    last.wait()
+
+
+def diffuse(src, tlo, thi, k, vn, kzl, kzh, ktl, kth):
+    any_ = pl.BlockSpec(memory_space=pl.ANY)
+    dma = pltpu.SemaphoreType.DMA
+    cells = (9, 8, 32, 256)
     return pl.pallas_call(
         diffuse_kernel,
-        grid=(9,),
-        out_shape=jax.ShapeDtypeStruct((9, 8, 32, 256), F32),
-        in_specs=[
-            each((8, 32, 256)), each((32, 256)), each((32, 256)), each((8, 256)), each((8, 256)),
-            whole((8, 32, 256)), whole((8, 32, 256)), whole((32, 256)), whole((32, 256)), whole((8, 256)), whole((8, 256)),
+        out_shape=jax.ShapeDtypeStruct(cells, F32),
+        in_specs=[any_] * 3 + [VM] * 6,
+        out_specs=any_,
+        scratch_shapes=[
+            pltpu.VMEM(cells, F32), pltpu.VMEM(cells, F32),
+            pltpu.VMEM((9, 32, 256), F32), pltpu.VMEM((9, 32, 256), F32),
+            pltpu.VMEM((9, 8, 256), F32), pltpu.VMEM((9, 8, 256), F32),
+            pltpu.VMEM((7, 8, 32, 256), F32), dma((4,)), dma((4,)), dma, dma((3,)),
         ],
-        out_specs=each((8, 32, 256)),
-        scratch_shapes=[pltpu.VMEM((7, 8, 32, 256), F32)],
+        compiler_params=pltpu.CompilerParams(has_side_effects=True, collective_id=1),
         name="diffuse",
-    )(src, zlo, zhi, tlo, thi, k, vn, kzl, kzh, ktl, kth)
+    )(src, tlo, thi, k, vn, kzl, kzh, ktl, kth)
 
 
 def exchange_kernel(
@@ -322,10 +374,6 @@
         )
         for n, (s, t, to) in enumerate(halo)
     ]
-    pl.semaphore_wait(barrier, 127)
-    for copy in copies:
-        copy.start()
-
     acc_ref[...] = jnp.zeros_like(acc_ref)
     part = 512
     for b in range(4096 // part):
@@ -342,6 +390,9 @@
     for s in range(5):
         out_buf[:, s, :] = acc_ref[s * 128 : (s + 1) * 128, :].T
 
+    pl.semaphore_wait(barrier, 127)
+    for copy in copies:
+        copy.start()
     own = pltpu.make_async_copy(out_buf.at[me], in_buf.at[me], own_sem)
     own.start()
 
@@ -448,32 +499,14 @@
     )(loads, dest.reshape(1, 4096), cell.reshape(1, 4096), sa, k, k, st, k, k, fields, areas, volume)
 
 
-def up(x):
-    return lax.ppermute(x, "slab", [(i, i + 1) for i in range(31)])
-
-
-def down(x):
-    return lax.ppermute(x, "slab", [(i + 1, i) for i in range(31)])
-
-
-def onward(x):
-    return lax.ppermute(x, "sector", [(i, (i + 1) % 4) for i in range(4)])
-
-
-def backward(x):
-    return lax.ppermute(x, "sector", [((i + 1) % 4, i) for i in range(4)])
-
-
 def local(fields, volume, swept_axial, swept_angular, swept_radial, conductivity, corner_areas, parcel_loads, dest_device, dest_cell):
     chan, saz, stt, kzl, kzh, ktl, kth, grads = exchange(
         parcel_loads, dest_device, dest_cell, fields, corner_areas, volume, swept_axial, swept_angular, conductivity
     )
-    vn, src, zlo, zhi, tlo, thi, grads = deposit(
+    vn, src, tlo, thi, grads = deposit(
         chan, fields, volume, swept_axial, swept_angular, swept_radial, saz, stt, grads
     )
-    below, above = up(zhi), down(zlo)
-    before_, after = onward(thi), backward(tlo)
-    diffused = diffuse(src, below, above, before_, after, conductivity, vn, kzl, kzh, ktl, kth)
+    diffused = diffuse(src, tlo, thi, conductivity, vn, kzl, kzh, ktl, kth)
     return vn, diffused, grads
 
 

time: 66.9 us -> 62 us (0.927)
  the two profiles are of different devices: /device:TPU:7 before, /device:TPU:0 now
where the time goes in v4:
time: 62 us; the launch traced here: 61.8 us
  Pallas kernels  57.8 us (93%)
  local copies, waits for them, and re-layouts  3.36 us (5%)
  between operations  0.66 us (1%)
    pallas_call x1, Pallas kernels, exchange(): pl.pallas_call(exchange_kernel, grid=(1,), out_shape=[jax.ShapeDtypeStruc...  30.7 us
    pallas_call x1, Pallas kernels, deposit(): pl.pallas_call(deposit_kernel, out_shape=(sd((8, 32, 256), F32), sd((9, 8...  14.1 us
    pallas_call x1, Pallas kernels, diffuse(): pl.pallas_call(diffuse_kernel, out_shape=jax.ShapeDtypeStruct(cells, F32)...  13 us
    unnamed x1, local copies, waits for them, and re-layouts  3.36 us

profile of v4, /device:TPU:0, one launch (start us, length us, event | category | flops | bytes accessed | tf_op | source)
XLA Modules:
  0.0 61.8 jit_solution(4710687193390738119)
XLA Ops:
  0.6 30.7 %exchange.1 = (f32[10,64,128]{2,1,0:T(8,128)}, f32[32,256]{1,0:T(8,128)}, f32[8,256]{1,0:T(8,128)}, f32[32,256]{1,0:T(8,128)}, f32[32,256]{1,0:T(8,128)}, /*inde...) custom-call(f32[9,4096]{1,0:T(8,128)} %loads_ref.1, s32[1,4096]{1,0:T(1,128)} %bitcast.2, ...), custom_call_target="tpu_custom_call" | custom-call | tf_op jit(solution)/shard_map/exchange/pallas_call | solution.py:478
  31.3 14.1 %deposit.1 = (f32[8,32,256]{2,1,0:T(8,128)}, f32[9,8,32,256]{3,2,1,0:T(8,128)}, f32[9,8,256]{2,1,0:T(8,128)}, f32[9,8,256]{2,1,0:T(8,128)}, f32[27,8,32,256]{3,2,1,0:T(8,128)}) custom-call(f32[10,64,128]{2,1,0:T(8,128)} %get-tuple-element.16.chan_ref, f32[9,8,32,256]{3,2,1,0:T(8,128)} %fields_ref.3, f32[8,32,256]{2,1,0:T(8,128)} %vol_ref.3, ...), custom_call_target="tpu_custom_call" | custom-call | tf_op jit(solution)/shard_map/deposit/pallas_call | solution.py:116
  45.4 13.0 %diffuse.1 = f32[9,8,32,256]{3,2,1,0:T(8,128)} custom-call(f32[9,8,32,256]{3,2,1,0:T(8,128)} %get-tuple-element.21.src_ref, f32[9,8,256]{2,1,0:T(8,128)} %get-tuple-element.22.tlo_ref, f32[9,8,256]{2,1,0:T(8,128)} %get-tuple-element.23.thi_ref, f32[8,32,256]{2,1,0:T(8,128)} %k_ref.1, f32[8,32,256]{2,1,0:T(8,128)} %get-tuple-element.32.vn_ref, ...), custom_call_target="tpu_custom_call" | custom-call | tf_op jit(solution)/shard_map/diffuse/pallas_call | solution.py:281
  58.4 3.4 %copy.14 = f32[9,8,32,256]{3,2,1,0:T(8,128)} copy(f32[9,8,32,256]{3,2,1,0:T(8,128)} %diffuse.1) | data formatting | bytes 4718592

commit v5 on v4

--- a/solution.py
+++ b/solution.py
@@ -35,13 +35,11 @@
 
 def deposit_kernel(
     chan_ref, fields_ref, vol_ref, sa_ref, st_ref, sr_ref, saz_ref, stt_ref, grads_ref,
-    vn_ref, src_ref, tlo_ref, thi_ref, grads_out_ref,
-    sort_ref, acc_ref, rank_ref, gbuf, sems,
+    vn_ref, vn2_ref, src_ref, tlo_ref, thi_ref, grads_out_ref,
+    sort_ref, acc_ref, rank_ref, sem,
 ):
-    arriving = pltpu.make_async_copy(grads_ref, gbuf, sems.at[0])
-    leaving = pltpu.make_async_copy(gbuf, grads_out_ref, sems.at[1])
-    arriving.start()
-    sa, st, sr = sa_ref[...], st_ref[...], sr_ref[...]
+    leaving = pltpu.make_async_copy(grads_ref, grads_out_ref, sem)
+    leaving.start()
     for a in range(8):
         below = saz_ref[...] if a == 0 else sa_ref[a - 1]
         stp = st_ref[a]
@@ -50,7 +48,9 @@
         srp = sr_ref[a]
         lane = iota((32, 256), 1)
         inner = jnp.where(lane == 0, 0.0, pltpu.roll(srp, 1, 1))
-        vn_ref[a] = vol_ref[a] + sa_ref[a] - below + stp - side + srp - inner
+        vn = vol_ref[a] + sa_ref[a] - below + stp - side + srp - inner
+        vn_ref[a] = vn
+        vn2_ref[a] = vn
     acc_ref[...] = jnp.zeros_like(acc_ref)
     earlier = before(256)
 
@@ -71,9 +71,6 @@
             count = jnp.dot(g[:, b * 256 : (b + 1) * 256], earlier, preferred_element_type=F32)
             ranks.append(jnp.sum(gb * (count + carry) , axis=0, keepdims=True))
             carry = carry + jnp.sum(gb, axis=1, keepdims=True)
-        if ch == 1:
-            arriving.wait()
-            leaving.start()
         rank_ref[...] = jnp.concatenate(ranks, 1).astype(I32)
         most = jnp.max(carry).astype(I32)
         his, los = [], []
@@ -101,14 +98,14 @@
             return carry_unused
 
         lax.fori_loop(0, (most + SLOTS - 1) // SLOTS, one_round, 0)
-    leaving.wait()
     for a in range(8):
-        inv = 1.0 / vn_ref[a]
+        inv = 1.0 / vn2_ref[a]
         for f in range(9):
             v = fields_ref[f, a] + acc_ref[f, a] * inv
             src_ref[f, a] = v
             tlo_ref[f, a : a + 1, :] = v[0:1]
             thi_ref[f, a : a + 1, :] = v[31:32]
+    leaving.wait()
 
 
 def deposit(chan, fields, volume, sa, st, sr, saz, stt, grads):
@@ -116,19 +113,19 @@
     return pl.pallas_call(
         deposit_kernel,
         out_shape=(
-            sd((8, 32, 256), F32), sd((9, 8, 32, 256), F32),
+            sd((8, 32, 256), F32), sd((8, 32, 256), F32), sd((9, 8, 32, 256), F32),
             sd((9, 8, 256), F32), sd((9, 8, 256), F32),
             sd((27, 8, 32, 256), F32),
         ),
         in_specs=[VM] * 8 + [pl.BlockSpec(memory_space=pl.ANY)],
-        out_specs=[VM] * 4 + [pl.BlockSpec(memory_space=pl.ANY)],
+        out_specs=[VM] * 5 + [pl.BlockSpec(memory_space=pl.ANY)],
         scratch_shapes=[
             pltpu.VMEM((320, 256), F32),
             pltpu.VMEM((9, 8, 32, 256), F32),
             pltpu.VMEM((1, CHUNK), I32),
-            pltpu.VMEM((27, 8, 32, 256), F32),
-            pltpu.SemaphoreType.DMA((2,)),
+            pltpu.SemaphoreType.DMA,
         ],
+        compiler_params=pltpu.CompilerParams(vmem_limit_bytes=24 << 20),
         name="deposit",
     )(chan, fields, volume, sa, st, sr, saz, stt, grads)
 
@@ -185,7 +182,7 @@
 
 def diffuse_kernel(
     src_ref, tlo_ref, thi_ref, k_ref, vn_ref, kzl_ref, kzh_ref, ktl_ref, kth_ref, out_ref,
-    sbuf, obuf, zlo, zhi, tlo, thi, w_ref, send_sems, recv_sems, load_sem, store_sems,
+    zlo, zhi, tlo, thi, w_ref, send_sems, recv_sems,
 ):
     slab, sector = lax.axis_index("slab"), lax.axis_index("sector")
     above = (lax.rem(slab + 1, 32), sector)
@@ -195,8 +192,6 @@
     barrier = pltpu.get_barrier_semaphore()
     for to in (above, below, ahead, behind):
         pl.semaphore_signal(barrier, inc=1, device_id=to, device_id_type=pl.DeviceIdType.MESH)
-    loading = pltpu.make_async_copy(src_ref, sbuf, load_sem)
-    loading.start()
     halo = [
         (thi_ref, tlo, ahead), (tlo_ref, thi, behind),
         (src_ref.at[:, 7], zlo, above), (src_ref.at[:, 0], zhi, below),
@@ -230,12 +225,11 @@
             w_ref[n, a] = w
             total = w if total is None else total + w
         w_ref[6, a] = 1.0 - total
-    loading.wait()
     copies[0].wait()
     copies[1].wait()
 
     def plane(f, a, under, over):
-        s = sbuf[f, a]
+        s = src_ref[f, a]
         near = [
             under, over,
             jnp.where(row == 0, tlo[f, a : a + 1], pltpu.roll(s, 1, 0)),
@@ -246,68 +240,62 @@
         out = w_ref[6, a] * s
         for n in range(6):
             out = out + w_ref[n, a] * near[n]
-        obuf[f, a] = out
+        out_ref[f, a] = out
 
     def inner(f, unused):
         for a in range(1, 7):
-            plane(f, a, sbuf[f, a - 1], sbuf[f, a + 1])
+            plane(f, a, src_ref[f, a - 1], src_ref[f, a + 1])
         return unused
 
     lax.fori_loop(0, 9, inner, 0)
-    middle = pltpu.make_async_copy(obuf.at[:, 1:7], out_ref.at[:, 1:7], store_sems.at[0])
-    middle.start()
     copies[2].wait()
     copies[3].wait()
 
     def ends(f, unused):
-        plane(f, 0, zlo[f], sbuf[f, 1])
-        plane(f, 7, sbuf[f, 6], zhi[f])
+        plane(f, 0, zlo[f], src_ref[f, 1])
+        plane(f, 7, src_ref[f, 6], zhi[f])
         return unused
 
     lax.fori_loop(0, 9, ends, 0)
-    first = pltpu.make_async_copy(obuf.at[:, 0], out_ref.at[:, 0], store_sems.at[1])
-    last = pltpu.make_async_copy(obuf.at[:, 7], out_ref.at[:, 7], store_sems.at[2])
-    first.start()
-    last.start()
-    middle.wait()
-    first.wait()
-    last.wait()
 
 
 def diffuse(src, tlo, thi, k, vn, kzl, kzh, ktl, kth):
-    any_ = pl.BlockSpec(memory_space=pl.ANY)
     dma = pltpu.SemaphoreType.DMA
     cells = (9, 8, 32, 256)
     return pl.pallas_call(
         diffuse_kernel,
         out_shape=jax.ShapeDtypeStruct(cells, F32),
-        in_specs=[any_] * 3 + [VM] * 6,
-        out_specs=any_,
+        in_specs=[VM] * 9,
+        out_specs=VM,
         scratch_shapes=[
-            pltpu.VMEM(cells, F32), pltpu.VMEM(cells, F32),
             pltpu.VMEM((9, 32, 256), F32), pltpu.VMEM((9, 32, 256), F32),
             pltpu.VMEM((9, 8, 256), F32), pltpu.VMEM((9, 8, 256), F32),
-            pltpu.VMEM((7, 8, 32, 256), F32), dma((4,)), dma((4,)), dma, dma((3,)),
+            pltpu.VMEM((7, 8, 32, 256), F32), dma((4,)), dma((4,)),
         ],
-        compiler_params=pltpu.CompilerParams(has_side_effects=True, collective_id=1),
+        compiler_params=pltpu.CompilerParams(has_side_effects=True, collective_id=1, vmem_limit_bytes=16 << 20),
         name="diffuse",
     )(src, tlo, thi, k, vn, kzl, kzh, ktl, kth)
 
 
 def exchange_kernel(
-    loads_ref, dest_ref, cell_ref, sz_ref, kz_ref, kz0_ref, st_ref, kt_ref, kt0_ref,
-    fields_ref, areas_ref, vol_ref,
+    loads_in, dest_in, cell_in, fields_in, areas_in, vol_in, sa_in, st_in, k_in,
     chan_ref, saz_ref, stt_ref, kzl_ref, kzh_ref, ktl_ref, kth_ref, grads_ref,
     acc_ref, d_ref, rank_ref, out_buf, in_buf, azs, ts, cs, kbs, zr, tr, cr, kar, knr,
-    fbuf, abuf, vbuf, gbuf, f_ref, w_ref, a0_ref, a1_ref,
-    send_sems, recv_sems, psend_sem, precv_sem, own_sem, load_sems, store_sems,
+    loads_ref, dest_ref, cell_ref, sz_ref, kz_ref, kz0_ref, st_ref, kt_ref, kt0_ref,
+    fbuf, abuf, vbuf, f_ref, w_ref, a0_ref, a1_ref,
+    send_sems, recv_sems, psend_sem, precv_sem, own_sem, load_sems,
 ):
     slab, sector = lax.axis_index("slab"), lax.axis_index("sector")
     me = slab * 4 + sector
     barrier = pltpu.get_barrier_semaphore()
     loading = [
         pltpu.make_async_copy(s, t, load_sems.at[n])
-        for n, (s, t) in enumerate(((fields_ref, fbuf), (areas_ref, abuf), (vol_ref, vbuf)))
+        for n, (s, t) in enumerate((
+            (dest_in, dest_ref), (loads_in, loads_ref), (cell_in, cell_ref),
+            (fields_in, fbuf), (areas_in, abuf), (vol_in, vbuf),
+            (sa_in.at[7], sz_ref), (k_in.at[7], kz_ref), (k_in.at[0], kz0_ref),
+            (st_in.at[:, 24:32], st_ref), (k_in.at[:, 24:32], kt_ref), (k_in.at[:, 0:8], kt0_ref),
+        ))
     ]
     for copy in loading:
         copy.start()
@@ -319,6 +307,7 @@
 
     lax.fori_loop(1, 128, greet, 0)
 
+    loading[0].wait()
     blk, devices = 256, 128
     earlier = before(blk)
     carry = jnp.zeros((devices, 1), F32)
@@ -333,7 +322,7 @@
         ).astype(I32)
         carry = carry + jnp.sum(df, axis=1, keepdims=True)
 
-    for copy in loading:
+    for copy in loading[1:]:
         copy.wait()
     for n in range(12):
         x = abuf[n // 4, 4 + n % 4, 7].astype(F32)
@@ -348,7 +337,7 @@
     cs[21:22] = vbuf[7, 31:32]
     for n, (t_ref, z_ref) in enumerate(((st_ref, sz_ref), (kt_ref, kz_ref))):
         ts[22 + n] = t_ref[:, 7, :]
-        cs[22 + n : 23 + n] = z_ref[0, 31:32]
+        cs[22 + n : 23 + n] = z_ref[31:32]
     kbs[...] = kt0_ref[:, 0, :]
 
     above = (lax.rem(slab + 1, 32), sector)
@@ -357,9 +346,9 @@
     behind = (slab, lax.rem(sector + 3, 4))
     across = (lax.rem(slab + 1, 32), lax.rem(sector + 1, 4))
     halo = [
-        (sz_ref.at[0], zr.at[22], above),
-        (kz_ref.at[0], zr.at[23], above),
-        (kz0_ref.at[0], kar, below),
+        (sz_ref, zr.at[22], above),
+        (kz_ref, zr.at[23], above),
+        (kz0_ref, kar, below),
         (kbs, knr, behind),
         (ts, tr, ahead),
         (cs, cr, across),
@@ -378,18 +367,21 @@
     part = 512
     for b in range(4096 // part):
         sl = pl.ds(b * part, part)
-        o = one_hot(rank_ref[:, sl], 64)
+        rank = rank_ref[:, sl]
+        o = one_hot(rank & 31, 32)
         hi, lo = split(loads_ref[:, sl])
         cell = cell_ref[:, sl]
         row = (lax.shift_right_logical(cell, 8) * 256).astype(F32).astype(BF16)
         col = ((cell & 255) + 1).astype(F32).astype(BF16)
         his = jnp.concatenate([hi[c : c + 1] * o for c in range(9)] + [row * o], 0)
         los = jnp.concatenate([lo[c : c + 1] * o for c in range(9)] + [col * o], 0)
-        d = jnp.concatenate([d_ref[(2 * b + i) * 128 : (2 * b + i + 1) * 128, :] for i in range(2)], 1)
+        d = one_hot(dest_ref[:, sl] + lax.shift_right_logical(rank, 5) * 128, 256)
         acc_ref[...] += nt(jnp.concatenate([his, los], 1), jnp.concatenate([d, d], 1))
     for s in range(5):
-        out_buf[:, s, :] = acc_ref[s * 128 : (s + 1) * 128, :].T
-
+        block = jnp.concatenate(
+            [acc_ref[c * 32 : (c + 1) * 32, h * 128 : (h + 1) * 128] for c in (2 * s, 2 * s + 1) for h in range(2)], 0
+        )
+        out_buf[:, s, :] = block.T
     pl.semaphore_wait(barrier, 127)
     for copy in copies:
         copy.start()
@@ -419,9 +411,6 @@
             lambda i, q: beside(plane)(9 + 4 * i + 2 * dz + q % 2),
         )
 
-    def store(a):
-        return pltpu.make_async_copy(gbuf.at[:, a], grads_ref.at[:, a], store_sems.at[a])
-
     prepare_own(1, 7)
 
     def plane(n, unused):
@@ -430,8 +419,7 @@
         prepare_own(1 - now, a - 1)
         own_areas(a0_ref, a, 0)
         own_areas(a1_ref, a - 1, 1)
-        gradient_plane(f_ref, w_ref, a0_ref, a1_ref, now, 1 - now, gbuf, a)
-        store(a).start()
+        gradient_plane(f_ref, w_ref, a0_ref, a1_ref, now, 1 - now, grads_ref, a)
         return unused
 
     lax.fori_loop(0, 7, plane, 0)
@@ -447,8 +435,7 @@
     prepare(f_ref, w_ref, 1, lambda f: under(zr[f]), under(zr[21]), lambda c: under(cr[c : c + 1, :]))
     own_areas(a0_ref, 0, 0)
     prepare_areas(a1_ref, lambda i, q: zr[9 + 4 * i + q], lambda i, q: cr[9 + 4 * i + q : 10 + 4 * i + q, :])
-    gradient_plane(f_ref, w_ref, a0_ref, a1_ref, 0, 1, gbuf, 0)
-    store(0).start()
+    gradient_plane(f_ref, w_ref, a0_ref, a1_ref, 0, 1, grads_ref, 0)
     saz_ref[...] = under(zr[22])
     kzl_ref[...] = under(zr[23])
     kzh_ref[...] = jnp.where(slab < 31, kar[...], 0.0)
@@ -463,50 +450,41 @@
         first, second = in_buf[0:64, s, :], in_buf[64:128, s, :]
         chan_ref[2 * s] = jnp.where(lane, first, pltpu.roll(second, 64, 1))
         chan_ref[2 * s + 1] = jnp.where(lane, pltpu.roll(first, 64, 1), second)
-    for a in range(8):
-        store(a).wait()
 
 
 def exchange(loads, dest, cell, fields, areas, volume, sa, st, k):
-    at = lambda shape, *index: pl.BlockSpec(shape, lambda i: index)
-    whole = lambda *shape: at(shape, *(0,) * len(shape))
-    any_ = pl.BlockSpec(memory_space=pl.ANY)
-    shapes = [(10, 64, 128), (32, 256), (8, 256), (32, 256), (32, 256), (8, 256), (8, 256)]
+    hbm = pl.BlockSpec(memory_space=pltpu.HBM)
+    shapes = [(10, 64, 128), (32, 256), (8, 256), (32, 256), (32, 256), (8, 256), (8, 256), (27, 8, 32, 256)]
     dma = pltpu.SemaphoreType.DMA
     vm = lambda *shape, t=F32: pltpu.VMEM(shape, t)
-    plane, column = (1, 32, 256), (8, 8, 256)
     return pl.pallas_call(
         exchange_kernel,
-        grid=(1,),
-        out_shape=[jax.ShapeDtypeStruct(s, F32) for s in shapes + [(27, 8, 32, 256)]],
-        in_specs=[
-            whole(9, 4096), whole(1, 4096), whole(1, 4096),
-            at(plane, 7, 0, 0), at(plane, 7, 0, 0), at(plane, 0, 0, 0),
-            at(column, 0, 3, 0), at(column, 0, 3, 0), at(column, 0, 0, 0),
-            any_, any_, any_,
-        ],
-        out_specs=[whole(*s) for s in shapes] + [any_],
+        out_shape=[jax.ShapeDtypeStruct(s, F32) for s in shapes],
+        in_specs=[hbm] * 9,
+        out_specs=[VM] * 8,
         scratch_shapes=[
-            vm(640, 128), vm(2048, 256, t=BF16), vm(1, 4096, t=I32), vm(128, 5, 128), vm(128, 5, 128),
+            vm(320, 256), vm(2048, 256, t=BF16), vm(1, 4096, t=I32), vm(128, 5, 128), vm(128, 5, 128),
             vm(12, 32, 256), vm(24, 8, 256), vm(24, 256), vm(8, 256),
             vm(24, 32, 256), vm(24, 8, 256), vm(24, 256), vm(32, 256), vm(8, 256),
-            vm(9, 8, 32, 256), vm(3, 8, 8, 32, 256, t=BF16), vm(8, 32, 256), vm(27, 8, 32, 256),
+            vm(9, 4096), vm(1, 4096, t=I32), vm(1, 4096, t=I32), vm(32, 256), vm(32, 256), vm(32, 256),
+            vm(8, 8, 256), vm(8, 8, 256), vm(8, 8, 256),
+            vm(9, 8, 32, 256), vm(3, 8, 8, 32, 256, t=BF16), vm(8, 32, 256),
             vm(2, 4, 9, 32, 256), vm(2, 32, 256), vm(3, 4, 32, 256), vm(3, 4, 32, 256),
-            dma((9,)), dma((9,)), dma, dma, dma, dma((3,)), dma((8,)),
+            dma((9,)), dma((9,)), dma, dma, dma, dma((12,)),
         ],
-        compiler_params=pltpu.CompilerParams(has_side_effects=True, collective_id=0),
+        compiler_params=pltpu.CompilerParams(has_side_effects=True, collective_id=0, vmem_limit_bytes=40 << 20),
         name="exchange",
-    )(loads, dest.reshape(1, 4096), cell.reshape(1, 4096), sa, k, k, st, k, k, fields, areas, volume)
+    )(loads, dest.reshape(1, 4096), cell.reshape(1, 4096), fields, areas, volume, sa, st, k)
 
 
 def local(fields, volume, swept_axial, swept_angular, swept_radial, conductivity, corner_areas, parcel_loads, dest_device, dest_cell):
     chan, saz, stt, kzl, kzh, ktl, kth, grads = exchange(
         parcel_loads, dest_device, dest_cell, fields, corner_areas, volume, swept_axial, swept_angular, conductivity
     )
-    vn, src, tlo, thi, grads = deposit(
+    vn, vn2, src, tlo, thi, grads = deposit(
         chan, fields, volume, swept_axial, swept_angular, swept_radial, saz, stt, grads
     )
-    diffused = diffuse(src, tlo, thi, conductivity, vn, kzl, kzh, ktl, kth)
+    diffused = diffuse(src, tlo, thi, conductivity, vn2, kzl, kzh, ktl, kth)
     return vn, diffused, grads
 
 

time: 62 us -> 62.7 us (1.011)
  local copies, waits for them, and re-layouts: 3.36 us -> 11.1 us
  Pallas kernels: 57.8 us -> 50.5 us
    unnamed x1 -> x21, local copies, waits for them, and re-layouts: 3.36 us -> 11.1 us
    pallas_call x2, Pallas kernels: 44.8 us -> 39.9 us  [the longest x1 28.8 us: exchange(): pl.pallas_call(exchange_kernel, out_shape=[jax.ShapeDtypeStruct(s, F32) f...]
    pallas_call x1, Pallas kernels: 13 us -> 10.6 us  [diffuse(): pl.pallas_call(diffuse_kernel, out_shape=jax.ShapeDtypeStruct(cells, F32)...]
where the time goes in v5:
time: 62.7 us; the launch traced here: 62.3 us
  Pallas kernels  50.5 us (81%)
  local copies, waits for them, and re-layouts  11.1 us (18%)
  between operations  0.68 us (1%)
    pallas_call x1, Pallas kernels, exchange(): pl.pallas_call(exchange_kernel, out_shape=[jax.ShapeDtypeStruct(s, F32) f...  28.8 us
    unnamed x21, local copies, waits for them, and re-layouts  11.1 us
    pallas_call x1, Pallas kernels, deposit(): pl.pallas_call(deposit_kernel, out_shape=(sd((8, 32, 256), F32), sd((8, 3...  11 us
    pallas_call x1, Pallas kernels, diffuse(): pl.pallas_call(diffuse_kernel, out_shape=jax.ShapeDtypeStruct(cells, F32)...  10.6 us

profile of v5, /device:TPU:0, one launch (start us, length us, event | category | flops | bytes accessed | tf_op | source)
XLA Modules:
  0.0 62.3 jit_solution(222115543708047552)
XLA Ops:
  0.6 0.0 copy-start
  0.6 1.7 %copy-done = f32[9,8,32,256]{3,2,1,0:T(8,128)S(1)} copy-done((f32[9,8,32,256]{3,2,1,0:T(8,128)S(1)}, f32[9,8,32,256]{3,2,1,0:T(8,128)}, u32[]{:S(2)}) %copy-start) | copy-done | bytes 2359320
  2.3 0.0 copy-start.1
  2.3 1.9 %copy-done.1 = bf16[3,8,8,32,256]{4,3,2,1,0:T(8,128)(2,1)S(1)} copy-done((bf16[3,8,8,32,256]{4,3,2,1,0:T(8,128)(2,1)S(1)}, bf16[3,8,8,32,256]{4,3,2,1,0:T(8,128)(2,1)}, u32[]{:S(2)}) %copy-start.1) | copy-done | bytes 3145752
  4.2 0.0 copy-start.2
  4.2 0.9 %copy-done.2 = f32[8,32,256]{2,1,0:T(8,128)S(1)} copy-done((f32[8,32,256]{2,1,0:T(8,128)S(1)}, f32[8,32,256]{2,1,0:T(8,128)}, u32[]{:S(2)}) %copy-start.2) | copy-done | bytes 262168
  5.1 0.0 copy-start.3
  5.1 0.9 %copy-done.3 = f32[8,32,256]{2,1,0:T(8,128)S(1)} copy-done((f32[8,32,256]{2,1,0:T(8,128)S(1)}, f32[8,32,256]{2,1,0:T(8,128)}, u32[]{:S(2)}) %copy-start.3) | copy-done | bytes 262168
  6.1 0.0 copy-start.4
  6.1 0.9 %copy-done.4 = f32[8,32,256]{2,1,0:T(8,128)S(1)} copy-done((f32[8,32,256]{2,1,0:T(8,128)S(1)}, f32[8,32,256]{2,1,0:T(8,128)}, u32[]{:S(2)}) %copy-start.4) | copy-done | bytes 262168
  7.0 0.0 copy-start.5
  7.0 0.9 %copy-done.5 = f32[8,32,256]{2,1,0:T(8,128)S(1)} copy-done((f32[8,32,256]{2,1,0:T(8,128)S(1)}, f32[8,32,256]{2,1,0:T(8,128)}, u32[]{:S(2)}) %copy-start.5) | copy-done | bytes 262168
  8.0 0.0 copy-start.7
  8.0 0.9 %copy-done.7 = f32[9,4096]{1,0:T(8,128)S(1)} copy-done((f32[9,4096]{1,0:T(8,128)S(1)}, f32[9,4096]{1,0:T(8,128)}, u32[]{:S(2)}) %copy-start.7) | copy-done | bytes 147480
  8.9 0.0 copy-start.8
  8.9 0.7 %copy-done.8 = s32[4096,1]{0,1:T(1,128)S(1)} copy-done((s32[4096,1]{0,1:T(1,128)S(1)}, s32[4096,1]{0,1:T(1,128)}, u32[]{:S(2)}) %copy-start.8) | copy-done | bytes 16408
  9.7 0.0 copy-start.9
  9.7 0.7 %copy-done.9 = s32[4096]{0:T(1024)S(1)} copy-done((s32[4096]{0:T(1024)S(1)}, s32[4096]{0:T(1024)}, u32[]{:S(2)}) %copy-start.9) | copy-done | bytes 16408
  10.4 0.0 copy-start.6
  10.4 28.8 %exchange.1 = (f32[10,64,128]{2,1,0:T(8,128)S(1)}, f32[32,256]{1,0:T(8,128)S(1)}, f32[8,256]{1,0:T(8,128)S(1)}, f32[32,256]{1,0:T(8,128)S(1)}, f32[32,256]{1,0:T...) custom-call(f32[9,4096]{1,0:T(8,128)S(1)} %copy-done.7, ...), custom_call_target="tpu_custom_call" | custom-call | tf_op jit(solution)/shard_map/exchange/pallas_call | solution.py:460
  39.2 0.0 copy-done.6
  39.2 11.0 %deposit.1 = (f32[8,32,256]{2,1,0:T(8,128)}, f32[8,32,256]{2,1,0:T(8,128)S(1)}, f32[9,8,32,256]{3,2,1,0:T(8,128)S(1)}, f32[9,8,256]{2,1,0:T(8,128)S(1)}, f32[9,8...) custom-call(f32[10,64,128]{2,1,0:T(8,128)S(1)} %get-tuple-element.17.chan_ref, f32[9,8,32,256]{3,2,1,0:T(8,128)S(1)} %copy-done, ...), custom_call_target="tpu_custom_call" | custom-call | tf_op jit(solution)/shard_map/deposit/pallas_call | solution.py:113
  50.3 10.6 %diffuse.1 = f32[9,8,32,256]{3,2,1,0:T(8,128)S(1)} custom-call(f32[9,8,32,256]{3,2,1,0:T(8,128)S(1)} %get-tuple-element.22.src_ref, f32[9,8,256]{2,1,0:T(8,128)S(1)} %get-tuple-element.23.tlo_ref, f32[9,8,256]{2,1,0:T(8,128)S(1)} %get-tuple-element.24.thi_ref, f32[8,32,256]{2,1,0:T(8,128)S(1)} %copy-done.5, f32[8,32,256]{2,1,0:T(8,128)S(1)} %get-tuple-element.25.vn_ref, ...), custom_call_target="tpu_custom_call" | custom-call | tf_op jit(solution)/shard_map/diffuse/pallas_call | solution.py:265
  60.9 1.4 %copy.14 = f32[9,8,32,256]{3,2,1,0:T(8,128)} copy(f32[9,8,32,256]{3,2,1,0:T(8,128)S(1)} %diffuse.1) | data formatting | bytes 4718592
Async XLA Ops:
  0.6 1.7 %copy-start = (f32[9,8,32,256]{3,2,1,0:T(8,128)S(1)}, f32[9,8,32,256]{3,2,1,0:T(8,128)}, u32[]{:S(2)}) copy-start(f32[9,8,32,256]{3,2,1,0:T(8,128)} %fields_ref.1) | copy-start | bytes 7077892
  2.3 1.9 %copy-start.1 = (bf16[3,8,8,32,256]{4,3,2,1,0:T(8,128)(2,1)S(1)}, bf16[3,8,8,32,256]{4,3,2,1,0:T(8,128)(2,1)}, u32[]{:S(2)}) copy-start(bf16[3,8,8,32,256]{4,3,2,1,0:T(8,128)(2,1)} %areas_in.1) | copy-start | bytes 9437188
  4.2 0.9 %copy-start.2 = (f32[8,32,256]{2,1,0:T(8,128)S(1)}, f32[8,32,256]{2,1,0:T(8,128)}, u32[]{:S(2)}) copy-start(f32[8,32,256]{2,1,0:T(8,128)} %vol_ref.1) | copy-start | bytes 786436
  5.1 0.9 %copy-start.3 = (f32[8,32,256]{2,1,0:T(8,128)S(1)}, f32[8,32,256]{2,1,0:T(8,128)}, u32[]{:S(2)}) copy-start(f32[8,32,256]{2,1,0:T(8,128)} %sa_ref.1) | copy-start | bytes 786436
  6.1 0.9 %copy-start.4 = (f32[8,32,256]{2,1,0:T(8,128)S(1)}, f32[8,32,256]{2,1,0:T(8,128)}, u32[]{:S(2)}) copy-start(f32[8,32,256]{2,1,0:T(8,128)} %st_ref.1) | copy-start | bytes 786436
  7.0 0.9 %copy-start.5 = (f32[8,32,256]{2,1,0:T(8,128)S(1)}, f32[8,32,256]{2,1,0:T(8,128)}, u32[]{:S(2)}) copy-start(f32[8,32,256]{2,1,0:T(8,128)} %k_ref.1) | copy-start | bytes 786436
  8.0 0.9 %copy-start.7 = (f32[9,4096]{1,0:T(8,128)S(1)}, f32[9,4096]{1,0:T(8,128)}, u32[]{:S(2)}) copy-start(f32[9,4096]{1,0:T(8,128)} %loads_in.1) | copy-start | bytes 442372
  8.9 0.7 %copy-start.8 = (s32[4096,1]{0,1:T(1,128)S(1)}, s32[4096,1]{0,1:T(1,128)}, u32[]{:S(2)}) copy-start(s32[4096,1]{0,1:T(1,128)} %param.18) | copy-start | bytes 49156
  9.7 0.7 %copy-start.9 = (s32[4096]{0:T(1024)S(1)}, s32[4096]{0:T(1024)}, u32[]{:S(2)}) copy-start(s32[4096]{0:T(1024)} %param.19) | copy-start | bytes 49156
  10.4 28.8 %copy-start.6 = (f32[8,32,256]{2,1,0:T(8,128)S(1)}, f32[8,32,256]{2,1,0:T(8,128)}, u32[]{:S(2)}) copy-start(f32[8,32,256]{2,1,0:T(8,128)} %sr_ref.1) | copy-start | bytes 786436

commit v6 on v5

--- a/solution.py
+++ b/solution.py
@@ -34,17 +34,20 @@
 
 
 def deposit_kernel(
-    chan_ref, fields_ref, vol_ref, sa_ref, st_ref, sr_ref, saz_ref, stt_ref, grads_ref,
+    chan_ref, fields_ref, vol_ref, sa_ref, st_ref, sr_ref, grads_ref,
     vn_ref, vn2_ref, src_ref, tlo_ref, thi_ref, grads_out_ref,
-    sort_ref, acc_ref, rank_ref, sem,
+    sort_ref, acc_ref, rank_ref, gbuf, sems,
 ):
-    leaving = pltpu.make_async_copy(grads_ref, grads_out_ref, sem)
-    leaving.start()
+    arriving = pltpu.make_async_copy(grads_ref, gbuf, sems.at[0])
+    leaving = pltpu.make_async_copy(gbuf, grads_out_ref, sems.at[1])
+    arriving.start()
+    beneath = jnp.concatenate([chan_ref[10, 0:32], chan_ref[10, 32:64]], 1)
+    aside = jnp.concatenate([chan_ref[11, 0:8], chan_ref[11, 8:16]], 1)
     for a in range(8):
-        below = saz_ref[...] if a == 0 else sa_ref[a - 1]
+        below = beneath if a == 0 else sa_ref[a - 1]
         stp = st_ref[a]
         row = iota((32, 256), 0)
-        side = jnp.where(row == 0, stt_ref[a : a + 1], pltpu.roll(stp, 1, 0))
+        side = jnp.where(row == 0, aside[a : a + 1], pltpu.roll(stp, 1, 0))
         srp = sr_ref[a]
         lane = iota((32, 256), 1)
         inner = jnp.where(lane == 0, 0.0, pltpu.roll(srp, 1, 1))
@@ -71,6 +74,9 @@
             count = jnp.dot(g[:, b * 256 : (b + 1) * 256], earlier, preferred_element_type=F32)
             ranks.append(jnp.sum(gb * (count + carry) , axis=0, keepdims=True))
             carry = carry + jnp.sum(gb, axis=1, keepdims=True)
+        if ch == 1:
+            arriving.wait()
+            leaving.start()
         rank_ref[...] = jnp.concatenate(ranks, 1).astype(I32)
         most = jnp.max(carry).astype(I32)
         his, los = [], []
@@ -108,7 +114,7 @@
     leaving.wait()
 
 
-def deposit(chan, fields, volume, sa, st, sr, saz, stt, grads):
+def deposit(chan, fields, volume, sa, st, sr, grads):
     sd = jax.ShapeDtypeStruct
     return pl.pallas_call(
         deposit_kernel,
@@ -117,17 +123,18 @@
             sd((9, 8, 256), F32), sd((9, 8, 256), F32),
             sd((27, 8, 32, 256), F32),
         ),
-        in_specs=[VM] * 8 + [pl.BlockSpec(memory_space=pl.ANY)],
+        in_specs=[VM] * 6 + [pl.BlockSpec(memory_space=pl.ANY)],
         out_specs=[VM] * 5 + [pl.BlockSpec(memory_space=pl.ANY)],
         scratch_shapes=[
             pltpu.VMEM((320, 256), F32),
             pltpu.VMEM((9, 8, 32, 256), F32),
             pltpu.VMEM((1, CHUNK), I32),
-            pltpu.SemaphoreType.DMA,
+            pltpu.VMEM((27, 8, 32, 256), F32),
+            pltpu.SemaphoreType.DMA((2,)),
         ],
-        compiler_params=pltpu.CompilerParams(vmem_limit_bytes=24 << 20),
+        compiler_params=pltpu.CompilerParams(vmem_limit_bytes=44 << 20),
         name="deposit",
-    )(chan, fields, volume, sa, st, sr, saz, stt, grads)
+    )(chan, fields, volume, sa, st, sr, grads)
 
 
 def t_shift(x, edge):
@@ -279,11 +286,11 @@
 
 def exchange_kernel(
     loads_in, dest_in, cell_in, fields_in, areas_in, vol_in, sa_in, st_in, k_in,
-    chan_ref, saz_ref, stt_ref, kzl_ref, kzh_ref, ktl_ref, kth_ref, grads_ref,
+    chan_ref, kzl_ref, kzh_ref, ktl_ref, kth_ref, grads_ref,
     acc_ref, d_ref, rank_ref, out_buf, in_buf, azs, ts, cs, kbs, zr, tr, cr, kar, knr,
     loads_ref, dest_ref, cell_ref, sz_ref, kz_ref, kz0_ref, st_ref, kt_ref, kt0_ref,
-    fbuf, abuf, vbuf, f_ref, w_ref, a0_ref, a1_ref,
-    send_sems, recv_sems, psend_sem, precv_sem, own_sem, load_sems,
+    fbuf, abuf, vbuf, gbuf, f_ref, w_ref, a0_ref, a1_ref,
+    send_sems, recv_sems, psend_sem, precv_sem, own_sem, load_sems, store_sems,
 ):
     slab, sector = lax.axis_index("slab"), lax.axis_index("sector")
     me = slab * 4 + sector
@@ -411,6 +418,9 @@
             lambda i, q: beside(plane)(9 + 4 * i + 2 * dz + q % 2),
         )
 
+    def store(a):
+        return pltpu.make_async_copy(gbuf.at[:, a], grads_ref.at[:, a], store_sems.at[a])
+
     prepare_own(1, 7)
 
     def plane(n, unused):
@@ -419,7 +429,8 @@
         prepare_own(1 - now, a - 1)
         own_areas(a0_ref, a, 0)
         own_areas(a1_ref, a - 1, 1)
-        gradient_plane(f_ref, w_ref, a0_ref, a1_ref, now, 1 - now, grads_ref, a)
+        gradient_plane(f_ref, w_ref, a0_ref, a1_ref, now, 1 - now, gbuf, a)
+        store(a).start()
         return unused
 
     lax.fori_loop(0, 7, plane, 0)
@@ -435,11 +446,13 @@
     prepare(f_ref, w_ref, 1, lambda f: under(zr[f]), under(zr[21]), lambda c: under(cr[c : c + 1, :]))
     own_areas(a0_ref, 0, 0)
     prepare_areas(a1_ref, lambda i, q: zr[9 + 4 * i + q], lambda i, q: cr[9 + 4 * i + q : 10 + 4 * i + q, :])
-    gradient_plane(f_ref, w_ref, a0_ref, a1_ref, 0, 1, grads_ref, 0)
-    saz_ref[...] = under(zr[22])
+    gradient_plane(f_ref, w_ref, a0_ref, a1_ref, 0, 1, gbuf, 0)
+    store(0).start()
+    for h in range(2):
+        chan_ref[10, 32 * h : 32 * h + 32] = under(zr[22, :, 128 * h : 128 * h + 128])
+        chan_ref[11, 8 * h : 8 * h + 8] = tr[22, :, 128 * h : 128 * h + 128]
     kzl_ref[...] = under(zr[23])
     kzh_ref[...] = jnp.where(slab < 31, kar[...], 0.0)
-    stt_ref[...] = tr[22]
     ktl_ref[...] = tr[23]
     kth_ref[...] = knr[...]
     most = pl.ds(0, 127)
@@ -450,39 +463,41 @@
         first, second = in_buf[0:64, s, :], in_buf[64:128, s, :]
         chan_ref[2 * s] = jnp.where(lane, first, pltpu.roll(second, 64, 1))
         chan_ref[2 * s + 1] = jnp.where(lane, pltpu.roll(first, 64, 1), second)
+    for a in range(8):
+        store(a).wait()
 
 
 def exchange(loads, dest, cell, fields, areas, volume, sa, st, k):
     hbm = pl.BlockSpec(memory_space=pltpu.HBM)
-    shapes = [(10, 64, 128), (32, 256), (8, 256), (32, 256), (32, 256), (8, 256), (8, 256), (27, 8, 32, 256)]
+    shapes = [(12, 64, 128), (32, 256), (32, 256), (8, 256), (8, 256), (27, 8, 32, 256)]
     dma = pltpu.SemaphoreType.DMA
     vm = lambda *shape, t=F32: pltpu.VMEM(shape, t)
     return pl.pallas_call(
         exchange_kernel,
         out_shape=[jax.ShapeDtypeStruct(s, F32) for s in shapes],
         in_specs=[hbm] * 9,
-        out_specs=[VM] * 8,
+        out_specs=[VM] * 5 + [hbm],
         scratch_shapes=[
             vm(320, 256), vm(2048, 256, t=BF16), vm(1, 4096, t=I32), vm(128, 5, 128), vm(128, 5, 128),
             vm(12, 32, 256), vm(24, 8, 256), vm(24, 256), vm(8, 256),
             vm(24, 32, 256), vm(24, 8, 256), vm(24, 256), vm(32, 256), vm(8, 256),
             vm(9, 4096), vm(1, 4096, t=I32), vm(1, 4096, t=I32), vm(32, 256), vm(32, 256), vm(32, 256),
             vm(8, 8, 256), vm(8, 8, 256), vm(8, 8, 256),
-            vm(9, 8, 32, 256), vm(3, 8, 8, 32, 256, t=BF16), vm(8, 32, 256),
+            vm(9, 8, 32, 256), vm(3, 8, 8, 32, 256, t=BF16), vm(8, 32, 256), vm(27, 8, 32, 256),
             vm(2, 4, 9, 32, 256), vm(2, 32, 256), vm(3, 4, 32, 256), vm(3, 4, 32, 256),
-            dma((9,)), dma((9,)), dma, dma, dma, dma((12,)),
+            dma((9,)), dma((9,)), dma, dma, dma, dma((12,)), dma((8,)),
         ],
-        compiler_params=pltpu.CompilerParams(has_side_effects=True, collective_id=0, vmem_limit_bytes=40 << 20),
+        compiler_params=pltpu.CompilerParams(has_side_effects=True, collective_id=0, vmem_limit_bytes=56 << 20),
         name="exchange",
     )(loads, dest.reshape(1, 4096), cell.reshape(1, 4096), fields, areas, volume, sa, st, k)
 
 
 def local(fields, volume, swept_axial, swept_angular, swept_radial, conductivity, corner_areas, parcel_loads, dest_device, dest_cell):
-    chan, saz, stt, kzl, kzh, ktl, kth, grads = exchange(
+    chan, kzl, kzh, ktl, kth, grads = exchange(
         parcel_loads, dest_device, dest_cell, fields, corner_areas, volume, swept_axial, swept_angular, conductivity
     )
     vn, vn2, src, tlo, thi, grads = deposit(
-        chan, fields, volume, swept_axial, swept_angular, swept_radial, saz, stt, grads
+        chan, fields, volume, swept_axial, swept_angular, swept_radial, grads
     )
     diffused = diffuse(src, tlo, thi, conductivity, vn2, kzl, kzh, ktl, kth)
     return vn, diffused, grads

time: 62.7 us -> 55.4 us (0.88)
  local copies, waits for them, and re-layouts: 11.1 us -> 2.44 us
  Pallas kernels: 50.5 us -> 52 us
    unnamed x21 -> x23, local copies, waits for them, and re-layouts: 11.1 us -> 2.44 us
    pallas_call x1, Pallas kernels: 28.8 us -> 29.9 us  [exchange(): pl.pallas_call(exchange_kernel, out_shape=[jax.ShapeDtypeStruct(s, F32) f...]
where the time goes in v6:
time: 55.4 us; the launch traced here: 55.2 us
  Pallas kernels  52 us (94%)
  local copies, waits for them, and re-layouts  2.44 us (4%)
  between operations  0.8 us (1%)
    pallas_call x1, Pallas kernels, exchange(): pl.pallas_call(exchange_kernel, out_shape=[jax.ShapeDtypeStruct(s, F32) f...  29.9 us
    pallas_call x1, Pallas kernels, deposit(): pl.pallas_call(deposit_kernel, out_shape=(sd((8, 32, 256), F32), sd((8, 3...  11.5 us
    pallas_call x1, Pallas kernels, diffuse(): pl.pallas_call(diffuse_kernel, out_shape=jax.ShapeDtypeStruct(cells, F32)...  10.6 us
    unnamed x23, local copies, waits for them, and re-layouts  2.44 us

profile of v6, /device:TPU:0, one launch (start us, length us, event | category | flops | bytes accessed | tf_op | source)
XLA Modules:
  0.0 55.2 jit_solution(12093671850175184897)
XLA Ops:
  0.6 0.0 copy-start
  0.6 0.0 copy-start.1
  0.7 0.0 copy-start.2
  0.7 0.0 copy-start.3
  0.7 0.0 copy-start.6
  0.7 29.9 %exchange.1 = (f32[12,64,128]{2,1,0:T(8,128)}, f32[32,256]{1,0:T(8,128)}, f32[32,256]{1,0:T(8,128)}, f32[8,256]{1,0:T(8,128)}, f32[8,256]{1,0:T(8,128)}, /*index=5*/f32[27,8,32,256]{3,2,1,0:T(8,128)}) custom-call(f32[9,4096]{1,0:T(8,128)} %loads_in.1, s32[1,4096]{1,0:T(1,128)} %bitcast.2, s32[1,4096]{1,0:T(1,128)} %bitcast.3, f32[9,8,32,256]{3,2,1,0:T(8,128)} %fields_ref.1, ...), custom_call_target="tpu_custom_call" | custom-call | tf_op jit(solution)/shard_map/exchange/pallas_call | solution.py:475
  30.6 0.0 copy-done
  30.6 0.0 copy-done.1
  30.6 0.0 copy-done.2
  30.6 0.0 copy-done.3
  30.6 0.0 copy-done.6
  30.6 0.0 copy-start.5
  30.7 1.0 %copy-done.5 = f32[12,64,128]{2,1,0:T(8,128)S(1)} copy-done((f32[12,64,128]{2,1,0:T(8,128)S(1)}, f32[12,64,128]{2,1,0:T(8,128)}, u32[]{:S(2)}) %copy-start.5) | copy-done | bytes 393240
  31.6 0.0 copy-start.4
  31.6 0.0 copy-start.7
  31.7 0.0 copy-start.10
  31.7 11.5 %deposit.1 = (f32[8,32,256]{2,1,0:T(8,128)}, f32[8,32,256]{2,1,0:T(8,128)S(1)}, f32[9,8,32,256]{3,2,1,0:T(8,128)S(1)}, f32[9,8,256]{2,1,0:T(8,128)S(1)}, f32[9,8...) custom-call(f32[12,64,128]{2,1,0:T(8,128)S(1)} %copy-done.5, f32[9,8,32,256]{3,2,1,0:T(8,128)S(1)} %copy-done, ...), custom_call_target="tpu_custom_call" | custom-call | tf_op jit(solution)/shard_map/deposit/pallas_call | solution.py:119
  43.2 0.0 copy-done.4
  43.2 0.0 copy-done.7
  43.2 0.0 copy-done.8
  43.2 0.0 copy-done.9
  43.2 0.0 copy-done.10
  43.2 10.6 %diffuse.1 = f32[9,8,32,256]{3,2,1,0:T(8,128)S(1)} custom-call(f32[9,8,32,256]{3,2,1,0:T(8,128)S(1)} %get-tuple-element.18.src_ref, f32[9,8,256]{2,1,0:T(8,128)S(1)} %get-tuple-element.19.tlo_ref, f32[9,8,256]{2,1,0:T(8,128)S(1)} %get-tuple-element.20.thi_ref, f32[8,32,256]{2,1,0:T(8,128)S(1)} %copy-done.4, f32[8,32,256]{2,1,0:T(8,128)S(1)} %get-tuple-element.21.vn_ref, ...), custom_call_target="tpu_custom_call" | custom-call | tf_op jit(solution)/shard_map/diffuse/pallas_call | solution.py:272
  53.8 1.4 %copy.14 = f32[9,8,32,256]{3,2,1,0:T(8,128)} copy(f32[9,8,32,256]{3,2,1,0:T(8,128)S(1)} %diffuse.1) | data formatting | bytes 4718592
  (2 shorter events, 0.0 us)
Async XLA Ops:
  0.6 30.0 %copy-start = (f32[9,8,32,256]{3,2,1,0:T(8,128)S(1)}, f32[9,8,32,256]{3,2,1,0:T(8,128)}, u32[]{:S(2)}) copy-start(f32[9,8,32,256]{3,2,1,0:T(8,128)} %fields_ref.1) | copy-start | bytes 7077892
  0.6 30.0 %copy-start.1 = (f32[8,32,256]{2,1,0:T(8,128)S(1)}, f32[8,32,256]{2,1,0:T(8,128)}, u32[]{:S(2)}) copy-start(f32[8,32,256]{2,1,0:T(8,128)} %vol_ref.1) | copy-start | bytes 786436
  0.7 30.0 %copy-start.2 = (f32[8,32,256]{2,1,0:T(8,128)S(1)}, f32[8,32,256]{2,1,0:T(8,128)}, u32[]{:S(2)}) copy-start(f32[8,32,256]{2,1,0:T(8,128)} %sa_ref.1) | copy-start | bytes 786436
  0.7 30.0 %copy-start.3 = (f32[8,32,256]{2,1,0:T(8,128)S(1)}, f32[8,32,256]{2,1,0:T(8,128)}, u32[]{:S(2)}) copy-start(f32[8,32,256]{2,1,0:T(8,128)} %st_ref.1) | copy-start | bytes 786436
  0.7 30.0 %copy-start.6 = (f32[8,32,256]{2,1,0:T(8,128)S(1)}, f32[8,32,256]{2,1,0:T(8,128)}, u32[]{:S(2)}) copy-start(f32[8,32,256]{2,1,0:T(8,128)} %sr_ref.1) | copy-start | bytes 786436
  30.6 1.0 %copy-start.5 = (f32[12,64,128]{2,1,0:T(8,128)S(1)}, f32[12,64,128]{2,1,0:T(8,128)}, u32[]{:S(2)}) copy-start(f32[12,64,128]{2,1,0:T(8,128)} %get-tuple-element.15.chan_ref) | copy-start | bytes 1179652
  31.6 11.5 %copy-start.4 = (f32[8,32,256]{2,1,0:T(8,128)S(1)}, f32[8,32,256]{2,1,0:T(8,128)}, u32[]{:S(2)}) copy-start(f32[8,32,256]{2,1,0:T(8,128)} %k_ref.1) | copy-start | bytes 786436
  31.6 11.5 %copy-start.7 = (f32[32,256]{1,0:T(8,128)S(1)}, f32[32,256]{1,0:T(8,128)}, u32[]{:S(2)}) copy-start(f32[32,256]{1,0:T(8,128)} %get-tuple-element.22.kzl_ref) | copy-start | bytes 98308
  31.6 11.5 %copy-start.8 = (f32[32,256]{1,0:T(8,128)S(1)}, f32[32,256]{1,0:T(8,128)}, u32[]{:S(2)}) copy-start(f32[32,256]{1,0:T(8,128)} %get-tuple-element.23.kzh_ref) | copy-start | bytes 98308
  31.6 11.5 %copy-start.9 = (f32[8,256]{1,0:T(8,128)S(1)}, f32[8,256]{1,0:T(8,128)}, u32[]{:S(2)}) copy-start(f32[8,256]{1,0:T(8,128)} %get-tuple-element.24.ktl_ref) | copy-start | bytes 24580
  31.7 11.6 %copy-start.10 = (f32[8,256]{1,0:T(8,128)S(1)}, f32[8,256]{1,0:T(8,128)}, u32[]{:S(2)}) copy-start(f32[8,256]{1,0:T(8,128)} %get-tuple-element.25.kth_ref) | copy-start | bytes 24580

commit v7 on v6

--- a/solution.py
+++ b/solution.py
@@ -30,7 +30,7 @@
     return jnp.where(iota((n, n), 0) < iota((n, n), 1), 1.0, 0.0).astype(BF16)
 
 
-GROUPS, ROWS, SLOTS, CHUNK = 16, 16, 256, 2048
+GROUPS, ROWS, SLOTS, CHUNK = 16, 16, 384, 4096
 
 
 def deposit_kernel(
@@ -126,7 +126,7 @@
         in_specs=[VM] * 6 + [pl.BlockSpec(memory_space=pl.ANY)],
         out_specs=[VM] * 5 + [pl.BlockSpec(memory_space=pl.ANY)],
         scratch_shapes=[
-            pltpu.VMEM((320, 256), F32),
+            pltpu.VMEM((20 * GROUPS, SLOTS), F32),
             pltpu.VMEM((9, 8, 32, 256), F32),
             pltpu.VMEM((1, CHUNK), I32),
             pltpu.VMEM((27, 8, 32, 256), F32),
@@ -434,20 +434,15 @@
         return unused
 
     lax.fori_loop(0, 7, plane, 0)
-    own.wait()
-    for n, copy in enumerate(copies):
-        if n != 4:
-            copy.wait()
+    own_areas(a0_ref, 0, 0)
     inside = slab > 0
 
     def under(x):
         return jnp.where(inside, x, 0.0)
 
-    prepare(f_ref, w_ref, 1, lambda f: under(zr[f]), under(zr[21]), lambda c: under(cr[c : c + 1, :]))
-    own_areas(a0_ref, 0, 0)
-    prepare_areas(a1_ref, lambda i, q: zr[9 + 4 * i + q], lambda i, q: cr[9 + 4 * i + q : 10 + 4 * i + q, :])
-    gradient_plane(f_ref, w_ref, a0_ref, a1_ref, 0, 1, gbuf, 0)
-    store(0).start()
+    own.wait()
+    for n in (0, 1, 2, 3, 5):
+        copies[n].wait()
     for h in range(2):
         chan_ref[10, 32 * h : 32 * h + 32] = under(zr[22, :, 128 * h : 128 * h + 128])
         chan_ref[11, 8 * h : 8 * h + 8] = tr[22, :, 128 * h : 128 * h + 128]
@@ -463,6 +458,12 @@
         first, second = in_buf[0:64, s, :], in_buf[64:128, s, :]
         chan_ref[2 * s] = jnp.where(lane, first, pltpu.roll(second, 64, 1))
         chan_ref[2 * s + 1] = jnp.where(lane, pltpu.roll(first, 64, 1), second)
+    for n in (6, 7, 8):
+        copies[n].wait()
+    prepare(f_ref, w_ref, 1, lambda f: under(zr[f]), under(zr[21]), lambda c: under(cr[c : c + 1, :]))
+    prepare_areas(a1_ref, lambda i, q: zr[9 + 4 * i + q], lambda i, q: cr[9 + 4 * i + q : 10 + 4 * i + q, :])
+    gradient_plane(f_ref, w_ref, a0_ref, a1_ref, 0, 1, gbuf, 0)
+    store(0).start()
     for a in range(8):
         store(a).wait()
 

time: 55.4 us -> 53.6 us (0.968)
  Pallas kernels: 52 us -> 50.2 us
    pallas_call x1, Pallas kernels: 11.5 us -> 8.88 us  [deposit(): pl.pallas_call(deposit_kernel, out_shape=(sd((8, 32, 256), F32), sd((8, 3...]
    pallas_call x1, Pallas kernels: 29.9 us -> 30.7 us  [exchange(): pl.pallas_call(exchange_kernel, out_shape=[jax.ShapeDtypeStruct(s, F32) f...]
where the time goes in v7:
time: 53.6 us; the launch traced here: 53.4 us
  Pallas kernels  50.2 us (94%)
  local copies, waits for them, and re-layouts  2.44 us (5%)
  between operations  0.8 us (1%)
    pallas_call x1, Pallas kernels, exchange(): pl.pallas_call(exchange_kernel, out_shape=[jax.ShapeDtypeStruct(s, F32) f...  30.7 us
    pallas_call x1, Pallas kernels, diffuse(): pl.pallas_call(diffuse_kernel, out_shape=jax.ShapeDtypeStruct(cells, F32)...  10.6 us
    pallas_call x1, Pallas kernels, deposit(): pl.pallas_call(deposit_kernel, out_shape=(sd((8, 32, 256), F32), sd((8, 3...  8.88 us
    unnamed x23, local copies, waits for them, and re-layouts  2.44 us

profile of v7, /device:TPU:0, one launch (start us, length us, event | category | flops | bytes accessed | tf_op | source)
XLA Modules:
  0.0 53.4 jit_solution(9621747277843272840)
XLA Ops:
  0.6 0.0 copy-start
  0.6 0.0 copy-start.1
  0.7 0.0 copy-start.2
  0.7 0.0 copy-start.3
  0.7 0.0 copy-start.6
  0.7 30.7 %exchange.1 = (f32[12,64,128]{2,1,0:T(8,128)}, f32[32,256]{1,0:T(8,128)}, f32[32,256]{1,0:T(8,128)}, f32[8,256]{1,0:T(8,128)}, f32[8,256]{1,0:T(8,128)}, /*index=5*/f32[27,8,32,256]{3,2,1,0:T(8,128)}) custom-call(f32[9,4096]{1,0:T(8,128)} %loads_in.1, s32[1,4096]{1,0:T(1,128)} %bitcast.2, s32[1,4096]{1,0:T(1,128)} %bitcast.3, f32[9,8,32,256]{3,2,1,0:T(8,128)} %fields_ref.1, ...), custom_call_target="tpu_custom_call" | custom-call | tf_op jit(solution)/shard_map/exchange/pallas_call | solution.py:476
  31.4 0.0 copy-done
  31.4 0.0 copy-done.1
  31.4 0.0 copy-done.2
  31.4 0.0 copy-done.3
  31.4 0.0 copy-done.6
  31.4 0.0 copy-start.5
  31.4 1.0 %copy-done.5 = f32[12,64,128]{2,1,0:T(8,128)S(1)} copy-done((f32[12,64,128]{2,1,0:T(8,128)S(1)}, f32[12,64,128]{2,1,0:T(8,128)}, u32[]{:S(2)}) %copy-start.5) | copy-done | bytes 393240
  32.4 0.0 copy-start.4
  32.4 0.0 copy-start.7
  32.4 0.0 copy-start.10
  32.5 8.9 %deposit.1 = (f32[8,32,256]{2,1,0:T(8,128)}, f32[8,32,256]{2,1,0:T(8,128)S(1)}, f32[9,8,32,256]{3,2,1,0:T(8,128)S(1)}, f32[9,8,256]{2,1,0:T(8,128)S(1)}, f32[9,8...) custom-call(f32[12,64,128]{2,1,0:T(8,128)S(1)} %copy-done.5, f32[9,8,32,256]{3,2,1,0:T(8,128)S(1)} %copy-done, ...), custom_call_target="tpu_custom_call" | custom-call | tf_op jit(solution)/shard_map/deposit/pallas_call | solution.py:119
  41.3 0.0 copy-done.4
  41.4 0.0 copy-done.7
  41.4 0.0 copy-done.8
  41.4 0.0 copy-done.9
  41.4 0.0 copy-done.10
  41.4 10.6 %diffuse.1 = f32[9,8,32,256]{3,2,1,0:T(8,128)S(1)} custom-call(f32[9,8,32,256]{3,2,1,0:T(8,128)S(1)} %get-tuple-element.18.src_ref, f32[9,8,256]{2,1,0:T(8,128)S(1)} %get-tuple-element.19.tlo_ref, f32[9,8,256]{2,1,0:T(8,128)S(1)} %get-tuple-element.20.thi_ref, f32[8,32,256]{2,1,0:T(8,128)S(1)} %copy-done.4, f32[8,32,256]{2,1,0:T(8,128)S(1)} %get-tuple-element.21.vn_ref, ...), custom_call_target="tpu_custom_call" | custom-call | tf_op jit(solution)/shard_map/diffuse/pallas_call | solution.py:272
  52.0 1.4 %copy.14 = f32[9,8,32,256]{3,2,1,0:T(8,128)} copy(f32[9,8,32,256]{3,2,1,0:T(8,128)S(1)} %diffuse.1) | data formatting | bytes 4718592
  (2 shorter events, 0.0 us)
Async XLA Ops:
  0.6 30.8 %copy-start = (f32[9,8,32,256]{3,2,1,0:T(8,128)S(1)}, f32[9,8,32,256]{3,2,1,0:T(8,128)}, u32[]{:S(2)}) copy-start(f32[9,8,32,256]{3,2,1,0:T(8,128)} %fields_ref.1) | copy-start | bytes 7077892
  0.6 30.8 %copy-start.1 = (f32[8,32,256]{2,1,0:T(8,128)S(1)}, f32[8,32,256]{2,1,0:T(8,128)}, u32[]{:S(2)}) copy-start(f32[8,32,256]{2,1,0:T(8,128)} %vol_ref.1) | copy-start | bytes 786436
  0.7 30.8 %copy-start.2 = (f32[8,32,256]{2,1,0:T(8,128)S(1)}, f32[8,32,256]{2,1,0:T(8,128)}, u32[]{:S(2)}) copy-start(f32[8,32,256]{2,1,0:T(8,128)} %sa_ref.1) | copy-start | bytes 786436
  0.7 30.8 %copy-start.3 = (f32[8,32,256]{2,1,0:T(8,128)S(1)}, f32[8,32,256]{2,1,0:T(8,128)}, u32[]{:S(2)}) copy-start(f32[8,32,256]{2,1,0:T(8,128)} %st_ref.1) | copy-start | bytes 786436
  0.7 30.8 %copy-start.6 = (f32[8,32,256]{2,1,0:T(8,128)S(1)}, f32[8,32,256]{2,1,0:T(8,128)}, u32[]{:S(2)}) copy-start(f32[8,32,256]{2,1,0:T(8,128)} %sr_ref.1) | copy-start | bytes 786436
  31.4 1.0 %copy-start.5 = (f32[12,64,128]{2,1,0:T(8,128)S(1)}, f32[12,64,128]{2,1,0:T(8,128)}, u32[]{:S(2)}) copy-start(f32[12,64,128]{2,1,0:T(8,128)} %get-tuple-element.15.chan_ref) | copy-start | bytes 1179652
  32.4 8.9 %copy-start.4 = (f32[8,32,256]{2,1,0:T(8,128)S(1)}, f32[8,32,256]{2,1,0:T(8,128)}, u32[]{:S(2)}) copy-start(f32[8,32,256]{2,1,0:T(8,128)} %k_ref.1) | copy-start | bytes 786436
  32.4 8.9 %copy-start.7 = (f32[32,256]{1,0:T(8,128)S(1)}, f32[32,256]{1,0:T(8,128)}, u32[]{:S(2)}) copy-start(f32[32,256]{1,0:T(8,128)} %get-tuple-element.22.kzl_ref) | copy-start | bytes 98308
  32.4 8.9 %copy-start.8 = (f32[32,256]{1,0:T(8,128)S(1)}, f32[32,256]{1,0:T(8,128)}, u32[]{:S(2)}) copy-start(f32[32,256]{1,0:T(8,128)} %get-tuple-element.23.kzh_ref) | copy-start | bytes 98308
  32.4 8.9 %copy-start.9 = (f32[8,256]{1,0:T(8,128)S(1)}, f32[8,256]{1,0:T(8,128)}, u32[]{:S(2)}) copy-start(f32[8,256]{1,0:T(8,128)} %get-tuple-element.24.ktl_ref) | copy-start | bytes 24580
  32.4 8.9 %copy-start.10 = (f32[8,256]{1,0:T(8,128)S(1)}, f32[8,256]{1,0:T(8,128)}, u32[]{:S(2)}) copy-start(f32[8,256]{1,0:T(8,128)} %get-tuple-element.25.kth_ref) | copy-start | bytes 24580

commit v8 on v7

--- a/solution.py
+++ b/solution.py
@@ -168,7 +168,7 @@
             a_ref[i, q] = x if q % 2 == 1 else pltpu.roll(x, 255, 1)
 
 
-def gradient_plane(f_ref, w_ref, a0_ref, a1_ref, now, prev, out_ref, a):
+def gradient_plane(f_ref, w_ref, a0_ref, a1_ref, now, prev, out_ref, a, first=0, last=12):
     def part(n, unused):
         i = lax.rem(n, 3)
         rows = pl.ds(pl.multiple_of(n // 3 * 8, 8), 8)
@@ -184,7 +184,7 @@
             out_ref[9 * i + f, a, rows] = acc[f] * inv
         return unused
 
-    lax.fori_loop(0, 12, part, 0)
+    lax.fori_loop(first, last, part, 0)
 
 
 def diffuse_kernel(
@@ -389,6 +389,12 @@
             [acc_ref[c * 32 : (c + 1) * 32, h * 128 : (h + 1) * 128] for c in (2 * s, 2 * s + 1) for h in range(2)], 0
         )
         out_buf[:, s, :] = block.T
+    nothing = jnp.zeros((1, 256), F32)
+    for slot, a in ((1, 7), (0, 6)):
+        prepare(f_ref, w_ref, slot, lambda f: fbuf[f, a], vbuf[a], lambda c: nothing)
+    prepare_areas(a0_ref, lambda i, q: abuf[i, q, 7].astype(F32), lambda i, q: nothing)
+    prepare_areas(a1_ref, lambda i, q: abuf[i, 4 + q, 6].astype(F32), lambda i, q: nothing)
+    gradient_plane(f_ref, w_ref, a0_ref, a1_ref, 1, 0, gbuf, 7, 3, 12)
     pl.semaphore_wait(barrier, 127)
     for copy in copies:
         copy.start()
@@ -421,7 +427,20 @@
     def store(a):
         return pltpu.make_async_copy(gbuf.at[:, a], grads_ref.at[:, a], store_sems.at[a])
 
-    prepare_own(1, 7)
+    for slot, a in ((1, 7), (0, 6)):
+        for f in range(9):
+            x = tr[f, a : a + 1, :]
+            f_ref[slot, 2, f, 0:1, :] = r_shift(x)
+            f_ref[slot, 3, f, 0:1, :] = x
+        v = vbuf[a, 0:1, :] * 0.125 + tr[21, a : a + 1, :] * 0.125
+        w_ref[slot, 0:1, :] = v + r_shift(v)
+    for ref, a, dz in ((a0_ref, 7, 0), (a1_ref, 6, 1)):
+        for i in range(3):
+            for q in (2, 3):
+                x = tr[9 + 4 * i + 2 * dz + q % 2, a : a + 1, :]
+                ref[i, q, 0:1, :] = x if q == 3 else pltpu.roll(x, 255, 1)
+    gradient_plane(f_ref, w_ref, a0_ref, a1_ref, 1, 0, gbuf, 7, 0, 3)
+    store(7).start()
 
     def plane(n, unused):
         a = 7 - n
@@ -433,7 +452,7 @@
         store(a).start()
         return unused
 
-    lax.fori_loop(0, 7, plane, 0)
+    lax.fori_loop(1, 7, plane, 0)
     own_areas(a0_ref, 0, 0)
     inside = slab > 0
 

time: 53.6 us -> 53.7 us (level)
  no operation moved by 1% of the time
where the time goes in v8:
time: 53.7 us; the launch traced here: 53.6 us
  Pallas kernels  50.3 us (94%)
  local copies, waits for them, and re-layouts  2.44 us (5%)
  between operations  0.8 us (1%)
    pallas_call x1, Pallas kernels, exchange(): pl.pallas_call(exchange_kernel, out_shape=[jax.ShapeDtypeStruct(s, F32) f...  30.9 us
    pallas_call x1, Pallas kernels, diffuse(): pl.pallas_call(diffuse_kernel, out_shape=jax.ShapeDtypeStruct(cells, F32)...  10.6 us
    pallas_call x1, Pallas kernels, deposit(): pl.pallas_call(deposit_kernel, out_shape=(sd((8, 32, 256), F32), sd((8, 3...  8.88 us
    unnamed x23, local copies, waits for them, and re-layouts  2.44 us

profile of v8, /device:TPU:0, one launch (start us, length us, event | category | flops | bytes accessed | tf_op | source)
XLA Modules:
  0.0 53.6 jit_solution(1933497793395595152)
XLA Ops:
  0.6 0.0 copy-start
  0.6 0.0 copy-start.1
  0.7 0.0 copy-start.2
  0.7 0.0 copy-start.3
  0.7 0.0 copy-start.6
  0.7 30.9 %exchange.1 = (f32[12,64,128]{2,1,0:T(8,128)}, f32[32,256]{1,0:T(8,128)}, f32[32,256]{1,0:T(8,128)}, f32[8,256]{1,0:T(8,128)}, f32[8,256]{1,0:T(8,128)}, /*index=5*/f32[27,8,32,256]{3,2,1,0:T(8,128)}) custom-call(f32[9,4096]{1,0:T(8,128)} %loads_in.1, s32[1,4096]{1,0:T(1,128)} %bitcast.2, s32[1,4096]{1,0:T(1,128)} %bitcast.3, f32[9,8,32,256]{3,2,1,0:T(8,128)} %fields_ref.1, ...), custom_call_target="tpu_custom_call" | custom-call | tf_op jit(solution)/shard_map/exchange/pallas_call | solution.py:495
  31.5 0.0 copy-done
  31.6 0.0 copy-done.1
  31.6 0.0 copy-done.2
  31.6 0.0 copy-done.3
  31.6 0.0 copy-done.6
  31.6 0.0 copy-start.5
  31.6 1.0 %copy-done.5 = f32[12,64,128]{2,1,0:T(8,128)S(1)} copy-done((f32[12,64,128]{2,1,0:T(8,128)S(1)}, f32[12,64,128]{2,1,0:T(8,128)}, u32[]{:S(2)}) %copy-start.5) | copy-done | bytes 393240
  32.6 0.0 copy-start.4
  32.6 0.0 copy-start.7
  32.6 0.0 copy-start.10
  32.6 8.9 %deposit.1 = (f32[8,32,256]{2,1,0:T(8,128)}, f32[8,32,256]{2,1,0:T(8,128)S(1)}, f32[9,8,32,256]{3,2,1,0:T(8,128)S(1)}, f32[9,8,256]{2,1,0:T(8,128)S(1)}, f32[9,8...) custom-call(f32[12,64,128]{2,1,0:T(8,128)S(1)} %copy-done.5, f32[9,8,32,256]{3,2,1,0:T(8,128)S(1)} %copy-done, ...), custom_call_target="tpu_custom_call" | custom-call | tf_op jit(solution)/shard_map/deposit/pallas_call | solution.py:119
  41.5 0.0 copy-done.4
  41.5 0.0 copy-done.7
  41.5 0.0 copy-done.8
  41.5 0.0 copy-done.9
  41.5 0.0 copy-done.10
  41.6 10.6 %diffuse.1 = f32[9,8,32,256]{3,2,1,0:T(8,128)S(1)} custom-call(f32[9,8,32,256]{3,2,1,0:T(8,128)S(1)} %get-tuple-element.18.src_ref, f32[9,8,256]{2,1,0:T(8,128)S(1)} %get-tuple-element.19.tlo_ref, f32[9,8,256]{2,1,0:T(8,128)S(1)} %get-tuple-element.20.thi_ref, f32[8,32,256]{2,1,0:T(8,128)S(1)} %copy-done.4, f32[8,32,256]{2,1,0:T(8,128)S(1)} %get-tuple-element.21.vn_ref, ...), custom_call_target="tpu_custom_call" | custom-call | tf_op jit(solution)/shard_map/diffuse/pallas_call | solution.py:272
  52.2 1.4 %copy.14 = f32[9,8,32,256]{3,2,1,0:T(8,128)} copy(f32[9,8,32,256]{3,2,1,0:T(8,128)S(1)} %diffuse.1) | data formatting | bytes 4718592
  (2 shorter events, 0.0 us)
Async XLA Ops:
  0.6 30.9 %copy-start = (f32[9,8,32,256]{3,2,1,0:T(8,128)S(1)}, f32[9,8,32,256]{3,2,1,0:T(8,128)}, u32[]{:S(2)}) copy-start(f32[9,8,32,256]{3,2,1,0:T(8,128)} %fields_ref.1) | copy-start | bytes 7077892
  0.6 30.9 %copy-start.1 = (f32[8,32,256]{2,1,0:T(8,128)S(1)}, f32[8,32,256]{2,1,0:T(8,128)}, u32[]{:S(2)}) copy-start(f32[8,32,256]{2,1,0:T(8,128)} %vol_ref.1) | copy-start | bytes 786436
  0.7 30.9 %copy-start.2 = (f32[8,32,256]{2,1,0:T(8,128)S(1)}, f32[8,32,256]{2,1,0:T(8,128)}, u32[]{:S(2)}) copy-start(f32[8,32,256]{2,1,0:T(8,128)} %sa_ref.1) | copy-start | bytes 786436
  0.7 30.9 %copy-start.3 = (f32[8,32,256]{2,1,0:T(8,128)S(1)}, f32[8,32,256]{2,1,0:T(8,128)}, u32[]{:S(2)}) copy-start(f32[8,32,256]{2,1,0:T(8,128)} %st_ref.1) | copy-start | bytes 786436
  0.7 30.9 %copy-start.6 = (f32[8,32,256]{2,1,0:T(8,128)S(1)}, f32[8,32,256]{2,1,0:T(8,128)}, u32[]{:S(2)}) copy-start(f32[8,32,256]{2,1,0:T(8,128)} %sr_ref.1) | copy-start | bytes 786436
  31.6 1.0 %copy-start.5 = (f32[12,64,128]{2,1,0:T(8,128)S(1)}, f32[12,64,128]{2,1,0:T(8,128)}, u32[]{:S(2)}) copy-start(f32[12,64,128]{2,1,0:T(8,128)} %get-tuple-element.15.chan_ref) | copy-start | bytes 1179652
  32.6 8.9 %copy-start.4 = (f32[8,32,256]{2,1,0:T(8,128)S(1)}, f32[8,32,256]{2,1,0:T(8,128)}, u32[]{:S(2)}) copy-start(f32[8,32,256]{2,1,0:T(8,128)} %k_ref.1) | copy-start | bytes 786436
  32.6 8.9 %copy-start.7 = (f32[32,256]{1,0:T(8,128)S(1)}, f32[32,256]{1,0:T(8,128)}, u32[]{:S(2)}) copy-start(f32[32,256]{1,0:T(8,128)} %get-tuple-element.22.kzl_ref) | copy-start | bytes 98308
  32.6 8.9 %copy-start.8 = (f32[32,256]{1,0:T(8,128)S(1)}, f32[32,256]{1,0:T(8,128)}, u32[]{:S(2)}) copy-start(f32[32,256]{1,0:T(8,128)} %get-tuple-element.23.kzh_ref) | copy-start | bytes 98308
  32.6 8.9 %copy-start.9 = (f32[8,256]{1,0:T(8,128)S(1)}, f32[8,256]{1,0:T(8,128)}, u32[]{:S(2)}) copy-start(f32[8,256]{1,0:T(8,128)} %get-tuple-element.24.ktl_ref) | copy-start | bytes 24580
  32.6 8.9 %copy-start.10 = (f32[8,256]{1,0:T(8,128)S(1)}, f32[8,256]{1,0:T(8,128)}, u32[]{:S(2)}) copy-start(f32[8,256]{1,0:T(8,128)} %get-tuple-element.25.kth_ref) | copy-start | bytes 24580

commit v9 on v7

--- a/solution.py
+++ b/solution.py
@@ -370,6 +370,9 @@
         )
         for n, (s, t, to) in enumerate(halo)
     ]
+    pl.semaphore_wait(barrier, 127)
+    for copy in copies:
+        copy.start()
     acc_ref[...] = jnp.zeros_like(acc_ref)
     part = 512
     for b in range(4096 // part):
@@ -389,9 +392,6 @@
             [acc_ref[c * 32 : (c + 1) * 32, h * 128 : (h + 1) * 128] for c in (2 * s, 2 * s + 1) for h in range(2)], 0
         )
         out_buf[:, s, :] = block.T
-    pl.semaphore_wait(barrier, 127)
-    for copy in copies:
-        copy.start()
     own = pltpu.make_async_copy(out_buf.at[me], in_buf.at[me], own_sem)
     own.start()
 

time: 53.6 us -> 54.3 us (1.013)
  Pallas kernels: 50.2 us -> 50.9 us
    pallas_call x1, Pallas kernels: 30.7 us -> 31.5 us  [exchange(): pl.pallas_call(exchange_kernel, out_shape=[jax.ShapeDtypeStruct(s, F32) f...]
where the time goes in v9:
time: 54.3 us; the launch traced here: 54.2 us
  Pallas kernels  50.9 us (94%)
  local copies, waits for them, and re-layouts  2.44 us (4%)
  between operations  0.8 us (1%)
    pallas_call x1, Pallas kernels, exchange(): pl.pallas_call(exchange_kernel, out_shape=[jax.ShapeDtypeStruct(s, F32) f...  31.5 us
    pallas_call x1, Pallas kernels, diffuse(): pl.pallas_call(diffuse_kernel, out_shape=jax.ShapeDtypeStruct(cells, F32)...  10.6 us
    pallas_call x1, Pallas kernels, deposit(): pl.pallas_call(deposit_kernel, out_shape=(sd((8, 32, 256), F32), sd((8, 3...  8.89 us
    unnamed x23, local copies, waits for them, and re-layouts  2.44 us

profile of v9, /device:TPU:0, one launch (start us, length us, event | category | flops | bytes accessed | tf_op | source)
XLA Modules:
  0.0 54.2 jit_solution(292247097791377794)
XLA Ops:
  0.6 0.0 copy-start
  0.6 0.0 copy-start.1
  0.7 0.0 copy-start.2
  0.7 0.0 copy-start.3
  0.7 0.0 copy-start.6
  0.7 31.5 %exchange.1 = (f32[12,64,128]{2,1,0:T(8,128)}, f32[32,256]{1,0:T(8,128)}, f32[32,256]{1,0:T(8,128)}, f32[8,256]{1,0:T(8,128)}, f32[8,256]{1,0:T(8,128)}, /*index=5*/f32[27,8,32,256]{3,2,1,0:T(8,128)}) custom-call(f32[9,4096]{1,0:T(8,128)} %loads_in.1, s32[1,4096]{1,0:T(1,128)} %bitcast.2, s32[1,4096]{1,0:T(1,128)} %bitcast.3, f32[9,8,32,256]{3,2,1,0:T(8,128)} %fields_ref.1, ...), custom_call_target="tpu_custom_call" | custom-call | tf_op jit(solution)/shard_map/exchange/pallas_call | solution.py:476
  32.1 0.0 copy-done
  32.2 0.0 copy-done.1
  32.2 0.0 copy-done.2
  32.2 0.0 copy-done.3
  32.2 0.0 copy-done.6
  32.2 0.0 copy-start.5
  32.2 1.0 %copy-done.5 = f32[12,64,128]{2,1,0:T(8,128)S(1)} copy-done((f32[12,64,128]{2,1,0:T(8,128)S(1)}, f32[12,64,128]{2,1,0:T(8,128)}, u32[]{:S(2)}) %copy-start.5) | copy-done | bytes 393240
  33.2 0.0 copy-start.4
  33.2 0.0 copy-start.7
  33.2 0.0 copy-start.10
  33.2 8.9 %deposit.1 = (f32[8,32,256]{2,1,0:T(8,128)}, f32[8,32,256]{2,1,0:T(8,128)S(1)}, f32[9,8,32,256]{3,2,1,0:T(8,128)S(1)}, f32[9,8,256]{2,1,0:T(8,128)S(1)}, f32[9,8...) custom-call(f32[12,64,128]{2,1,0:T(8,128)S(1)} %copy-done.5, f32[9,8,32,256]{3,2,1,0:T(8,128)S(1)} %copy-done, ...), custom_call_target="tpu_custom_call" | custom-call | tf_op jit(solution)/shard_map/deposit/pallas_call | solution.py:119
  42.1 0.0 copy-done.4
  42.1 0.0 copy-done.7
  42.1 0.0 copy-done.8
  42.1 0.0 copy-done.9
  42.2 0.0 copy-done.10
  42.2 10.6 %diffuse.1 = f32[9,8,32,256]{3,2,1,0:T(8,128)S(1)} custom-call(f32[9,8,32,256]{3,2,1,0:T(8,128)S(1)} %get-tuple-element.18.src_ref, f32[9,8,256]{2,1,0:T(8,128)S(1)} %get-tuple-element.19.tlo_ref, f32[9,8,256]{2,1,0:T(8,128)S(1)} %get-tuple-element.20.thi_ref, f32[8,32,256]{2,1,0:T(8,128)S(1)} %copy-done.4, f32[8,32,256]{2,1,0:T(8,128)S(1)} %get-tuple-element.21.vn_ref, ...), custom_call_target="tpu_custom_call" | custom-call | tf_op jit(solution)/shard_map/diffuse/pallas_call | solution.py:272
  52.8 1.4 %copy.14 = f32[9,8,32,256]{3,2,1,0:T(8,128)} copy(f32[9,8,32,256]{3,2,1,0:T(8,128)S(1)} %diffuse.1) | data formatting | bytes 4718592
  (2 shorter events, 0.0 us)
Async XLA Ops:
  0.6 31.5 %copy-start = (f32[9,8,32,256]{3,2,1,0:T(8,128)S(1)}, f32[9,8,32,256]{3,2,1,0:T(8,128)}, u32[]{:S(2)}) copy-start(f32[9,8,32,256]{3,2,1,0:T(8,128)} %fields_ref.1) | copy-start | bytes 7077892
  0.6 31.5 %copy-start.1 = (f32[8,32,256]{2,1,0:T(8,128)S(1)}, f32[8,32,256]{2,1,0:T(8,128)}, u32[]{:S(2)}) copy-start(f32[8,32,256]{2,1,0:T(8,128)} %vol_ref.1) | copy-start | bytes 786436
  0.7 31.5 %copy-start.2 = (f32[8,32,256]{2,1,0:T(8,128)S(1)}, f32[8,32,256]{2,1,0:T(8,128)}, u32[]{:S(2)}) copy-start(f32[8,32,256]{2,1,0:T(8,128)} %sa_ref.1) | copy-start | bytes 786436
  0.7 31.5 %copy-start.3 = (f32[8,32,256]{2,1,0:T(8,128)S(1)}, f32[8,32,256]{2,1,0:T(8,128)}, u32[]{:S(2)}) copy-start(f32[8,32,256]{2,1,0:T(8,128)} %st_ref.1) | copy-start | bytes 786436
  0.7 31.5 %copy-start.6 = (f32[8,32,256]{2,1,0:T(8,128)S(1)}, f32[8,32,256]{2,1,0:T(8,128)}, u32[]{:S(2)}) copy-start(f32[8,32,256]{2,1,0:T(8,128)} %sr_ref.1) | copy-start | bytes 786436
  32.2 1.0 %copy-start.5 = (f32[12,64,128]{2,1,0:T(8,128)S(1)}, f32[12,64,128]{2,1,0:T(8,128)}, u32[]{:S(2)}) copy-start(f32[12,64,128]{2,1,0:T(8,128)} %get-tuple-element.15.chan_ref) | copy-start | bytes 1179652
  33.2 8.9 %copy-start.4 = (f32[8,32,256]{2,1,0:T(8,128)S(1)}, f32[8,32,256]{2,1,0:T(8,128)}, u32[]{:S(2)}) copy-start(f32[8,32,256]{2,1,0:T(8,128)} %k_ref.1) | copy-start | bytes 786436
  33.2 8.9 %copy-start.7 = (f32[32,256]{1,0:T(8,128)S(1)}, f32[32,256]{1,0:T(8,128)}, u32[]{:S(2)}) copy-start(f32[32,256]{1,0:T(8,128)} %get-tuple-element.22.kzl_ref) | copy-start | bytes 98308
  33.2 8.9 %copy-start.8 = (f32[32,256]{1,0:T(8,128)S(1)}, f32[32,256]{1,0:T(8,128)}, u32[]{:S(2)}) copy-start(f32[32,256]{1,0:T(8,128)} %get-tuple-element.23.kzh_ref) | copy-start | bytes 98308
  33.2 8.9 %copy-start.9 = (f32[8,256]{1,0:T(8,128)S(1)}, f32[8,256]{1,0:T(8,128)}, u32[]{:S(2)}) copy-start(f32[8,256]{1,0:T(8,128)} %get-tuple-element.24.ktl_ref) | copy-start | bytes 24580
  33.2 8.9 %copy-start.10 = (f32[8,256]{1,0:T(8,128)S(1)}, f32[8,256]{1,0:T(8,128)}, u32[]{:S(2)}) copy-start(f32[8,256]{1,0:T(8,128)} %get-tuple-element.25.kth_ref) | copy-start | bytes 24580
